TPU v7x, 32 devices: a whole 2x2x4 slice. The times are simulated.
32 devices in a mesh: groups: 2 (over y), seq: 4 (over z), dp: 2 (over x), fsdp: 2 (over core).
Axes of the slice: x: 2, y: 2, z: 4, core: 2. Of those that a mesh axis runs over, the one named last changes fastest.
Arguments:
- tokens: bfloat16 [8, 4, 8, 16, 1024], P(('groups', 'dp', 'fsdp'), 'seq'), parts along dimension 0, may hold values from -6 to 6
- timesteps: int32 [8], P(('groups', 'dp', 'fsdp')), parts along dimension 0, may hold values from 0 to 999
- pxrd_mod: float32 [8, 3, 1024], P(('groups', 'dp', 'fsdp')), parts along dimension 0, may hold values from -3 to 3
- time_weight: bfloat16 [256, 3072], P('fsdp'), may hold values from -0.375 to 0.375
- conv_kernel: float32 [27, 1024], replicated, may hold values from -0.9 to 0.9
- qkv_weight: bfloat16 [1024, 1536], P('fsdp'), may hold values from -0.75 to 0.75
- out_weight: bfloat16 [512, 1024], P('fsdp'), may hold values from -1 to 1
- out_cot: bfloat16 [8, 4, 8, 16, 1024], P(('groups', 'dp', 'fsdp'), 'seq'), parts along dimension 0, may hold values from -6 to 6
Outputs:
- out_tokens: bfloat16 [8, 4, 8, 16, 1024], P(('groups', 'dp', 'fsdp'), 'seq'), parts along dimension 0
- d_tokens: bfloat16 [8, 4, 8, 16, 1024], P(('groups', 'dp', 'fsdp'), 'seq'), parts along dimension 0
- d_kernel: float32 [54, 1024], P('groups'), parts along dimension 0
There are 2 independent parts, one for each index of `groups`. A program takes and returns all parts, laid end to end along the dimension named above; an argument that names none is the same for every part. Nothing has to cross between parts.
All inputs are finite; a program needn't handle non-finite values.
Results may differ from a plain program's by a relative error of at most 0.024.
Values may be sent and summed in bfloat16 or wider, within the bound.
No kernel may reach another device: no remote copies, remote signals or barrier semaphores. Data moves between devices by JAX's collectives and lax.ppermute only.
A program may use at most 64 MiB of HBM per device.

v0:
```python
import math

import jax
import jax.numpy as jnp
from jax import lax
from jax.sharding import PartitionSpec as P

H = 8
HD = 64


def padded_2(value, sides, width):
    for axis, dim in sides:
        count, length = (lax.axis_size(axis), value.shape[dim])
        up = [(i, (i + 1) % count) for i in range(count - 1)]
        down = [(j, i) for i, j in up]
        last = lax.slice_in_dim(value, length - width, length, axis=dim)
        leading = lax.slice_in_dim(value, 0, width, axis=dim)
        before = lax.ppermute(last, axis, up)
        after = lax.ppermute(leading, axis, down)
        value = jnp.concatenate([before, value, after], axis=dim)
    return value


def time_features(steps_int, freq_width):
    half_width = freq_width // 2
    freq_index = jnp.arange(half_width).astype(jnp.float32)
    frequency = jnp.exp(freq_index * (-math.log(10000.0) / half_width))
    angles = steps_int.astype(jnp.float32)[:, None] * frequency[None, :]
    return jnp.concatenate([jnp.cos(angles), jnp.sin(angles)], axis=1).astype(jnp.bfloat16)


def modulation(steps_int, pxrd_mod, time_weight):
    features = time_features(steps_int, time_weight.shape[0])
    projected = jnp.dot(features, time_weight, preferred_element_type=jnp.float32)
    return projected.reshape(steps_int.shape[0], 3, time_weight.shape[1] // 3) + pxrd_mod


def depthwise(padded_z, kernel_taps, plane_count):
    framed = jnp.pad(padded_z, ((0, 0), (1, 1), (1, 1), (0, 0)))
    side_y = framed.shape[1] - 2
    side_x = framed.shape[2] - 2
    result = jnp.zeros((plane_count, side_y, side_x, framed.shape[3]), jnp.float32)
    for tap_z in range(3):
        for tap_y in range(3):
            for tap_x in range(3):
                window = framed[
                    tap_z : tap_z + plane_count, tap_y : tap_y + side_y, tap_x : tap_x + side_x
                ]
                result = result + kernel_taps[9 * tap_z + 3 * tap_y + tap_x] * window.astype(
                    jnp.float32
                )
    return result


def kernel_terms(padded_z, upstream, plane_count):
    framed = jnp.pad(padded_z, ((0, 0), (1, 1), (1, 1), (0, 0)))
    side_y = framed.shape[1] - 2
    side_x = framed.shape[2] - 2
    upstream_f = upstream.astype(jnp.float32)
    collected = []
    for tap_z in range(3):
        for tap_y in range(3):
            for tap_x in range(3):
                window = framed[
                    tap_z : tap_z + plane_count, tap_y : tap_y + side_y, tap_x : tap_x + side_x
                ]
                collected.append(jnp.sum(window.astype(jnp.float32) * upstream_f, axis=(0, 1, 2)))
    return jnp.stack(collected)


def modulate(stream, shift_row, scale_row):
    centre = stream - jnp.mean(stream, axis=-1, keepdims=True)
    spread = jnp.mean(centre * centre, axis=-1, keepdims=True)
    return centre * lax.rsqrt(spread + 1e-06) * (1.0 + scale_row) + shift_row


def head_norms(projected):
    row_count = projected.shape[0]
    sections = projected.reshape(row_count, 3, H, HD)
    query_key = sections[:, :2]
    normed = query_key * lax.rsqrt(jnp.mean(query_key * query_key, axis=-1, keepdims=True) + 1e-06)
    return (
        normed[:, 0].reshape(row_count, H * HD),
        normed[:, 1].reshape(row_count, H * HD),
        sections[:, 2].reshape(row_count, H * HD),
    )


def attend_both(queries, grads, key_rows, value_rows):
    count = queries.shape[0]
    heads = queries.shape[1]
    block = min(512, count)
    steps = count // block
    scale_dot = 1.0 / math.sqrt(HD)

    def one_block(carry, pieces):
        query_blk, grad_blk = pieces
        scores = (
            jnp.einsum("qhd,khd->hqk", query_blk, key_rows, preferred_element_type=jnp.float32)
            * scale_dot
        )
        expo = jnp.exp(scores)
        totals = jnp.sum(expo, axis=-1, keepdims=True)
        weights = expo / totals
        probs = weights.astype(jnp.bfloat16)
        attn_blk = jnp.einsum(
            "hqk,khd->qhd", probs, value_rows, preferred_element_type=jnp.float32
        ).astype(jnp.bfloat16)
        delta = jnp.sum(grad_blk.astype(jnp.float32) * attn_blk.astype(jnp.float32), axis=-1).T
        dprob = jnp.einsum("qhd,khd->hqk", grad_blk, value_rows, preferred_element_type=jnp.float32)
        dscore = (weights * (dprob - delta[:, :, None]) * scale_dot).astype(jnp.bfloat16)
        dquery = jnp.einsum("hqk,khd->qhd", dscore, key_rows, preferred_element_type=jnp.float32)
        dkey = carry[0] + jnp.einsum(
            "hqk,qhd->khd", dscore, query_blk, preferred_element_type=jnp.float32
        )
        dvalue = carry[1] + jnp.einsum(
            "hqk,qhd->khd", probs, grad_blk, preferred_element_type=jnp.float32
        )
        return ((dkey, dvalue), (attn_blk, dquery))

    zeros_kv = jnp.zeros(key_rows.shape, jnp.float32)
    (dkey, dvalue), (attn_all, dquery) = lax.scan(
        one_block,
        (zeros_kv, zeros_kv),
        (queries.reshape(steps, block, heads, HD), grads.reshape(steps, block, heads, HD)),
    )
    return (attn_all.reshape(count, heads, HD), dquery.reshape(count, heads, HD), dkey, dvalue)


def shards(tokens, timesteps, pxrd_mod, time_weight, conv_kernel, qkv_weight, out_weight, out_cot):
    w_qkv, w_out, w_time = (
        lax.all_gather(qkv_weight, "fsdp", axis=0, tiled=True),
        lax.all_gather(out_weight, "fsdp", axis=0, tiled=True),
        lax.all_gather(time_weight, "fsdp", axis=0, tiled=True),
    )
    plane_count = tokens.shape[1]
    side_y = tokens.shape[2]
    side_x = tokens.shape[3]
    width_model = tokens.shape[4]
    row_count = plane_count * side_y * side_x
    inner_width = H * HD
    seq_count = lax.axis_size("seq")
    head_groups = min(H, seq_count)
    per_device = H // head_groups
    row_split = seq_count // head_groups
    part_rows = row_count // row_split
    group_width = per_device * HD
    padded = padded_2(tokens, (("seq", 1),), 1)[0]
    mixed = depthwise(padded, conv_kernel, plane_count)
    resid = (
        (tokens[0].astype(jnp.float32) + mixed).astype(jnp.bfloat16).reshape(row_count, width_model)
    )
    modul = modulation(timesteps, pxrd_mod, w_time)
    shift_row = modul[0, 0]
    scale_row = modul[0, 1]
    gate_row = modul[0, 2]
    resid_f = resid.astype(jnp.float32)
    normed = modulate(resid_f, shift_row, scale_row).astype(jnp.bfloat16)
    projected = jnp.dot(normed, w_qkv, preferred_element_type=jnp.float32)
    query_f, key_f, value_f = head_norms(projected)
    cotangent = out_cot[0].reshape(row_count, width_model).astype(jnp.float32)
    gated = (gate_row * cotangent).astype(jnp.bfloat16)
    grad_attn = lax.dot_general(
        gated, w_out, (((1,), (1,)), ((), ())), preferred_element_type=jnp.float32
    ).astype(jnp.bfloat16)

    def to_heads(token_rows):
        shaped = token_rows.reshape(row_split, part_rows, head_groups, group_width)
        return shaped.transpose(2, 0, 1, 3).reshape(seq_count, part_rows, group_width)

    def from_heads(head_rows):
        shaped = head_rows.reshape(head_groups, row_split, part_rows, group_width)
        return shaped.transpose(1, 2, 0, 3).reshape(row_count, inner_width)

    query_heads, grad_heads = (
        lax.all_to_all(
            to_heads(query_f.astype(jnp.bfloat16)), "seq", split_axis=0, concat_axis=0, tiled=True
        ),
        lax.all_to_all(to_heads(grad_attn), "seq", split_axis=0, concat_axis=0, tiled=True),
    )
    query_count = seq_count * part_rows
    query_heads = query_heads.reshape(query_count, per_device, HD)
    grad_heads = grad_heads.reshape(query_count, per_device, HD)
    stacked = jnp.stack(
        [
            key_f.astype(jnp.bfloat16).reshape(row_count, head_groups, group_width),
            value_f.astype(jnp.bfloat16).reshape(row_count, head_groups, group_width),
        ],
        axis=2,
    )
    by_group = stacked.transpose(1, 0, 2, 3).reshape(head_groups, row_count, 2 * group_width)
    copies = jnp.broadcast_to(
        by_group[:, None], (head_groups, row_split, row_count, 2 * group_width)
    )
    arrived = lax.all_to_all(
        copies.reshape(seq_count, row_count, 2 * group_width),
        "seq",
        split_axis=0,
        concat_axis=0,
        tiled=True,
    )
    key_value = arrived.reshape(seq_count * row_count, 2, per_device, HD)
    attn_heads, dquery, dkey, dvalue = attend_both(
        query_heads, grad_heads, key_value[:, 0], key_value[:, 1]
    )
    attn_tok = from_heads(
        lax.all_to_all(
            attn_heads.reshape(seq_count, part_rows, group_width),
            "seq",
            split_axis=0,
            concat_axis=0,
            tiled=True,
        )
    )
    projected_out = jnp.dot(attn_tok, w_out, preferred_element_type=jnp.float32)
    out_rows = (resid_f + gate_row * projected_out).astype(jnp.bfloat16)
    dquery_tok = from_heads(
        lax.all_to_all(
            dquery.reshape(seq_count, part_rows, group_width),
            "seq",
            split_axis=0,
            concat_axis=0,
            tiled=True,
        )
    )
    grads_kv = jnp.stack([dkey, dvalue], axis=1)
    returned = lax.all_to_all(
        grads_kv.reshape(seq_count, row_count, 2 * group_width).astype(jnp.bfloat16),
        "seq",
        split_axis=0,
        concat_axis=0,
        tiled=True,
    ).astype(jnp.float32)
    summed = jnp.sum(returned.reshape(head_groups, row_split, row_count, 2 * group_width), axis=1)
    grads_tok = (
        summed.reshape(head_groups, row_count, 2, group_width)
        .transpose(2, 1, 0, 3)
        .reshape(2, row_count, inner_width)
    )
    _, pullback = jax.vjp(head_norms, projected)
    (grad_projected,) = pullback((dquery_tok, grads_tok[0], grads_tok[1]))
    grad_proj_b = grad_projected.astype(jnp.bfloat16)
    grad_normed = lax.dot_general(
        grad_proj_b, w_qkv, (((1,), (1,)), ((), ())), preferred_element_type=jnp.float32
    )
    _, pull_norm = jax.vjp(lambda stream: modulate(stream, shift_row, scale_row), resid_f)
    (grad_stream,) = pull_norm(grad_normed)
    grad_resid = (
        (cotangent + grad_stream)
        .astype(jnp.bfloat16)
        .reshape(1, plane_count, side_y, side_x, width_model)
    )
    grad_padded = padded_2(grad_resid, (("seq", 1),), 1)[0]
    grad_tokens = (
        grad_resid[0].astype(jnp.float32) + depthwise(grad_padded, conv_kernel[::-1], plane_count)
    ).astype(jnp.bfloat16)
    local_terms = kernel_terms(padded, grad_resid[0], plane_count)
    norm_factor = 1.0 / math.sqrt(
        lax.axis_size("dp") * lax.axis_size("fsdp") * seq_count * row_count
    )
    grad_kernel = lax.psum(local_terms, ("seq", "dp", "fsdp")) * norm_factor
    return (out_rows.reshape(tokens.shape), grad_tokens.reshape(tokens.shape), grad_kernel)


def solution(mesh):
    placed = (
        P(("groups", "dp", "fsdp"), "seq", None, None, None),
        P(("groups", "dp", "fsdp")),
        P(("groups", "dp", "fsdp"), None, None),
        P("fsdp", None),
        P(),
        P("fsdp", None),
        P("fsdp", None),
        P(("groups", "dp", "fsdp"), "seq", None, None, None),
    )
    return jax.shard_map(
        shards,
        mesh=mesh,
        in_specs=placed,
        out_specs=(
            P(("groups", "dp", "fsdp"), "seq", None, None, None),
            P(("groups", "dp", "fsdp"), "seq", None, None, None),
            P("groups", None),
        ),
        check_vma=False,
    )
```

profile of v0, /device:TPU:0, one launch (start us, length us, event | category | flops | bytes accessed | tf_op | source)
XLA Modules:
  0.0 220.2 jit_solution(6687539041669319922)
XLA Ops:
  7.2 2.3 %copy.35 = bf16[128,3072]{0,1:T(8,128)(2,1)} copy(bf16[128,3072]{1,0:T(8,128)(2,1)} %param.11) | data formatting | bytes 1572864 | tf_op args[3]
  11.0 4.9 %collective-permute-start = (bf16[1,1,8,16,1024]{4,3,2,1,0:T(8,128)(2,1)S(1)}, bf16[1,1,8,16,1024]{4,3,2,1,0:T(8,128)(2,1)S(1)}, u32[]{:S(2)}, u32[]{:S(2)}) collective-permute-start(bf16[1,1,8,16,1024]{4,3,2,1,0:T(8,128)(2,1)S(1)} %copy-done.6), channel_id=1, source_target_pairs={{0,4},{4,8},{8,12},{1,5},{5,9},{9,13},{2,6},{6,10},{10,14},{3,7},{... | collective-permute-start | bytes 786440 | tf_op jit(solution)/shard_map/ppermute | solution.py:19
  16.0 1.3 collective-permute-start.1
  18.4 3.2 %collective-permute-done = bf16[1,1,8,16,1024]{4,3,2,1,0:T(8,128)(2,1)S(1)} collective-permute-done((bf16[1,1,8,16,1024]{4,3,2,1,0:T(8,128)(2,1)S(1)}, bf16[1,1,8,16,1024]{4,3,2,1,0:T(8,128)(2,1)S(1)}, u32[]{:S(2)}, u32[]{:S(2)}) %collective-permute-start) | collective-permute-done | bytes 262176 | tf_op jit(solution)/shard_map/ppermute | solution.py:19
  21.5 4.1 %collective-permute-done.1 = bf16[1,1,8,16,1024]{4,3,2,1,0:T(8,128)(2,1)S(1)} collective-permute-done((bf16[1,1,8,16,1024]{4,3,2,1,0:T(8,128)(2,1)S(1)}, bf16[1,1,8,16,1024]{4,3,2,1,0:T(8,128)(2,1)S(1)}, u32[]{:S(2)}, u32[]{:S(2)}) %collective-permute-start.1) | collective-permute-done | bytes 262176 | tf_op jit(solution)/shard_map/ppermute | solution.py:20
  26.7 2.7 %convert_reduce_fusion = (f32[8,16]{1,0:T(8,128)S(1)}, bf16[1,8,16,1024]{3,2,1,0:T(8,128)(2,1)S(1)}) fusion(f32[1024]{0:T(1024)S(1)} %bitcast.275, f32[1024]{0:T(1024)S(1)} %bitcast.277, f32[1024]{0:T(1024)S(1)} %bitcast.281, f32[1024]{0:T(1024)S(1)} %bitcast.283, bf16[1,1,8,16,1024]{4,3,2,1,0:T(8,128)(2,1)S(1)} %collective-permute-done.1, ...), kind=kLoop, calls=%fused_computation.221 | loop fusion | flops 11009920 | bytes 1946112 | tf_op jit(solution)/shard_map/reduce_sum | solution.py:73
  30.5 2.0 fusion.103
  32.6 1.3 all-gather.8.cloned.1.call-done
  33.9 1.7 convolution_convert_fusion.2
  36.3 4.9 %all-to-all-start.3 = ((bf16[4,128,128]{1,2,0:T(8,128)(2,1)}), bf16[4,128,128]{1,2,0:T(8,128)(2,1)S(1)}, u32[]{:S(2)}, u32[]{:S(2)}) async-start(bf16[4,128,128]{1,2,0:T(8,128)(2,1)} %bitcast.65), calls=%async_computation.3 | async-start | bytes 262144 | tf_op jit(solution)/shard_map/all_to_all | solution.py:180
  42.2 6.6 %all-gather.6.cloned.1.call-done = bf16[1024,1536]{1,0:T(8,128)(2,1)} async-done(((bf16[512,1536]{1,0:T(8,128)(2,1)}), bf16[1024,1536]{1,0:T(8,128)(2,1)}) %all-gather.6.cloned.1.call-update) | async-done | bytes 3145744 | tf_op jit(solution)/shard_map/all_gather | solution.py:133
  48.8 3.2 %copy.36 = bf16[1536,1024]{1,0:T(8,128)(2,1)S(1)} copy(bf16[1536,1024]{0,1:T(8,128)(2,1)} %bitcast.242) | data formatting | bytes 6291456 | tf_op jit(solution)/shard_map/dot_general | solution.py:160
  51.9 1.9 fusion.104
  55.5 4.9 %all-to-all-start.1 = ((bf16[4,128,128]{1,2,0:T(8,128)(2,1)}), bf16[4,128,128]{1,2,0:T(8,128)(2,1)S(1)}, u32[]{:S(2)}, u32[]{:S(2)}) async-start(bf16[4,128,128]{1,2,0:T(8,128)(2,1)} %bitcast.54), calls=%async_computation.1 | async-start | bytes 262144 | tf_op jit(solution)/shard_map/all_to_all | solution.py:177
  62.1 4.7 %all-to-all-done.1 = bf16[4,128,128]{1,2,0:T(8,128)(2,1)S(1)} async-done(((bf16[4,128,128]{1,2,0:T(8,128)(2,1)}), bf16[4,128,128]{1,2,0:T(8,128)(2,1)S(1)}, u32[]{:S(2)}, u32[]{:S(2)}) %all-to-all-start.1) | async-done | bytes 131104 | tf_op jit(solution)/shard_map/all_to_all | solution.py:177
  66.7 3.4 %all-to-all-start = ((bf16[4,128,256]{1,2,0:T(8,128)(2,1)}), bf16[4,128,256]{1,2,0:T(8,128)(2,1)S(1)}, u32[]{:S(2)}, u32[]{:S(2)}) async-start(bf16[4,128,256]{1,2,0:T(8,128)(2,1)} %bitcast.50), calls=%async_computation | async-start | bytes 524288 | tf_op jit(solution)/shard_map/all_to_all | solution.py:196
  70.5 7.8 %all-to-all-done = bf16[4,128,256]{1,2,0:T(8,128)(2,1)S(1)} async-done(((bf16[4,128,256]{1,2,0:T(8,128)(2,1)}), bf16[4,128,256]{1,2,0:T(8,128)(2,1)S(1)}, u32[]{:S(2)}, u32[]{:S(2)}) %all-to-all-start) | async-done | bytes 262176 | tf_op jit(solution)/shard_map/all_to_all | solution.py:196
  82.2 3.4 %all-to-all-start.4 = ((bf16[4,128,256]{1,2,0:T(8,128)(2,1)}), bf16[4,128,256]{1,2,0:T(8,128)(2,1)S(1)}, u32[]{:S(2)}, u32[]{:S(2)}) async-start(bf16[4,128,256]{1,2,0:T(8,128)(2,1)} %copy.48), calls=%async_computation.4 | async-start | bytes 524288 | tf_op jit(solution)/shard_map/all_to_all | solution.py:228
  87.6 4.7 %all-to-all-done.4 = bf16[4,128,256]{1,2,0:T(8,128)(2,1)S(1)} async-done(((bf16[4,128,256]{1,2,0:T(8,128)(2,1)}), bf16[4,128,256]{1,2,0:T(8,128)(2,1)S(1)}, u32[]{:S(2)}, u32[]{:S(2)}) %all-to-all-start.4) | async-done | bytes 262176 | tf_op jit(solution)/shard_map/all_to_all | solution.py:228
  92.4 3.4 %all-to-all-start.5 = ((f32[4,128,128]{1,2,0:T(8,128)}), f32[4,128,128]{1,2,0:T(8,128)S(1)}, u32[]{:S(2)}, u32[]{:S(2)}) async-start(f32[4,128,128]{1,2,0:T(8,128)} %copy.50), calls=%async_computation.5 | async-start | bytes 524288 | tf_op jit(solution)/shard_map/all_to_all | solution.py:219
  95.9 6.7 %all-to-all-done.5 = f32[4,128,128]{1,2,0:T(8,128)S(1)} async-done(((f32[4,128,128]{1,2,0:T(8,128)}), f32[4,128,128]{1,2,0:T(8,128)S(1)}, u32[]{:S(2)}, u32[]{:S(2)}) %all-to-all-start.5) | async-done | bytes 262176 | tf_op jit(solution)/shard_map/all_to_all | solution.py:219
  102.6 3.4 %all-to-all-start.2 = ((bf16[4,128,128]{1,2,0:T(8,128)(2,1)}), bf16[4,128,128]{1,2,0:T(8,128)(2,1)S(1)}, u32[]{:S(2)}, u32[]{:S(2)}) async-start(bf16[4,128,128]{1,2,0:T(8,128)(2,1)} %copy.42), calls=%async_computation.2 | async-start | bytes 262144 | tf_op jit(solution)/shard_map/all_to_all | solution.py:208
  106.3 1.6 copy-done
  108.0 1.2 multiply_reduce_fusion
  109.6 1.3 fusion.75
  110.8 1.3 collective-permute-start.3
  112.1 4.7 %collective-permute-start.2 = (bf16[1,1,8,16,1024]{4,3,2,1,0:T(8,128)(2,1)S(1)}, bf16[1,1,8,16,1024]{4,3,2,1,0:T(8,128)(2,1)S(1)}, u32[]{:S(2)}, u32[]{:S(2)}) collective-permute-start(bf16[1,1,8,16,1024]{4,3,2,1,0:T(8,128)(2,1)S(1)} %bitcast.245), channel_id=1, source_target_pairs={{0,4},{4,8},{8,12},{1,5},{5,9},{9,13},{2,6},{6,10},{10,14},{3,7},{... | collective-permute-start | bytes 786440 | tf_op jit(solution)/shard_map/ppermute | solution.py:19
  116.9 1.6 fusion.76
  118.5 2.6 %stack.130 = f32[27,1024]{1,0:T(8,128)} concatenate(f32[1,1024]{1,0:T(1,128)S(1)} %bitcast.331, f32[1,1024]{1,0:T(1,128)S(1)} %bitcast.332, f32[1,1024]{1,0:T(1,128)S(1)} %bitcast.333, f32[1,1024]{1,0:T(1,128)S(1)} %bitcast.334, f32[1,1024]{1,0:T(1,128)S(1)} %bitcast.329, f32[1,1024]{1,0:T(1,128)S(1)} %bitcast.335, f32[1,1024]{1,0:T(1,128)S(1)} %bitcast.336, ...), dimensions={0} | concatenate | bytes 221184 | tf_op jit(solution)/shard_map/stack | solution.py:69
  122.5 86.3 %all-reduce.8.cloned.1.call-done = f32[27,1024]{1,0:T(8,128)} async-done(((f32[27,1024]{1,0:T(8,128)}), f32[27,1024]{1,0:T(8,128)}) %all-reduce.8.cloned.1.call-update) | async-done | bytes 110608 | tf_op jit(solution)/shard_map/psum | solution.py:262
  208.8 1.6 broadcast_multiply_fusion
  210.7 3.0 %fusion.90 = bf16[1,1,8,16,1024]{4,3,2,1,0:T(8,128)(2,1)} fusion(bf16[3,8,16,1024]{3,2,1,0:T(8,128)(2,1)S(1)} %maximum_bitcast_fusion.1, f32[1024]{0:T(1024)S(1)} %bitcast.280, f32[1024]{0:T(1024)S(1)} %bitcast.264, f32[1024]{0:T(1024)S(1)} %bitcast.274, f32[1024]{0:T(1024)S(1)} %bitcast.272, bf16[1,1,8,16,1024]{4,3,2,1,0:T(8,128)(2,1)S(1)} %collective-permute-done.3, ...), kind=kLoop, calls=%fused_computation.227 | loop fusion | flops 10747904 | bytes 1945600 | tf_op jit(solution)/shard_map/reshape | solution.py:263
  (203 shorter events, 16.8 us)
Async XLA Ops:
  7.2 23.3 %all-gather.4.cloned.1.call-start = ((), (), s32[]{:S(2)}) async-start(), calls=%async_computation.6 | async-start | bytes 2359296 | tf_op jit(solution)/shard_map/all_gather | solution.py:135
  9.5 24.3 %all-gather.8.cloned.1.call-start = ((), (), s32[]{:S(2)}) async-start(), calls=%async_computation.8 | async-start | bytes 1572864 | tf_op jit(solution)/shard_map/all_gather | solution.py:134
  10.3 38.5 %all-gather.6.cloned.1.call-start = ((), (), s32[]{:S(2)}) async-start(), calls=%async_computation.7 | async-start | bytes 4718592 | tf_op jit(solution)/shard_map/all_gather | solution.py:133
  11.0 10.5 %collective-permute-start = (bf16[1,1,8,16,1024]{4,3,2,1,0:T(8,128)(2,1)S(1)}, bf16[1,1,8,16,1024]{4,3,2,1,0:T(8,128)(2,1)S(1)}, u32[]{:S(2)}, u32[]{:S(2)}) collective-permute-start(bf16[1,1,8,16,1024]{4,3,2,1,0:T(8,128)(2,1)S(1)} %copy-done.6), channel_id=1, source_target_pairs={{0,4},{4,8},{8,12},{1,5},{5,9},{9,13},{2,6},{6,10},{10,14},{3,7},{... | collective-permute-start | bytes 786440 | tf_op jit(solution)/shard_map/ppermute | solution.py:19
  16.0 9.7 %collective-permute-start.1 = (bf16[1,1,8,16,1024]{4,3,2,1,0:T(8,128)(2,1)S(1)}, bf16[1,1,8,16,1024]{4,3,2,1,0:T(8,128)(2,1)S(1)}, u32[]{:S(2)}, u32[]{:S(2)}) collective-permute-start(bf16[1,1,8,16,1024]{4,3,2,1,0:T(8,128)(2,1)S(1)} %copy-done.6), channel_id=1, source_target_pairs={{4,0},{8,4},{12,8},{5,1},{9,5},{13,9},{6,2},{10,6},{14,10},{7,3},{... | collective-permute-start | bytes 786440 | tf_op jit(solution)/shard_map/ppermute | solution.py:20
  36.3 19.2 %all-to-all-start.3 = ((bf16[4,128,128]{1,2,0:T(8,128)(2,1)}), bf16[4,128,128]{1,2,0:T(8,128)(2,1)S(1)}, u32[]{:S(2)}, u32[]{:S(2)}) async-start(bf16[4,128,128]{1,2,0:T(8,128)(2,1)} %bitcast.65), calls=%async_computation.3 | async-start | bytes 262144 | tf_op jit(solution)/shard_map/all_to_all | solution.py:180
  55.5 11.2 %all-to-all-start.1 = ((bf16[4,128,128]{1,2,0:T(8,128)(2,1)}), bf16[4,128,128]{1,2,0:T(8,128)(2,1)S(1)}, u32[]{:S(2)}, u32[]{:S(2)}) async-start(bf16[4,128,128]{1,2,0:T(8,128)(2,1)} %bitcast.54), calls=%async_computation.1 | async-start | bytes 262144 | tf_op jit(solution)/shard_map/all_to_all | solution.py:177
  66.7 11.6 %all-to-all-start = ((bf16[4,128,256]{1,2,0:T(8,128)(2,1)}), bf16[4,128,256]{1,2,0:T(8,128)(2,1)S(1)}, u32[]{:S(2)}, u32[]{:S(2)}) async-start(bf16[4,128,256]{1,2,0:T(8,128)(2,1)} %bitcast.50), calls=%async_computation | async-start | bytes 524288 | tf_op jit(solution)/shard_map/all_to_all | solution.py:196
  82.2 10.2 %all-to-all-start.4 = ((bf16[4,128,256]{1,2,0:T(8,128)(2,1)}), bf16[4,128,256]{1,2,0:T(8,128)(2,1)S(1)}, u32[]{:S(2)}, u32[]{:S(2)}) async-start(bf16[4,128,256]{1,2,0:T(8,128)(2,1)} %copy.48), calls=%async_computation.4 | async-start | bytes 524288 | tf_op jit(solution)/shard_map/all_to_all | solution.py:228
  92.4 10.2 %all-to-all-start.5 = ((f32[4,128,128]{1,2,0:T(8,128)}), f32[4,128,128]{1,2,0:T(8,128)S(1)}, u32[]{:S(2)}, u32[]{:S(2)}) async-start(f32[4,128,128]{1,2,0:T(8,128)} %copy.50), calls=%async_computation.5 | async-start | bytes 524288 | tf_op jit(solution)/shard_map/all_to_all | solution.py:219
  102.6 18.6 %all-to-all-start.2 = ((bf16[4,128,128]{1,2,0:T(8,128)(2,1)}), bf16[4,128,128]{1,2,0:T(8,128)(2,1)S(1)}, u32[]{:S(2)}, u32[]{:S(2)}) async-start(bf16[4,128,128]{1,2,0:T(8,128)(2,1)} %copy.42), calls=%async_computation.2 | async-start | bytes 262144 | tf_op jit(solution)/shard_map/all_to_all | solution.py:208
  106.0 102.8 %all-reduce.8.cloned.1.call-start = ((), (), s32[]{:S(2)}) async-start(), calls=%async_computation.9 | async-start | bytes 262144 | tf_op jit(solution)/shard_map/psum | solution.py:262
  110.8 99.5 %collective-permute-start.3 = (bf16[1,1,8,16,1024]{4,3,2,1,0:T(8,128)(2,1)S(1)}, bf16[1,1,8,16,1024]{4,3,2,1,0:T(8,128)(2,1)S(1)}, u32[]{:S(2)}, u32[]{:S(2)}) collective-permute-start(bf16[1,1,8,16,1024]{4,3,2,1,0:T(8,128)(2,1)S(1)} %bitcast.244), channel_id=1, source_target_pairs={{4,0},{8,4},{12,8},{5,1},{9,5},{13,9},{6,2},{10,6},{14,10},{7,3},{... | collective-permute-start | bytes 786440 | tf_op jit(solution)/shard_map/ppermute | solution.py:20
  112.1 98.2 %collective-permute-start.2 = (bf16[1,1,8,16,1024]{4,3,2,1,0:T(8,128)(2,1)S(1)}, bf16[1,1,8,16,1024]{4,3,2,1,0:T(8,128)(2,1)S(1)}, u32[]{:S(2)}, u32[]{:S(2)}) collective-permute-start(bf16[1,1,8,16,1024]{4,3,2,1,0:T(8,128)(2,1)S(1)} %bitcast.245), channel_id=1, source_target_pairs={{0,4},{4,8},{8,12},{1,5},{5,9},{9,13},{2,6},{6,10},{10,14},{3,7},{... | collective-permute-start | bytes 786440 | tf_op jit(solution)/shard_map/ppermute | solution.py:19
  121.2 89.3 %copy-start.16 = (f32[1,1024]{1,0:T(1,128)S(1)}, f32[1,1024]{1,0:T(1,128)}, u32[]{:S(2)}) copy-start(f32[1,1024]{1,0:T(1,128)} %copy-done.15) | copy-start | bytes 12292
  121.2 89.3 %copy-start.18 = (f32[1,1024]{1,0:T(1,128)S(1)}, f32[1,1024]{1,0:T(1,128)}, u32[]{:S(2)}) copy-start(f32[1,1024]{1,0:T(1,128)} %copy-done.17) | copy-start | bytes 12292
  121.2 89.3 %copy-start.20 = (f32[1,1024]{1,0:T(1,128)S(1)}, f32[1,1024]{1,0:T(1,128)}, u32[]{:S(2)}) copy-start(f32[1,1024]{1,0:T(1,128)} %copy-done.19) | copy-start | bytes 12292
  121.2 89.3 %copy-start.22 = (f32[1,1024]{1,0:T(1,128)S(1)}, f32[1,1024]{1,0:T(1,128)}, u32[]{:S(2)}) copy-start(f32[1,1024]{1,0:T(1,128)} %copy-done.21) | copy-start | bytes 12292
  121.3 89.3 %copy-start.24 = (f32[1,1024]{1,0:T(1,128)S(1)}, f32[1,1024]{1,0:T(1,128)}, u32[]{:S(2)}) copy-start(f32[1,1024]{1,0:T(1,128)} %copy-done.23) | copy-start | bytes 12292
  121.3 89.3 %copy-start.26 = (f32[1,1024]{1,0:T(1,128)S(1)}, f32[1,1024]{1,0:T(1,128)}, u32[]{:S(2)}) copy-start(f32[1,1024]{1,0:T(1,128)} %copy-done.25) | copy-start | bytes 12292
  121.3 89.3 %copy-start.28 = (f32[1,1024]{1,0:T(1,128)S(1)}, f32[1,1024]{1,0:T(1,128)}, u32[]{:S(2)}) copy-start(f32[1,1024]{1,0:T(1,128)} %copy-done.27) | copy-start | bytes 12292
  121.3 89.3 %copy-start.30 = (f32[1,1024]{1,0:T(1,128)S(1)}, f32[1,1024]{1,0:T(1,128)}, u32[]{:S(2)}) copy-start(f32[1,1024]{1,0:T(1,128)} %copy-done.29) | copy-start | bytes 12292
  121.3 89.3 %copy-start.32 = (f32[1,1024]{1,0:T(1,128)S(1)}, f32[1,1024]{1,0:T(1,128)}, u32[]{:S(2)}) copy-start(f32[1,1024]{1,0:T(1,128)} %copy-done.31) | copy-start | bytes 12292
  121.3 89.3 %copy-start.34 = (f32[1,1024]{1,0:T(1,128)S(1)}, f32[1,1024]{1,0:T(1,128)}, u32[]{:S(2)}) copy-start(f32[1,1024]{1,0:T(1,128)} %copy-done.33) | copy-start | bytes 12292
  121.3 89.3 %copy-start.36 = (f32[1,1024]{1,0:T(1,128)S(1)}, f32[1,1024]{1,0:T(1,128)}, u32[]{:S(2)}) copy-start(f32[1,1024]{1,0:T(1,128)} %copy-done.35) | copy-start | bytes 12292
  121.3 89.3 %copy-start.38 = (f32[1,1024]{1,0:T(1,128)S(1)}, f32[1,1024]{1,0:T(1,128)}, u32[]{:S(2)}) copy-start(f32[1,1024]{1,0:T(1,128)} %copy-done.37) | copy-start | bytes 12292
  121.3 89.3 %copy-start.40 = (f32[1,1024]{1,0:T(1,128)S(1)}, f32[1,1024]{1,0:T(1,128)}, u32[]{:S(2)}) copy-start(f32[1,1024]{1,0:T(1,128)} %copy-done.39) | copy-start | bytes 12292
  121.3 89.3 %copy-start.42 = (f32[1,1024]{1,0:T(1,128)S(1)}, f32[1,1024]{1,0:T(1,128)}, u32[]{:S(2)}) copy-start(f32[1,1024]{1,0:T(1,128)} %copy-done.41) | copy-start | bytes 12292
  121.4 89.3 %copy-start.44 = (f32[1,1024]{1,0:T(1,128)S(1)}, f32[1,1024]{1,0:T(1,128)}, u32[]{:S(2)}) copy-start(f32[1,1024]{1,0:T(1,128)} %copy-done.43) | copy-start | bytes 12292
  121.4 89.3 %copy-start.46 = (f32[1,1024]{1,0:T(1,128)S(1)}, f32[1,1024]{1,0:T(1,128)}, u32[]{:S(2)}) copy-start(f32[1,1024]{1,0:T(1,128)} %copy-done.45) | copy-start | bytes 12292
  121.4 89.3 %copy-start.48 = (f32[1,1024]{1,0:T(1,128)S(1)}, f32[1,1024]{1,0:T(1,128)}, u32[]{:S(2)}) copy-start(f32[1,1024]{1,0:T(1,128)} %copy-done.47) | copy-start | bytes 12292
  121.4 89.3 %copy-start.50 = (f32[1,1024]{1,0:T(1,128)S(1)}, f32[1,1024]{1,0:T(1,128)}, u32[]{:S(2)}) copy-start(f32[1,1024]{1,0:T(1,128)} %copy-done.49) | copy-start | bytes 12292
  (51 other events, 934.6 us)
Sparse Core Ops, SparseCore 0:
  9.7 12.3 all-gather.3
  23.6 10.2 all-gather.7
  35.4 13.2 all-gather.5
  121.3 87.4 all-reduce.7
where the time goes:
time: 222 us; the launch traced here: 220 us
  waiting for transfers between devices  127 us (57%)
  starting transfers between devices  35.8 us (16%)
  local copies, waits for them, and re-layouts  17.4 us (8%)
  between operations  15.7 us (7%)
  other arithmetic  13.9 us (6%)
  matrix products  10.6 us (5%)
    psum x1, waiting for transfers between devices, shards(): grad_kernel = lax.psum(local_terms, ('seq', 'dp', 'fsdp')) * norm_factor  86.3 us
    ppermute x2, starting transfers between devices, padded_2(): before = lax.ppermute(last, axis, up)  9.69 us
    all_to_all x1, waiting for transfers between devices, shards(): lax.all_to_all(copies.reshape(seq_count, row_count, 2 * group_width), 'se...  7.8 us
    all_to_all x1, waiting for transfers between devices, shards(): lax.all_to_all(dquery.reshape(seq_count, part_rows, group_width), 'seq',...  6.69 us
    all_gather x1, waiting for transfers between devices, shards(): lax.all_gather(qkv_weight, 'fsdp', axis=0, tiled=True)  6.59 us
    unnamed x139, local copies, waits for them, and re-layouts  5.94 us
    all_to_all x1, starting transfers between devices, shards(): lax.all_to_all(to_heads(grad_attn), 'seq', split_axis=0, concat_axis=0, t...  4.87 us
    all_to_all x1, starting transfers between devices, shards(): lax.all_to_all(to_heads(query_f.astype(jnp.bfloat16)), 'seq', split_axis=...  4.86 us
  transfers between devices with their start and end apart: 14, of which 9 were waited for; matrix products, arithmetic and copies ran while one was open for 13% of the time, Pallas kernels for 0%

commit v1 on v0

--- a/solution.py
+++ b/solution.py
@@ -1,8 +1,11 @@
+import functools
 import math
 
 import jax
 import jax.numpy as jnp
 from jax import lax
+from jax.experimental import pallas as pl
+from jax.experimental.pallas import tpu as pltpu
 from jax.sharding import PartitionSpec as P
 
 H = 8
@@ -263,7 +266,462 @@
     return (out_rows.reshape(tokens.shape), grad_tokens.reshape(tokens.shape), grad_kernel)
 
 
+def as_f32(value):
+    return value.astype(jnp.float32)
+
+
+def row_shift(value, step, inner):
+    rows = value.shape[0]
+    moved = pltpu.roll(value, step % rows, axis=0)
+    place = lax.rem(lax.broadcasted_iota(jnp.int32, value.shape, 0), inner)
+    return jnp.where(place == (0 if step == 1 else inner - 1), 0.0, moved)
+
+
+def slab_shift(value, step, inner):
+    if step == 0:
+        return value
+    empty = jnp.zeros((inner, value.shape[1]), value.dtype)
+    if step == 1:
+        return jnp.concatenate([empty, value[:-inner]], axis=0)
+    return jnp.concatenate([value[inner:], empty], axis=0)
+
+
+def conv_lanes(planes, taps, flipped, inner):
+    by_x = []
+    for tap_x in range(3):
+        total = None
+        for tap_y in range(3):
+            part = None
+            for tap_z in range(3):
+                index = 9 * tap_z + 3 * tap_y + tap_x
+                index = 26 - index if flipped else index
+                term = taps[index : index + 1] * planes[tap_z]
+                part = term if part is None else part + term
+            part = slab_shift(part, 1 - tap_y, inner)
+            total = part if total is None else total + part
+        by_x.append(total)
+    return by_x[1] + row_shift(by_x[0], 1, inner) + row_shift(by_x[2], -1, inner)
+
+
+def head_mean(value):
+    width = value.shape[1]
+    left = lax.broadcasted_iota(jnp.int32, (width, width), 0) // HD
+    right = lax.broadcasted_iota(jnp.int32, (width, width), 1) // HD
+    same = jnp.where(left == right, 1.0, 0.0).astype(jnp.bfloat16)
+    high = value.astype(jnp.bfloat16)
+    low = (value - as_f32(high)).astype(jnp.bfloat16)
+    total = jnp.dot(high, same, preferred_element_type=jnp.float32)
+    total = total + jnp.dot(low, same, preferred_element_type=jnp.float32)
+    return total * (1.0 / HD)
+
+
+def nt_dot(left, right):
+    return lax.dot_general(
+        left, right, (((1,), (1,)), ((), ())), preferred_element_type=jnp.float32
+    )
+
+
+def tn_dot(left, right):
+    return lax.dot_general(
+        left, right, (((0,), (0,)), ((), ())), preferred_element_type=jnp.float32
+    )
+
+
+def nn_dot(left, right):
+    return jnp.dot(left, right, preferred_element_type=jnp.float32)
+
+
+def front_body(slots, ids, feats, pxrd, wt_own, wt_oth, cot, wo_own, wo_oth, *rest):
+    mod, sends, by_group = rest[0], rest[1 : 1 + slots], rest[1 + slots]
+    me, half = ids[0], ids[1]
+    width = pxrd.shape[1]
+    projected = nn_dot(feats[0], wt_own[...]) + nn_dot(feats[1], wt_oth[...])
+    for row in range(3):
+        mod[row : row + 1, :] = projected[0:1, row * width : (row + 1) * width] + pxrd[row : row + 1, :]
+    gated = (mod[2:3, :] * as_f32(cot[...])).astype(jnp.bfloat16)
+    lanes = sends[0].shape[1]
+    per_half = wo_own.shape[0] // lanes
+    for weight, part in ((wo_own, half), (wo_oth, 1 - half)):
+        grads = nt_dot(gated, weight[...]).astype(jnp.bfloat16)
+        for j in range(per_half):
+            by_group[part * per_half + j] = grads[:, j * lanes : (j + 1) * lanes]
+    for k in range(slots):
+        sends[k][...] = by_group[lax.bitwise_xor(me, k)]
+
+
+def mix_body(slots, inner, ids, tok, up, down, taps, mod, w_own, w_oth, *rest):
+    resid, sections = rest[0], rest[1]
+    sends = rest[2 : 2 + slots]
+    normed, by_group = rest[2 + slots :]
+    me, half = ids[0], ids[1]
+    rows, width = tok.shape
+    step = 128
+    sums = jnp.zeros((rows, step), jnp.float32)
+    for start in range(0, width, step):
+        cols = slice(start, start + step)
+        planes = [as_f32(ref[:, cols]) for ref in (up, tok, down)]
+        mixed = conv_lanes(planes, taps[:, cols], False, inner)
+        rounded = (planes[1] + mixed).astype(jnp.bfloat16)
+        resid[:, cols] = rounded
+        sums = sums + as_f32(rounded)
+    mean = jnp.sum(sums, axis=1, keepdims=True) * (1.0 / width)
+    squares = jnp.zeros((rows, step), jnp.float32)
+    for start in range(0, width, step):
+        centre = as_f32(resid[:, start : start + step]) - mean
+        squares = squares + centre * centre
+    spread = jnp.sum(squares, axis=1, keepdims=True) * (1.0 / width)
+    inverse = lax.rsqrt(spread + 1e-06)
+    per_half = width // 2
+    for start in range(0, width, step):
+        cols = slice(start, start + step)
+        centre = as_f32(resid[:, cols]) - mean
+        value = centre * inverse * (1.0 + mod[1:2, cols]) + mod[0:1, cols]
+        inside = start % per_half
+        normed[start // per_half, :, inside : inside + step] = value.astype(jnp.bfloat16)
+    projected = nn_dot(normed[half], w_own[...]) + nn_dot(normed[1 - half], w_oth[...])
+    lanes = sends[0].shape[1] // 3
+    inner_width = H * HD
+    sections[...] = projected[:, : 2 * inner_width]
+    for group in range(slots):
+        for part in range(3):
+            block = projected[:, part * inner_width + group * lanes :][:, :lanes]
+            if part < 2:
+                block = block * lax.rsqrt(head_mean(block * block) + 1e-06)
+            by_group[group, :, part * lanes : (part + 1) * lanes] = block.astype(jnp.bfloat16)
+    for k in range(slots):
+        sends[k][...] = by_group[lax.bitwise_xor(me, k)]
+
+
+def attend_body(slots, *refs):
+    qkv_in, grads_in = refs[:slots], refs[slots : 2 * slots]
+    backs, attns = refs[2 * slots : 3 * slots], refs[3 * slots : 4 * slots]
+    keys, values, probs_all, dscore_all = refs[4 * slots :]
+    rows, lanes = grads_in[0].shape
+    heads = lanes // HD
+    scale = 1.0 / math.sqrt(HD)
+    for k in range(slots):
+        keys[k * rows : (k + 1) * rows, :] = qkv_in[k][:, lanes : 2 * lanes]
+        values[k * rows : (k + 1) * rows, :] = qkv_in[k][:, 2 * lanes :]
+    owner = lax.broadcasted_iota(jnp.int32, (rows, lanes), 1) // HD
+    for k in range(slots):
+        query = qkv_in[k][:, :lanes]
+        grad = grads_in[k][...]
+        attn_total = None
+        pieces = []
+        for head in range(heads):
+            mine = owner == head
+            scores = nt_dot(jnp.where(mine, query, jnp.zeros_like(query)), keys[...]) * scale
+            expo = jnp.exp(scores)
+            weights = expo * (1.0 / jnp.sum(expo, axis=1, keepdims=True))
+            probs = weights.astype(jnp.bfloat16)
+            probs_all[head, k * rows : (k + 1) * rows, :] = probs
+            attn = jnp.where(mine, nn_dot(probs, values[...]), 0.0)
+            attn_total = attn if attn_total is None else attn_total + attn
+            pieces.append(weights)
+        attn_total = attn_total.astype(jnp.bfloat16)
+        attns[k][...] = attn_total
+        product = as_f32(attn_total) * as_f32(grad)
+        dquery = None
+        for head in range(heads):
+            mine = owner == head
+            delta = jnp.sum(jnp.where(mine, product, 0.0), axis=1, keepdims=True)
+            dprob = nt_dot(jnp.where(mine, grad, jnp.zeros_like(grad)), values[...])
+            dscore = (pieces[head] * (dprob - delta) * scale).astype(jnp.bfloat16)
+            dscore_all[head, k * rows : (k + 1) * rows, :] = dscore
+            part = jnp.where(mine, nn_dot(dscore, keys[...]), 0.0)
+            dquery = part if dquery is None else dquery + part
+        backs[k][:, :lanes] = dquery.astype(jnp.bfloat16)
+    queries = jnp.concatenate([ref[:, :lanes] for ref in qkv_in], axis=0)
+    grads = jnp.concatenate([ref[...] for ref in grads_in], axis=0)
+    owner_all = lax.broadcasted_iota(jnp.int32, queries.shape, 1) // HD
+    dkeys = None
+    dvalues = None
+    for head in range(heads):
+        mine = owner_all == head
+        dkey = jnp.where(mine, tn_dot(dscore_all[head], queries), 0.0)
+        dvalue = jnp.where(mine, tn_dot(probs_all[head], grads), 0.0)
+        dkeys = dkey if dkeys is None else dkeys + dkey
+        dvalues = dvalue if dvalues is None else dvalues + dvalue
+    for k in range(slots):
+        backs[k][:, lanes : 2 * lanes] = dkeys[k * rows : (k + 1) * rows].astype(jnp.bfloat16)
+        backs[k][:, 2 * lanes :] = dvalues[k * rows : (k + 1) * rows].astype(jnp.bfloat16)
+
+
+def tail_body(slots, inner, ids, *refs):
+    backs = refs[:slots]
+    sections, resid, cot, mod, w_own, w_oth, tok, up, down = refs[slots : slots + 9]
+    dresid, terms = refs[slots + 9 : slots + 11]
+    by_group, dproj, dnormed, sums = refs[slots + 11 :]
+    me, half = ids[0], ids[1]
+    rows, width = resid.shape
+    lanes = by_group.shape[3]
+    inner_width = H * HD
+    for k in range(slots):
+        group = lax.bitwise_xor(me, k)
+        for part in range(3):
+            by_group[group, part] = backs[k][:, part * lanes : (part + 1) * lanes]
+    for group in range(slots):
+        for part in range(3):
+            start = part * inner_width + group * lanes
+            grad = by_group[group, part]
+            if part < 2:
+                grad = as_f32(grad)
+                block = sections[:, start : start + lanes]
+                inverse = lax.rsqrt(head_mean(block * block) + 1e-06)
+                unit = block * inverse
+                grad = (inverse * (grad - unit * head_mean(grad * unit))).astype(jnp.bfloat16)
+            dproj[:, start : start + lanes] = grad
+    dnormed[half] = nt_dot(dproj[...], w_own[...])
+    dnormed[1 - half] = nt_dot(dproj[...], w_oth[...])
+    step = 128
+    per_half = width // 2
+    total = jnp.zeros((rows, step), jnp.float32)
+    for start in range(0, width, step):
+        total = total + as_f32(resid[:, start : start + step])
+    mean = jnp.sum(total, axis=1, keepdims=True) * (1.0 / width)
+    total = jnp.zeros((rows, step), jnp.float32)
+    for start in range(0, width, step):
+        centre = as_f32(resid[:, start : start + step]) - mean
+        total = total + centre * centre
+    inverse = lax.rsqrt(jnp.sum(total, axis=1, keepdims=True) * (1.0 / width) + 1e-06)
+    plain = jnp.zeros((rows, step), jnp.float32)
+    crossed = jnp.zeros((rows, step), jnp.float32)
+    for start in range(0, width, step):
+        cols = slice(start, start + step)
+        inside = start % per_half
+        grad = dnormed[start // per_half, :, inside : inside + step] * (1.0 + mod[1:2, cols])
+        unit = (as_f32(resid[:, cols]) - mean) * inverse
+        plain = plain + grad
+        crossed = crossed + grad * unit
+    plain = jnp.sum(plain, axis=1, keepdims=True) * (1.0 / width)
+    crossed = jnp.sum(crossed, axis=1, keepdims=True) * (1.0 / width)
+    for start in range(0, width, step):
+        cols = slice(start, start + step)
+        inside = start % per_half
+        grad = dnormed[start // per_half, :, inside : inside + step] * (1.0 + mod[1:2, cols])
+        unit = (as_f32(resid[:, cols]) - mean) * inverse
+        stream = as_f32(cot[:, cols]) + inverse * (grad - plain - unit * crossed)
+        dresid[:, cols] = stream.astype(jnp.bfloat16)
+    for start in range(0, width, step):
+        cols = slice(start, start + step)
+        grad = as_f32(dresid[:, cols])
+        moved = [row_shift(grad, -1, inner), grad, row_shift(grad, 1, inner)]
+        for tap_z, ref in enumerate((up, tok, down)):
+            plane = as_f32(ref[:, cols])
+            for tap_y in range(3):
+                low, high = max(0, 1 - tap_y), max(0, tap_y - 1)
+                for tap_x in range(3):
+                    index = 9 * tap_z + 3 * tap_y + tap_x
+                    prod = (
+                        plane[high * inner : rows - low * inner]
+                        * moved[tap_x][low * inner : rows - high * inner]
+                    )
+                    prod = jnp.sum(prod.reshape(-1, 8, step), axis=0)
+                    terms[index : index + 1, cols] = jnp.sum(prod, axis=0, keepdims=True)
+
+
+def out_body(slots, ids, *refs):
+    attns = refs[:slots]
+    resid, mod, wo_own, wo_oth, out, by_group = refs[slots:]
+    me, half = ids[0], ids[1]
+    lanes = attns[0].shape[1]
+    per_half = wo_own.shape[0] // lanes
+    for k in range(slots):
+        by_group[lax.bitwise_xor(me, k)] = attns[k][...]
+    total = None
+    for weight, part in ((wo_own, half), (wo_oth, 1 - half)):
+        for j in range(per_half):
+            term = nn_dot(by_group[part * per_half + j], weight[j * lanes : (j + 1) * lanes, :])
+            total = term if total is None else total + term
+    out[...] = (as_f32(resid[...]) + mod[2:3, :] * total).astype(jnp.bfloat16)
+
+
+def back_conv_body(inner, grad, up, down, taps, out):
+    width = grad.shape[1]
+    step = 128
+    for start in range(0, width, step):
+        cols = slice(start, start + step)
+        planes = [as_f32(ref[:, cols]) for ref in (up, grad, down)]
+        mixed = conv_lanes(planes, taps[:, cols], True, inner)
+        out[:, cols] = (planes[1] + mixed).astype(jnp.bfloat16)
+
+
+def pair_body(last, left, right, out):
+    total = as_f32(left[...]) + as_f32(right[...])
+    out[...] = total.astype(out.dtype)
+
+
+def final_body(factor, slots, *refs):
+    values = [as_f32(ref[...]) for ref in refs[:slots]]
+    while len(values) > 1:
+        values = [values[i] + values[i + 1] for i in range(0, len(values), 2)]
+    refs[slots][...] = values[0] * factor
+
+
+def call(body, name, outs, args, scratch=(), flops=0, scalars=False):
+    whole = pl.BlockSpec(memory_space=pltpu.VMEM)
+    specs = [whole] * len(args)
+    if scalars:
+        specs[0] = pl.BlockSpec(memory_space=pltpu.SMEM)
+    sizes = [math.prod(a.shape) * a.dtype.itemsize for a in list(args) + list(outs)]
+    return pl.pallas_call(
+        body,
+        out_shape=tuple(outs),
+        in_specs=specs,
+        out_specs=(whole,) * len(outs),
+        scratch_shapes=list(scratch),
+        compiler_params=pltpu.CompilerParams(vmem_limit_bytes=40 * 2**20),
+        cost_estimate=pl.CostEstimate(flops=flops, bytes_accessed=sum(sizes), transcendentals=0),
+        name=name,
+    )(*args)
+
+
+def swapped(value, axis, distance):
+    count = lax.axis_size(axis)
+    return lax.ppermute(value, axis, [(i, i ^ distance) for i in range(count)])
+
+
+def exchanged(pieces):
+    return [pieces[0]] + [swapped(pieces[k], "seq", k) for k in range(1, len(pieces))]
+
+
+def neighbours(value):
+    count = lax.axis_size("seq")
+    up = [(i, i + 1) for i in range(count - 1)]
+    down = [(i + 1, i) for i in range(count - 1)]
+    return lax.ppermute(value, "seq", up), lax.ppermute(value, "seq", down)
+
+
+def slab_shards(
+    tokens, timesteps, pxrd_mod, time_weight, conv_kernel, qkv_weight, out_weight, out_cot
+):
+    bf16, f32 = jnp.bfloat16, jnp.float32
+    side_y, inner, width = tokens.shape[2:]
+    rows = side_y * inner
+    slots = lax.axis_size("seq")
+    lanes = H * HD // slots
+    me = lax.axis_index("seq")
+    half = lax.axis_index("fsdp")
+    ids = jnp.stack([me, half]).astype(jnp.int32)
+    tok = tokens.reshape(rows, width)
+    cot = out_cot.reshape(rows, width)
+    shape = jax.ShapeDtypeStruct
+
+    wo_oth = swapped(out_weight, "fsdp", 1)
+    wt_oth = swapped(time_weight, "fsdp", 1)
+    up, down = neighbours(tok)
+    wq_oth = swapped(qkv_weight, "fsdp", 1)
+
+    freq = 2 * time_weight.shape[0]
+    feats = time_features(timesteps, freq).reshape(2, freq // 2)
+    own = lax.dynamic_slice_in_dim(feats, half, 1, axis=0)
+    oth = lax.dynamic_slice_in_dim(feats, 1 - half, 1, axis=0)
+    feats = jnp.broadcast_to(jnp.stack([own, oth]), (2, 8, freq // 2))
+    front = call(
+        functools.partial(front_body, slots),
+        "front",
+        [shape((3, width), f32)] + [shape((rows, lanes), bf16)] * slots,
+        (ids, feats, pxrd_mod[0], time_weight, wt_oth, cot, out_weight, wo_oth),
+        [pltpu.VMEM((slots, rows, lanes), bf16)],
+        flops=2 * rows * width * H * HD,
+        scalars=True,
+    )
+    mod = front[0]
+    grads_in = exchanged(front[1:])
+
+    mixed = call(
+        functools.partial(mix_body, slots, inner),
+        "mix",
+        [shape((rows, width), bf16), shape((rows, 2 * H * HD), f32)]
+        + [shape((rows, 3 * lanes), bf16)] * slots,
+        (ids, tok, up, down, conv_kernel, mod, qkv_weight, wq_oth),
+        [pltpu.VMEM((2, rows, width // 2), bf16), pltpu.VMEM((slots, rows, 3 * lanes), bf16)],
+        flops=2 * rows * width * 3 * H * HD,
+        scalars=True,
+    )
+    resid, sections = mixed[:2]
+    qkv_in = exchanged(mixed[2:])
+    count = slots * rows
+    attended = call(
+        functools.partial(attend_body, slots),
+        "attend",
+        [shape((rows, 3 * lanes), bf16)] * slots + [shape((rows, lanes), bf16)] * slots,
+        (*qkv_in, *grads_in),
+        [pltpu.VMEM((count, lanes), bf16)] * 2
+        + [pltpu.VMEM((lanes // HD, count, count), bf16)] * 2,
+        flops=12 * count * count * lanes,
+    )
+    backs = exchanged(attended[:slots])
+    attns = exchanged(attended[slots:])
+    dresid, terms = call(
+        functools.partial(tail_body, slots, inner),
+        "tail",
+        [shape((rows, width), bf16), shape((27, width), f32)],
+        (ids, *backs, sections, resid, cot, mod, qkv_weight, wq_oth, tok, up, down),
+        [
+            pltpu.VMEM((slots, 3, rows, lanes), bf16),
+            pltpu.VMEM((rows, 3 * H * HD), bf16),
+            pltpu.VMEM((2, rows, width // 2), f32),
+            pltpu.VMEM((8, width), f32),
+        ],
+        flops=2 * rows * width * 3 * H * HD,
+        scalars=True,
+    )
+    (out,) = call(
+        functools.partial(out_body, slots),
+        "out",
+        [shape((rows, width), bf16)],
+        (ids, *attns, resid, mod, out_weight, wo_oth),
+        [pltpu.VMEM((slots, rows, lanes), bf16)],
+        flops=2 * rows * width * H * HD,
+        scalars=True,
+    )
+    (terms,) = call(
+        functools.partial(pair_body, False),
+        "add_fsdp",
+        [shape((27, width), bf16)],
+        (terms, swapped(terms, "fsdp", 1)),
+    )
+    (terms,) = call(
+        functools.partial(pair_body, False),
+        "add_dp",
+        [shape((27, width), bf16)],
+        (terms, swapped(terms, "dp", 1)),
+    )
+    factor = 1.0 / math.sqrt(lax.axis_size("dp") * lax.axis_size("fsdp") * slots * rows)
+    (kernel_grad,) = call(
+        functools.partial(final_body, factor, slots),
+        "add_seq",
+        [shape((27, width), f32)],
+        exchanged([terms] * slots),
+    )
+    grad_up, grad_down = neighbours(dresid)
+    (token_grad,) = call(
+        functools.partial(back_conv_body, inner),
+        "back_conv",
+        [shape((rows, width), bf16)],
+        (dresid, grad_up, grad_down, conv_kernel),
+    )
+    return out.reshape(tokens.shape), token_grad.reshape(tokens.shape), kernel_grad
+
+
 def solution(mesh):
+    count = mesh.shape["seq"]
+
+    def pick(*args):
+        tokens, time_weight = args[0], args[3]
+        lanes = H * HD // count
+        fits = (
+            count in (2, 4)
+            and tokens.shape[0] == 1
+            and tokens.shape[1] == 1
+            and tokens.shape[3] % 16 == 0
+            and lanes % 128 == 0
+            and mesh.shape["dp"] == 2
+            and mesh.shape["fsdp"] == 2
+        )
+        return slab_shards(*args) if fits else shards(*args)
+
     placed = (
         P(("groups", "dp", "fsdp"), "seq", None, None, None),
         P(("groups", "dp", "fsdp")),
@@ -275,7 +733,7 @@
         P(("groups", "dp", "fsdp"), "seq", None, None, None),
     )
     return jax.shard_map(
-        shards,
+        pick,
         mesh=mesh,
         in_specs=placed,
         out_specs=(

time: 222 us -> 79 us (0.36)
  waiting for transfers between devices: 127 us -> 14.2 us
  Pallas kernels: 0 us -> 18.3 us
  between operations: 15.7 us -> 1.49 us
  other arithmetic: 13.9 us -> 0.15 us
  local copies, waits for them, and re-layouts: 17.4 us -> 3.86 us
  matrix products: 10.6 us -> 0 us
  starting transfers between devices: 35.8 us -> 40.5 us
    psum x1 -> x0, waiting for transfers between devices: 86.3 us -> none  [shards(): grad_kernel = lax.psum(local_terms, ('seq', 'dp', 'fsdp')) * norm_factor]
    ppermute x4 -> x24, starting transfers between devices: 12.3 us -> 40.5 us  [the longest x20 27.5 us: swapped(): return lax.ppermute(value, axis, [(i, i ^ distance) for i in range(count)])]
    all_to_all x6 -> x0, waiting for transfers between devices: 23.9 us -> none  [the longest x1 7.8 us: shards(): lax.all_to_all(copies.reshape(seq_count, row_count, 2 * group_width), 'se...]
    all_to_all x6 -> x0, starting transfers between devices: 23.4 us -> none  [the longest x1 4.87 us: shards(): lax.all_to_all(to_heads(grad_attn), 'seq', split_axis=0, concat_axis=0, t...]
    pallas_call x0 -> x9, Pallas kernels: none -> 18.3 us  [call(): pl.pallas_call(body, out_shape=tuple(outs), in_specs=specs, out_specs=(wh...]
    dot_general x11 -> x0, matrix products: 10.6 us -> none  [the longest x1 2.01 us: modulation(): jnp.dot(features, time_weight, preferred_element_type=jnp.float32)]
    all_gather x3 -> x0, waiting for transfers between devices: 7.88 us -> none  [the longest x1 6.59 us: shards(): lax.all_gather(qkv_weight, 'fsdp', axis=0, tiled=True)]
    ppermute x4 -> x24, waiting for transfers between devices: 7.28 us -> 14.2 us  [the longest x20 14.2 us: swapped(): return lax.ppermute(value, axis, [(i, i ^ distance) for i in range(count)])]
  transfers between devices with their start and end apart: 14 -> 24, of which waited for: 9 -> 11; matrix products, arithmetic and copies ran while one was open for 13% -> 1% of each run, Pallas kernels for 0% -> 6%
where the time goes in v1:
time: 79 us; the launch traced here: 78.5 us
  starting transfers between devices  40.5 us (51%)
  Pallas kernels  18.3 us (23%)
  waiting for transfers between devices  14.2 us (18%)
  local copies, waits for them, and re-layouts  3.86 us (5%)
  between operations  1.49 us (2%)
    ppermute x20, starting transfers between devices, swapped(): return lax.ppermute(value, axis, [(i, i ^ distance) for i in range(count)])  27.5 us
    pallas_call x9, Pallas kernels, call(): pl.pallas_call(body, out_shape=tuple(outs), in_specs=specs, out_specs=(wh...  18.3 us
    ppermute x20, waiting for transfers between devices, swapped(): return lax.ppermute(value, axis, [(i, i ^ distance) for i in range(count)])  14.2 us
    ppermute x4, starting transfers between devices, neighbours(): return (lax.ppermute(value, 'seq', up), lax.ppermute(value, 'seq', down))  13 us
    unnamed x14, local copies, waits for them, and re-layouts  3.85 us
  transfers between devices with their start and end apart: 24, of which 11 were waited for; matrix products, arithmetic and copies ran while one was open for 1% of the time, Pallas kernels for 6%

profile of v1, /device:TPU:0, one launch (start us, length us, event | category | flops | bytes accessed | tf_op | source)
XLA Modules:
  0.0 78.5 jit_solution(5212095315013353684)
XLA Ops:
  1.7 1.3 %collective-permute-start.1 = (bf16[128,1024]{1,0:T(8,128)(2,1)}, bf16[128,1024]{1,0:T(8,128)(2,1)S(1)}, u32[]{:S(2)}, u32[]{:S(2)}) collective-permute-start(bf16[128,1024]{1,0:T(8,128)(2,1)} %bitcast.18), channel_id=1, source_target_pairs={{4,0},{8,4},{12,8},{5,1},{9,5},{13,9},{6,2},{10,6},{14,10},{7,3},{... | collective-permute-start | bytes 786440 | tf_op jit(solution)/shard_map/ppermute | solution.py:592
  3.0 5.9 %collective-permute-start = (bf16[128,1024]{1,0:T(8,128)(2,1)}, bf16[128,1024]{1,0:T(8,128)(2,1)}, u32[]{:S(2)}, u32[]{:S(2)}) collective-permute-start(bf16[128,1024]{1,0:T(8,128)(2,1)} %bitcast.19), channel_id=1, source_target_pairs={{0,4},{4,8},{8,12},{1,5},{5,9},{9,13},{2,6},{6,10},{10,14},{3,7},{... | collective-permute-start | bytes 786440 | tf_op jit(solution)/shard_map/ppermute | solution.py:592
  9.6 0.7 copy.15
  10.4 1.0 %copy-done.1 = bf16[256,1024]{1,0:T(8,128)(2,1)S(1)} copy-done((bf16[256,1024]{1,0:T(8,128)(2,1)S(1)}, bf16[256,1024]{1,0:T(8,128)(2,1)}, u32[]{:S(2)}) %copy-start.1) | copy-done | bytes 524312
  11.5 0.9 %copy-done.3 = bf16[1,1,8,16,1024]{4,3,2,1,0:T(8,128)(2,1)S(1)} copy-done((bf16[1,1,8,16,1024]{4,3,2,1,0:T(8,128)(2,1)S(1)}, bf16[1,1,8,16,1024]{4,3,2,1,0:T(8,128)(2,1)}, u32[]{:S(2)}) %copy-start.3) | copy-done | bytes 262168
  12.4 1.1 %copy-done.4 = bf16[128,3072]{1,0:T(8,128)(2,1)S(1)} copy-done((bf16[128,3072]{1,0:T(8,128)(2,1)S(1)}, bf16[128,3072]{1,0:T(8,128)(2,1)}, u32[]{:S(2)}) %copy-start.4) | copy-done | bytes 786456
  13.6 2.1 %front.1 = (f32[3,1024]{1,0:T(4,128)S(1)}, bf16[128,128]{1,0:T(8,128)(2,1)S(1)}, bf16[128,128]{1,0:T(8,128)(2,1)S(1)}, bf16[128,128]{1,0:T(8,128)(2,1)S(1)}, bf16[128,128]{1,0:T(8,128)(2,1)S(1)}) custom-call(s32[2]{0:T(128)S(1)} %pad_add_fusion.ids, bf16[2,8,128]{2,1,0:T(8,128)(2,1)S(1)} %broadcast_in_dim.10.feats, f32[3,1024]{1,0:T(4,128)S(1)} %bitcast.24, ...), custom_call_target="tpu_custom_call" | custom-call | flops 134217728 | bytes 3043336 | tf_op jit(solution)/shard_map/front/pallas_call | solution.py:567
  15.7 3.1 %mix.1 = (bf16[128,1024]{1,0:T(8,128)(2,1)S(1)}, f32[128,1024]{1,0:T(8,128)S(1)}, bf16[128,384]{1,0:T(8,128)(2,1)S(1)}, bf16[128,384]{1,0:T(8,128)(2,1)S(1)}, bf...) custom-call(s32[2]{0:T(128)S(1)} %pad_add_fusion.ids, bf16[128,1024]{1,0:T(8,128)(2,1)S(1)} %bitcast.20, ...), custom_call_target="tpu_custom_call" | custom-call | flops 402653184 | bytes 5234696 | tf_op jit(solution)/shard_map/mix/pallas_call | solution.py:567
  18.8 1.5 %collective-permute-start.5 = (bf16[128,384]{1,0:T(8,128)(2,1)S(1)}, bf16[128,384]{1,0:T(8,128)(2,1)S(1)}, u32[]{:S(2)}, u32[]{:S(2)}) collective-permute-start(bf16[128,384]{1,0:T(8,128)(2,1)S(1)} %get-tuple-element.26), channel_id=1, source_target_pairs={{0,4},{4,0},{8,12},{12,8},{1,5},{5,1},{9,13},{13,9},{2,6},{6,2},{1... | collective-permute-start | bytes 294920 | tf_op jit(solution)/shard_map/ppermute | solution.py:581
  20.3 2.8 %collective-permute-start.6 = (bf16[128,384]{1,0:T(8,128)(2,1)S(1)}, bf16[128,384]{1,0:T(8,128)(2,1)S(1)}, u32[]{:S(2)}, u32[]{:S(2)}) collective-permute-start(bf16[128,384]{1,0:T(8,128)(2,1)S(1)} %get-tuple-element.27), channel_id=1, source_target_pairs={{0,8},{4,12},{8,0},{12,4},{1,9},{5,13},{9,1},{13,5},{2,10},{6,14},... | collective-permute-start | bytes 294920 | tf_op jit(solution)/shard_map/ppermute | solution.py:581
  23.8 3.7 %collective-permute-start.9 = (bf16[128,128]{1,0:T(8,128)(2,1)S(1)}, bf16[128,128]{1,0:T(8,128)(2,1)S(1)}, u32[]{:S(2)}, u32[]{:S(2)}) collective-permute-start(bf16[128,128]{1,0:T(8,128)(2,1)S(1)} %get-tuple-element.31), channel_id=1, source_target_pairs={{0,8},{4,12},{8,0},{12,4},{1,9},{5,13},{9,1},{13,5},{2,10},{6,14},... | collective-permute-start | bytes 98312 | tf_op jit(solution)/shard_map/ppermute | solution.py:581
  27.7 4.3 %collective-permute-start.10 = (bf16[128,128]{1,0:T(8,128)(2,1)S(1)}, bf16[128,128]{1,0:T(8,128)(2,1)S(1)}, u32[]{:S(2)}, u32[]{:S(2)}) collective-permute-start(bf16[128,128]{1,0:T(8,128)(2,1)S(1)} %get-tuple-element.32), channel_id=1, source_target_pairs={{0,12},{4,8},{8,4},{12,0},{1,13},{5,9},{9,5},{13,1},{2,14},{6,10},... | collective-permute-start | bytes 98312 | tf_op jit(solution)/shard_map/ppermute | solution.py:581
  31.9 2.2 %collective-permute-done.9.refs_6_ = bf16[128,128]{1,0:T(8,128)(2,1)S(1)} collective-permute-done((bf16[128,128]{1,0:T(8,128)(2,1)S(1)}, bf16[128,128]{1,0:T(8,128)(2,1)S(1)}, u32[]{:S(2)}, u32[]{:S(2)}) %collective-permute-start.9) | collective-permute-done | bytes 32800 | tf_op jit(solution)/shard_map/ppermute | solution.py:581
  34.2 4.4 %attend.1 = (bf16[128,384]{1,0:T(8,128)(2,1)S(1)}, bf16[128,384]{1,0:T(8,128)(2,1)S(1)}, bf16[128,384]{1,0:T(8,128)(2,1)S(1)}, bf16[128,384]{1,0:T(8,128)(2,1)S(...) custom-call(bf16[128,384]{1,0:T(8,128)(2,1)S(1)} %get-tuple-element., ...), custom_call_target="tpu_custom_call" | custom-call | flops 402653184 | bytes 1048576 | tf_op jit(solution)/shard_map/attend/pallas_call | solution.py:567
  38.6 1.0 %collective-permute-start.14 = (bf16[128,384]{1,0:T(8,128)(2,1)S(1)}, bf16[128,384]{1,0:T(8,128)(2,1)S(1)}, u32[]{:S(2)}, u32[]{:S(2)}) collective-permute-start(bf16[128,384]{1,0:T(8,128)(2,1)S(1)} %get-tuple-element.39), channel_id=1, source_target_pairs={{0,4},{4,0},{8,12},{12,8},{1,5},{5,1},{9,13},{13,9},{2,6},{6,2},{1... | collective-permute-start | bytes 294920 | tf_op jit(solution)/shard_map/ppermute | solution.py:581
  39.6 3.1 %collective-permute-start.15 = (bf16[128,384]{1,0:T(8,128)(2,1)S(1)}, bf16[128,384]{1,0:T(8,128)(2,1)S(1)}, u32[]{:S(2)}, u32[]{:S(2)}) collective-permute-start(bf16[128,384]{1,0:T(8,128)(2,1)S(1)} %get-tuple-element.40), channel_id=1, source_target_pairs={{0,8},{4,12},{8,0},{12,4},{1,9},{5,13},{9,1},{13,5},{2,10},{6,14},... | collective-permute-start | bytes 294920 | tf_op jit(solution)/shard_map/ppermute | solution.py:581
  43.6 4.2 %collective-permute-done.15.refs_2_ = bf16[128,384]{1,0:T(8,128)(2,1)S(1)} collective-permute-done((bf16[128,384]{1,0:T(8,128)(2,1)S(1)}, bf16[128,384]{1,0:T(8,128)(2,1)S(1)}, u32[]{:S(2)}, u32[]{:S(2)}) %collective-permute-start.15) | collective-permute-done | bytes 98336 | tf_op jit(solution)/shard_map/ppermute | solution.py:581
  47.8 1.4 %collective-permute-done.16.refs_3_ = bf16[128,384]{1,0:T(8,128)(2,1)S(1)} collective-permute-done((bf16[128,384]{1,0:T(8,128)(2,1)S(1)}, bf16[128,384]{1,0:T(8,128)(2,1)S(1)}, u32[]{:S(2)}, u32[]{:S(2)}) %collective-permute-start.16) | collective-permute-done | bytes 98336 | tf_op jit(solution)/shard_map/ppermute | solution.py:581
  49.2 4.0 %tail.1 = (bf16[128,1024]{1,0:T(8,128)(2,1)S(1)}, f32[27,1024]{1,0:T(8,128)S(1)}) custom-call(s32[2]{0:T(128)S(1)} %pad_add_fusion.ids, bf16[128,384]{1,0:T(8,128)(2,1)S(1)} %get-tuple-element.38.refs_0_, bf16[128,384]{1,0:T(8,128)(2,1)S(1)} %collective-permute-done.14.refs_1_, bf16[128,384]{1,0:T(8,128)(2,1)S(1)} %collective-permute-done.15.refs_2_, ...), custom_call_target="tpu_custom_call" | custom-call | flops 402653184 | bytes 5758984 | tf_op jit(solution)/shard_map/tail/pallas_call | solution.py:567
  53.2 1.3 %collective-permute-start.18 = (bf16[128,1024]{1,0:T(8,128)(2,1)S(1)}, bf16[128,1024]{1,0:T(8,128)(2,1)S(1)}, u32[]{:S(2)}, u32[]{:S(2)}) collective-permute-start(bf16[128,1024]{1,0:T(8,128)(2,1)S(1)} %get-tuple-element.43.grad), channel_id=1, source_target_pairs={{4,0},{8,4},{12,8},{5,1},{9,5},{13,9},{6,2},{10,6},{14,10},{7,3},{... | collective-permute-start | bytes 786440 | tf_op jit(solution)/shard_map/ppermute | solution.py:592
  54.5 4.6 %collective-permute-start.17 = (bf16[128,1024]{1,0:T(8,128)(2,1)S(1)}, bf16[128,1024]{1,0:T(8,128)(2,1)S(1)}, u32[]{:S(2)}, u32[]{:S(2)}) collective-permute-start(bf16[128,1024]{1,0:T(8,128)(2,1)S(1)} %get-tuple-element.43.grad), channel_id=1, source_target_pairs={{0,4},{4,8},{8,12},{1,5},{5,9},{9,13},{2,6},{6,10},{10,14},{3,7},{... | collective-permute-start | bytes 786440 | tf_op jit(solution)/shard_map/ppermute | solution.py:592
  59.2 1.3 %collective-permute-done.19.right = f32[27,1024]{1,0:T(8,128)S(1)} collective-permute-done((f32[27,1024]{1,0:T(8,128)S(1)}, f32[27,1024]{1,0:T(8,128)S(1)}, u32[]{:S(2)}, u32[]{:S(2)}) %collective-permute-start.19) | collective-permute-done | bytes 110624 | tf_op jit(solution)/shard_map/ppermute | solution.py:581
  60.6 1.5 %collective-permute-start.20 = (bf16[27,1024]{1,0:T(8,128)(2,1)S(1)}, bf16[27,1024]{1,0:T(8,128)(2,1)S(1)}, u32[]{:S(2)}, u32[]{:S(2)}) collective-permute-start(bf16[27,1024]{1,0:T(8,128)(2,1)S(1)} %add_fsdp.1.left), channel_id=1, source_target_pairs={{0,2},{2,0},{1,3},{3,1},{4,6},{6,4},{5,7},{7,5},{8,10},{10,8},{9,1... | collective-permute-start | bytes 165896 | tf_op jit(solution)/shard_map/ppermute | solution.py:581
  62.0 1.3 %collective-permute-start.11 = (bf16[128,128]{1,0:T(8,128)(2,1)S(1)}, bf16[128,128]{1,0:T(8,128)(2,1)S(1)}, u32[]{:S(2)}, u32[]{:S(2)}) collective-permute-start(bf16[128,128]{1,0:T(8,128)(2,1)S(1)} %get-tuple-element.34), channel_id=1, source_target_pairs={{0,4},{4,0},{8,12},{12,8},{1,5},{5,1},{9,13},{13,9},{2,6},{6,2},{1... | collective-permute-start | bytes 98312 | tf_op jit(solution)/shard_map/ppermute | solution.py:581
  63.3 1.0 %collective-permute-start.12 = (bf16[128,128]{1,0:T(8,128)(2,1)S(1)}, bf16[128,128]{1,0:T(8,128)(2,1)S(1)}, u32[]{:S(2)}, u32[]{:S(2)}) collective-permute-start(bf16[128,128]{1,0:T(8,128)(2,1)S(1)} %get-tuple-element.35), channel_id=1, source_target_pairs={{0,8},{4,12},{8,0},{12,4},{1,9},{5,13},{9,1},{13,5},{2,10},{6,14},... | collective-permute-start | bytes 98312 | tf_op jit(solution)/shard_map/ppermute | solution.py:581
  64.9 1.5 %collective-permute-start.13 = (bf16[128,128]{1,0:T(8,128)(2,1)S(1)}, bf16[128,128]{1,0:T(8,128)(2,1)S(1)}, u32[]{:S(2)}, u32[]{:S(2)}) collective-permute-start(bf16[128,128]{1,0:T(8,128)(2,1)S(1)} %get-tuple-element.36), channel_id=1, source_target_pairs={{0,12},{4,8},{8,4},{12,0},{1,13},{5,9},{9,5},{13,1},{2,14},{6,10},... | collective-permute-start | bytes 98312 | tf_op jit(solution)/shard_map/ppermute | solution.py:581
  66.4 2.4 %collective-permute-start.23 = (bf16[27,1024]{1,0:T(8,128)(2,1)S(1)}, bf16[27,1024]{1,0:T(8,128)(2,1)S(1)}, u32[]{:S(2)}, u32[]{:S(2)}) collective-permute-start(bf16[27,1024]{1,0:T(8,128)(2,1)S(1)} %add_dp.1.refs_0_), channel_id=1, source_target_pairs={{0,12},{4,8},{8,4},{12,0},{1,13},{5,9},{9,5},{13,1},{2,14},{6,10},... | collective-permute-start | bytes 165896 | tf_op jit(solution)/shard_map/ppermute | solution.py:581
  69.3 1.8 %collective-permute-done.13.refs_3_ = bf16[128,128]{1,0:T(8,128)(2,1)S(1)} collective-permute-done((bf16[128,128]{1,0:T(8,128)(2,1)S(1)}, bf16[128,128]{1,0:T(8,128)(2,1)S(1)}, u32[]{:S(2)}, u32[]{:S(2)}) %collective-permute-start.13) | collective-permute-done | bytes 32800 | tf_op jit(solution)/shard_map/ppermute | solution.py:581
  71.0 1.3 %collective-permute-start.21 = (bf16[27,1024]{1,0:T(8,128)(2,1)S(1)}, bf16[27,1024]{1,0:T(8,128)(2,1)S(1)}, u32[]{:S(2)}, u32[]{:S(2)}) collective-permute-start(bf16[27,1024]{1,0:T(8,128)(2,1)S(1)} %add_dp.1.refs_0_), channel_id=1, source_target_pairs={{0,4},{4,0},{8,12},{12,8},{1,5},{5,1},{9,13},{13,9},{2,6},{6,2},{1... | collective-permute-start | bytes 165896 | tf_op jit(solution)/shard_map/ppermute | solution.py:581
  72.3 2.2 %out.1 = bf16[128,1024]{1,0:T(8,128)(2,1)} custom-call(s32[2]{0:T(128)S(1)} %pad_add_fusion.ids, bf16[128,128]{1,0:T(8,128)(2,1)S(1)} %get-tuple-element.33.refs_0_, bf16[128,128]{1,0:T(8,128)(2,1)S(1)} %collective-permute-done.11.refs_1_, bf16[128,128]{1,0:T(8,128)(2,1)S(1)} %collective-permute-done.12.refs_2_, ...), custom_call_target="tpu_custom_call" | custom-call | flops 134217728 | bytes 1716232 | tf_op jit(solution)/shard_map/out/pallas_call | solution.py:567
  74.5 0.9 %collective-permute-done.22.refs_2_ = bf16[27,1024]{1,0:T(8,128)(2,1)S(1)} collective-permute-done((bf16[27,1024]{1,0:T(8,128)(2,1)S(1)}, bf16[27,1024]{1,0:T(8,128)(2,1)S(1)}, u32[]{:S(2)}, u32[]{:S(2)}) %collective-permute-start.22) | collective-permute-done | bytes 55328 | tf_op jit(solution)/shard_map/ppermute | solution.py:581
  76.7 1.8 %back_conv.1 = bf16[128,1024]{1,0:T(8,128)(2,1)} custom-call(bf16[128,1024]{1,0:T(8,128)(2,1)S(1)} %get-tuple-element.43.grad, bf16[128,1024]{1,0:T(8,128)(2,1)S(1)} %collective-permute-done.17.up, bf16[128,1024]{1,0:T(8,128)(2,1)S(1)} %collective-permute-done.18.down, f32[27,1024]{1,0:T(8,128)S(1)} %copy-done.5), custom_call_target="tpu_custom_call" | custom-call | bytes 1159168 | tf_op jit(solution)/shard_map/back_conv/pallas_call | solution.py:567
  (45 shorter events, 5.7 us)
Async XLA Ops:
  0.6 15.1 %copy-start = (bf16[512,1536]{1,0:T(8,128)(2,1)S(1)}, bf16[512,1536]{1,0:T(8,128)(2,1)}, u32[]{:S(2)}) copy-start(bf16[512,1536]{1,0:T(8,128)(2,1)} %refs_8_.1) | copy-start | bytes 4718596
  0.6 15.0 %collective-permute-start.4 = (bf16[512,1536]{1,0:T(8,128)(2,1)}, bf16[512,1536]{1,0:T(8,128)(2,1)S(1)}, u32[]{:S(2)}, u32[]{:S(2)}) collective-permute-start(bf16[512,1536]{1,0:T(8,128)(2,1)} %refs_8_.1), channel_id=1, source_target_pairs={{0,1},{1,0},{2,3},{3,2},{4,5},{5,4},{6,7},{7,6},{8,9},{9,8},{10,11... | collective-permute-start | bytes 4718600 | tf_op jit(solution)/shard_map/ppermute | solution.py:581
  1.2 9.3 %collective-permute-start.2 = (bf16[128,3072]{1,0:T(8,128)(2,1)}, bf16[128,3072]{1,0:T(8,128)(2,1)}, u32[]{:S(2)}, u32[]{:S(2)}) collective-permute-start(bf16[128,3072]{1,0:T(8,128)(2,1)} %wt_own.1), channel_id=1, source_target_pairs={{0,1},{1,0},{2,3},{3,2},{4,5},{5,4},{6,7},{7,6},{8,9},{9,8},{10,11... | collective-permute-start | bytes 2359304 | tf_op jit(solution)/shard_map/ppermute | solution.py:581
  1.2 9.2 %collective-permute-start.3 = (bf16[256,1024]{1,0:T(8,128)(2,1)}, bf16[256,1024]{1,0:T(8,128)(2,1)}, u32[]{:S(2)}, u32[]{:S(2)}) collective-permute-start(bf16[256,1024]{1,0:T(8,128)(2,1)} %refs_6_.1), channel_id=1, source_target_pairs={{0,1},{1,0},{2,3},{3,2},{4,5},{5,4},{6,7},{7,6},{8,9},{9,8},{10,11... | collective-permute-start | bytes 1572872 | tf_op jit(solution)/shard_map/ppermute | solution.py:581
  1.7 14.0 %collective-permute-start.1 = (bf16[128,1024]{1,0:T(8,128)(2,1)}, bf16[128,1024]{1,0:T(8,128)(2,1)S(1)}, u32[]{:S(2)}, u32[]{:S(2)}) collective-permute-start(bf16[128,1024]{1,0:T(8,128)(2,1)} %bitcast.18), channel_id=1, source_target_pairs={{4,0},{8,4},{12,8},{5,1},{9,5},{13,9},{6,2},{10,6},{14,10},{7,3},{... | collective-permute-start | bytes 786440 | tf_op jit(solution)/shard_map/ppermute | solution.py:592
  3.0 12.7 %collective-permute-start = (bf16[128,1024]{1,0:T(8,128)(2,1)}, bf16[128,1024]{1,0:T(8,128)(2,1)}, u32[]{:S(2)}, u32[]{:S(2)}) collective-permute-start(bf16[128,1024]{1,0:T(8,128)(2,1)} %bitcast.19), channel_id=1, source_target_pairs={{0,4},{4,8},{8,12},{1,5},{5,9},{9,13},{2,6},{6,10},{10,14},{3,7},{... | collective-permute-start | bytes 786440 | tf_op jit(solution)/shard_map/ppermute | solution.py:592
  10.4 1.0 %copy-start.1 = (bf16[256,1024]{1,0:T(8,128)(2,1)S(1)}, bf16[256,1024]{1,0:T(8,128)(2,1)}, u32[]{:S(2)}) copy-start(bf16[256,1024]{1,0:T(8,128)(2,1)} %refs_6_.1) | copy-start | bytes 1572868
  11.5 0.9 %copy-start.3 = (bf16[1,1,8,16,1024]{4,3,2,1,0:T(8,128)(2,1)S(1)}, bf16[1,1,8,16,1024]{4,3,2,1,0:T(8,128)(2,1)}, u32[]{:S(2)}) copy-start(bf16[1,1,8,16,1024]{4,3,2,1,0:T(8,128)(2,1)} %param.15) | copy-start | bytes 786436
  12.4 1.1 %copy-start.4 = (bf16[128,3072]{1,0:T(8,128)(2,1)S(1)}, bf16[128,3072]{1,0:T(8,128)(2,1)}, u32[]{:S(2)}) copy-start(bf16[128,3072]{1,0:T(8,128)(2,1)} %wt_own.1) | copy-start | bytes 2359300
  13.6 2.1 %copy-start.2 = (bf16[1,1,8,16,1024]{4,3,2,1,0:T(8,128)(2,1)S(1)}, bf16[1,1,8,16,1024]{4,3,2,1,0:T(8,128)(2,1)}, u32[]{:S(2)}) copy-start(bf16[1,1,8,16,1024]{4,3,2,1,0:T(8,128)(2,1)} %param.8) | copy-start | bytes 786436
  13.6 2.2 %copy-start.5 = (f32[27,1024]{1,0:T(8,128)S(1)}, f32[27,1024]{1,0:T(8,128)}, u32[]{:S(2)}) copy-start(f32[27,1024]{1,0:T(8,128)} %taps.3) | copy-start | bytes 331780
  18.8 15.4 %collective-permute-start.5 = (bf16[128,384]{1,0:T(8,128)(2,1)S(1)}, bf16[128,384]{1,0:T(8,128)(2,1)S(1)}, u32[]{:S(2)}, u32[]{:S(2)}) collective-permute-start(bf16[128,384]{1,0:T(8,128)(2,1)S(1)} %get-tuple-element.26), channel_id=1, source_target_pairs={{0,4},{4,0},{8,12},{12,8},{1,5},{5,1},{9,13},{13,9},{2,6},{6,2},{1... | collective-permute-start | bytes 294920 | tf_op jit(solution)/shard_map/ppermute | solution.py:581
  20.3 13.9 %collective-permute-start.6 = (bf16[128,384]{1,0:T(8,128)(2,1)S(1)}, bf16[128,384]{1,0:T(8,128)(2,1)S(1)}, u32[]{:S(2)}, u32[]{:S(2)}) collective-permute-start(bf16[128,384]{1,0:T(8,128)(2,1)S(1)} %get-tuple-element.27), channel_id=1, source_target_pairs={{0,8},{4,12},{8,0},{12,4},{1,9},{5,13},{9,1},{13,5},{2,10},{6,14},... | collective-permute-start | bytes 294920 | tf_op jit(solution)/shard_map/ppermute | solution.py:581
  23.0 11.2 %collective-permute-start.7 = (bf16[128,384]{1,0:T(8,128)(2,1)S(1)}, bf16[128,384]{1,0:T(8,128)(2,1)S(1)}, u32[]{:S(2)}, u32[]{:S(2)}) collective-permute-start(bf16[128,384]{1,0:T(8,128)(2,1)S(1)} %get-tuple-element.28), channel_id=1, source_target_pairs={{0,12},{4,8},{8,4},{12,0},{1,13},{5,9},{9,5},{13,1},{2,14},{6,10},... | collective-permute-start | bytes 294920 | tf_op jit(solution)/shard_map/ppermute | solution.py:581
  23.3 4.4 %collective-permute-start.8 = (bf16[128,128]{1,0:T(8,128)(2,1)S(1)}, bf16[128,128]{1,0:T(8,128)(2,1)S(1)}, u32[]{:S(2)}, u32[]{:S(2)}) collective-permute-start(bf16[128,128]{1,0:T(8,128)(2,1)S(1)} %get-tuple-element.30), channel_id=1, source_target_pairs={{0,4},{4,0},{8,12},{12,8},{1,5},{5,1},{9,13},{13,9},{2,6},{6,2},{1... | collective-permute-start | bytes 98312 | tf_op jit(solution)/shard_map/ppermute | solution.py:581
  23.8 10.4 %collective-permute-start.9 = (bf16[128,128]{1,0:T(8,128)(2,1)S(1)}, bf16[128,128]{1,0:T(8,128)(2,1)S(1)}, u32[]{:S(2)}, u32[]{:S(2)}) collective-permute-start(bf16[128,128]{1,0:T(8,128)(2,1)S(1)} %get-tuple-element.31), channel_id=1, source_target_pairs={{0,8},{4,12},{8,0},{12,4},{1,9},{5,13},{9,1},{13,5},{2,10},{6,14},... | collective-permute-start | bytes 98312 | tf_op jit(solution)/shard_map/ppermute | solution.py:581
  27.7 6.5 %collective-permute-start.10 = (bf16[128,128]{1,0:T(8,128)(2,1)S(1)}, bf16[128,128]{1,0:T(8,128)(2,1)S(1)}, u32[]{:S(2)}, u32[]{:S(2)}) collective-permute-start(bf16[128,128]{1,0:T(8,128)(2,1)S(1)} %get-tuple-element.32), channel_id=1, source_target_pairs={{0,12},{4,8},{8,4},{12,0},{1,13},{5,9},{9,5},{13,1},{2,14},{6,10},... | collective-permute-start | bytes 98312 | tf_op jit(solution)/shard_map/ppermute | solution.py:581
  38.6 5.0 %collective-permute-start.14 = (bf16[128,384]{1,0:T(8,128)(2,1)S(1)}, bf16[128,384]{1,0:T(8,128)(2,1)S(1)}, u32[]{:S(2)}, u32[]{:S(2)}) collective-permute-start(bf16[128,384]{1,0:T(8,128)(2,1)S(1)} %get-tuple-element.39), channel_id=1, source_target_pairs={{0,4},{4,0},{8,12},{12,8},{1,5},{5,1},{9,13},{13,9},{2,6},{6,2},{1... | collective-permute-start | bytes 294920 | tf_op jit(solution)/shard_map/ppermute | solution.py:581
  39.6 8.2 %collective-permute-start.15 = (bf16[128,384]{1,0:T(8,128)(2,1)S(1)}, bf16[128,384]{1,0:T(8,128)(2,1)S(1)}, u32[]{:S(2)}, u32[]{:S(2)}) collective-permute-start(bf16[128,384]{1,0:T(8,128)(2,1)S(1)} %get-tuple-element.40), channel_id=1, source_target_pairs={{0,8},{4,12},{8,0},{12,4},{1,9},{5,13},{9,1},{13,5},{2,10},{6,14},... | collective-permute-start | bytes 294920 | tf_op jit(solution)/shard_map/ppermute | solution.py:581
  42.7 6.5 %collective-permute-start.16 = (bf16[128,384]{1,0:T(8,128)(2,1)S(1)}, bf16[128,384]{1,0:T(8,128)(2,1)S(1)}, u32[]{:S(2)}, u32[]{:S(2)}) collective-permute-start(bf16[128,384]{1,0:T(8,128)(2,1)S(1)} %get-tuple-element.41), channel_id=1, source_target_pairs={{0,12},{4,8},{8,4},{12,0},{1,13},{5,9},{9,5},{13,1},{2,14},{6,10},... | collective-permute-start | bytes 294920 | tf_op jit(solution)/shard_map/ppermute | solution.py:581
  53.2 23.5 %collective-permute-start.18 = (bf16[128,1024]{1,0:T(8,128)(2,1)S(1)}, bf16[128,1024]{1,0:T(8,128)(2,1)S(1)}, u32[]{:S(2)}, u32[]{:S(2)}) collective-permute-start(bf16[128,1024]{1,0:T(8,128)(2,1)S(1)} %get-tuple-element.43.grad), channel_id=1, source_target_pairs={{4,0},{8,4},{12,8},{5,1},{9,5},{13,9},{6,2},{10,6},{14,10},{7,3},{... | collective-permute-start | bytes 786440 | tf_op jit(solution)/shard_map/ppermute | solution.py:592
  54.5 22.2 %collective-permute-start.17 = (bf16[128,1024]{1,0:T(8,128)(2,1)S(1)}, bf16[128,1024]{1,0:T(8,128)(2,1)S(1)}, u32[]{:S(2)}, u32[]{:S(2)}) collective-permute-start(bf16[128,1024]{1,0:T(8,128)(2,1)S(1)} %get-tuple-element.43.grad), channel_id=1, source_target_pairs={{0,4},{4,8},{8,12},{1,5},{5,9},{9,13},{2,6},{6,10},{10,14},{3,7},{... | collective-permute-start | bytes 786440 | tf_op jit(solution)/shard_map/ppermute | solution.py:592
  59.1 1.4 %collective-permute-start.19 = (f32[27,1024]{1,0:T(8,128)S(1)}, f32[27,1024]{1,0:T(8,128)S(1)}, u32[]{:S(2)}, u32[]{:S(2)}) collective-permute-start(f32[27,1024]{1,0:T(8,128)S(1)} %get-tuple-element.44.left), channel_id=1, source_target_pairs={{0,1},{1,0},{2,3},{3,2},{4,5},{5,4},{6,7},{7,6},{8,9},{9,8},{10,11... | collective-permute-start | bytes 331784 | tf_op jit(solution)/shard_map/ppermute | solution.py:581
  60.6 4.3 %collective-permute-start.20 = (bf16[27,1024]{1,0:T(8,128)(2,1)S(1)}, bf16[27,1024]{1,0:T(8,128)(2,1)S(1)}, u32[]{:S(2)}, u32[]{:S(2)}) collective-permute-start(bf16[27,1024]{1,0:T(8,128)(2,1)S(1)} %add_fsdp.1.left), channel_id=1, source_target_pairs={{0,2},{2,0},{1,3},{3,1},{4,6},{6,4},{5,7},{7,5},{8,10},{10,8},{9,1... | collective-permute-start | bytes 165896 | tf_op jit(solution)/shard_map/ppermute | solution.py:581
  62.0 4.4 %collective-permute-start.11 = (bf16[128,128]{1,0:T(8,128)(2,1)S(1)}, bf16[128,128]{1,0:T(8,128)(2,1)S(1)}, u32[]{:S(2)}, u32[]{:S(2)}) collective-permute-start(bf16[128,128]{1,0:T(8,128)(2,1)S(1)} %get-tuple-element.34), channel_id=1, source_target_pairs={{0,4},{4,0},{8,12},{12,8},{1,5},{5,1},{9,13},{13,9},{2,6},{6,2},{1... | collective-permute-start | bytes 98312 | tf_op jit(solution)/shard_map/ppermute | solution.py:581
  63.3 5.9 %collective-permute-start.12 = (bf16[128,128]{1,0:T(8,128)(2,1)S(1)}, bf16[128,128]{1,0:T(8,128)(2,1)S(1)}, u32[]{:S(2)}, u32[]{:S(2)}) collective-permute-start(bf16[128,128]{1,0:T(8,128)(2,1)S(1)} %get-tuple-element.35), channel_id=1, source_target_pairs={{0,8},{4,12},{8,0},{12,4},{1,9},{5,13},{9,1},{13,5},{2,10},{6,14},... | collective-permute-start | bytes 98312 | tf_op jit(solution)/shard_map/ppermute | solution.py:581
  64.9 6.2 %collective-permute-start.13 = (bf16[128,128]{1,0:T(8,128)(2,1)S(1)}, bf16[128,128]{1,0:T(8,128)(2,1)S(1)}, u32[]{:S(2)}, u32[]{:S(2)}) collective-permute-start(bf16[128,128]{1,0:T(8,128)(2,1)S(1)} %get-tuple-element.36), channel_id=1, source_target_pairs={{0,12},{4,8},{8,4},{12,0},{1,13},{5,9},{9,5},{13,1},{2,14},{6,10},... | collective-permute-start | bytes 98312 | tf_op jit(solution)/shard_map/ppermute | solution.py:581
  66.4 8.1 %collective-permute-start.23 = (bf16[27,1024]{1,0:T(8,128)(2,1)S(1)}, bf16[27,1024]{1,0:T(8,128)(2,1)S(1)}, u32[]{:S(2)}, u32[]{:S(2)}) collective-permute-start(bf16[27,1024]{1,0:T(8,128)(2,1)S(1)} %add_dp.1.refs_0_), channel_id=1, source_target_pairs={{0,12},{4,8},{8,4},{12,0},{1,13},{5,9},{9,5},{13,1},{2,14},{6,10},... | collective-permute-start | bytes 165896 | tf_op jit(solution)/shard_map/ppermute | solution.py:581
  69.1 6.3 %collective-permute-start.22 = (bf16[27,1024]{1,0:T(8,128)(2,1)S(1)}, bf16[27,1024]{1,0:T(8,128)(2,1)S(1)}, u32[]{:S(2)}, u32[]{:S(2)}) collective-permute-start(bf16[27,1024]{1,0:T(8,128)(2,1)S(1)} %add_dp.1.refs_0_), channel_id=1, source_target_pairs={{0,8},{4,12},{8,0},{12,4},{1,9},{5,13},{9,1},{13,5},{2,10},{6,14},... | collective-permute-start | bytes 165896 | tf_op jit(solution)/shard_map/ppermute | solution.py:581
  71.0 5.0 %collective-permute-start.21 = (bf16[27,1024]{1,0:T(8,128)(2,1)S(1)}, bf16[27,1024]{1,0:T(8,128)(2,1)S(1)}, u32[]{:S(2)}, u32[]{:S(2)}) collective-permute-start(bf16[27,1024]{1,0:T(8,128)(2,1)S(1)} %add_dp.1.refs_0_), channel_id=1, source_target_pairs={{0,4},{4,0},{8,12},{12,8},{1,5},{5,1},{9,13},{13,9},{2,6},{6,2},{1... | collective-permute-start | bytes 165896 | tf_op jit(solution)/shard_map/ppermute | solution.py:581

commit v2 on v1

--- a/solution.py
+++ b/solution.py
@@ -286,16 +286,20 @@
     return jnp.concatenate([value[inner:], empty], axis=0)
 
 
-def conv_lanes(planes, taps, flipped, inner):
+def sided_taps(taps, odd):
+    before, after = taps[0:9], taps[18:27]
+    return jnp.where(odd, before, after), taps[9:18], jnp.where(odd, after, before)
+
+
+def conv_lanes(planes, taps, inner):
     by_x = []
     for tap_x in range(3):
         total = None
         for tap_y in range(3):
             part = None
             for tap_z in range(3):
-                index = 9 * tap_z + 3 * tap_y + tap_x
-                index = 26 - index if flipped else index
-                term = taps[index : index + 1] * planes[tap_z]
+                index = 3 * tap_y + tap_x
+                term = taps[tap_z][index : index + 1] * planes[tap_z]
                 part = term if part is None else part + term
             part = slab_shift(part, 1 - tap_y, inner)
             total = part if total is None else total + part
@@ -331,13 +335,27 @@
     return jnp.dot(left, right, preferred_element_type=jnp.float32)
 
 
-def front_body(slots, ids, feats, pxrd, wt_own, wt_oth, cot, wo_own, wo_oth, *rest):
-    mod, sends, by_group = rest[0], rest[1 : 1 + slots], rest[1 + slots]
+def front_body(slots, ids, feats, *rest):
+    fetched = rest[:6]
+    mod, sends, by_group = rest[6], rest[7 : 7 + slots], rest[7 + slots]
+    wt_own, wt_oth, pxrd, wo_own, wo_oth, cot = held = rest[8 + slots : 14 + slots]
+    arrive = rest[14 + slots]
     me, half = ids[0], ids[1]
-    width = pxrd.shape[1]
+    width = cot.shape[1]
+    copies = [
+        pltpu.make_async_copy(source, place, arrive.at[i])
+        for i, (source, place) in enumerate(zip(fetched, held))
+    ]
+    for copy in copies:
+        copy.start()
+    for copy in copies[:3]:
+        copy.wait()
     projected = nn_dot(feats[0], wt_own[...]) + nn_dot(feats[1], wt_oth[...])
     for row in range(3):
-        mod[row : row + 1, :] = projected[0:1, row * width : (row + 1) * width] + pxrd[row : row + 1, :]
+        cols = slice(row * width, (row + 1) * width)
+        mod[row : row + 1, :] = projected[0:1, cols] + pxrd[row : row + 1, :]
+    for copy in copies[3:]:
+        copy.wait()
     gated = (mod[2:3, :] * as_f32(cot[...])).astype(jnp.bfloat16)
     lanes = sends[0].shape[1]
     per_half = wo_own.shape[0] // lanes
@@ -345,22 +363,23 @@
         grads = nt_dot(gated, weight[...]).astype(jnp.bfloat16)
         for j in range(per_half):
             by_group[part * per_half + j] = grads[:, j * lanes : (j + 1) * lanes]
-    for k in range(slots):
-        sends[k][...] = by_group[lax.bitwise_xor(me, k)]
-
-
-def mix_body(slots, inner, ids, tok, up, down, taps, mod, w_own, w_oth, *rest):
+    for k, gap in enumerate(distances(slots)):
+        sends[k][...] = by_group[lax.bitwise_xor(me, gap)]
+
+
+def mix_body(slots, inner, ids, tok, near, far, taps, mod, w_own, w_oth, *rest):
     resid, sections = rest[0], rest[1]
     sends = rest[2 : 2 + slots]
     normed, by_group = rest[2 + slots :]
     me, half = ids[0], ids[1]
+    odd = lax.rem(me, 2) == 1
     rows, width = tok.shape
     step = 128
     sums = jnp.zeros((rows, step), jnp.float32)
     for start in range(0, width, step):
         cols = slice(start, start + step)
-        planes = [as_f32(ref[:, cols]) for ref in (up, tok, down)]
-        mixed = conv_lanes(planes, taps[:, cols], False, inner)
+        planes = [as_f32(ref[:, cols]) for ref in (near, tok, far)]
+        mixed = conv_lanes(planes, sided_taps(taps[:, cols], odd), inner)
         rounded = (planes[1] + mixed).astype(jnp.bfloat16)
         resid[:, cols] = rounded
         sums = sums + as_f32(rounded)
@@ -388,14 +407,14 @@
             if part < 2:
                 block = block * lax.rsqrt(head_mean(block * block) + 1e-06)
             by_group[group, :, part * lanes : (part + 1) * lanes] = block.astype(jnp.bfloat16)
-    for k in range(slots):
-        sends[k][...] = by_group[lax.bitwise_xor(me, k)]
+    for k, gap in enumerate(distances(slots)):
+        sends[k][...] = by_group[lax.bitwise_xor(me, gap)]
 
 
 def attend_body(slots, *refs):
     qkv_in, grads_in = refs[:slots], refs[slots : 2 * slots]
-    backs, attns = refs[2 * slots : 3 * slots], refs[3 * slots : 4 * slots]
-    keys, values, probs_all, dscore_all = refs[4 * slots :]
+    backs = refs[2 * slots : 3 * slots]
+    keys, values, probs_all, dscore_all = refs[3 * slots :]
     rows, lanes = grads_in[0].shape
     heads = lanes // HD
     scale = 1.0 / math.sqrt(HD)
@@ -419,7 +438,7 @@
             attn_total = attn if attn_total is None else attn_total + attn
             pieces.append(weights)
         attn_total = attn_total.astype(jnp.bfloat16)
-        attns[k][...] = attn_total
+        backs[k][:, 3 * lanes :] = attn_total
         product = as_f32(attn_total) * as_f32(grad)
         dquery = None
         for head in range(heads):
@@ -444,20 +463,21 @@
         dvalues = dvalue if dvalues is None else dvalues + dvalue
     for k in range(slots):
         backs[k][:, lanes : 2 * lanes] = dkeys[k * rows : (k + 1) * rows].astype(jnp.bfloat16)
-        backs[k][:, 2 * lanes :] = dvalues[k * rows : (k + 1) * rows].astype(jnp.bfloat16)
+        backs[k][:, 2 * lanes : 3 * lanes] = dvalues[k * rows : (k + 1) * rows].astype(jnp.bfloat16)
 
 
 def tail_body(slots, inner, ids, *refs):
     backs = refs[:slots]
-    sections, resid, cot, mod, w_own, w_oth, tok, up, down = refs[slots : slots + 9]
+    sections, resid, cot, mod, w_own, w_oth, tok, near, far = refs[slots : slots + 9]
     dresid, terms = refs[slots + 9 : slots + 11]
-    by_group, dproj, dnormed, sums = refs[slots + 11 :]
+    by_group, dproj, dnormed = refs[slots + 11 :]
     me, half = ids[0], ids[1]
+    odd = lax.rem(me, 2) == 1
     rows, width = resid.shape
     lanes = by_group.shape[3]
     inner_width = H * HD
-    for k in range(slots):
-        group = lax.bitwise_xor(me, k)
+    for k, gap in enumerate(distances(slots)):
+        group = lax.bitwise_xor(me, gap)
         for part in range(3):
             by_group[group, part] = backs[k][:, part * lanes : (part + 1) * lanes]
     for group in range(slots):
@@ -506,28 +526,35 @@
         cols = slice(start, start + step)
         grad = as_f32(dresid[:, cols])
         moved = [row_shift(grad, -1, inner), grad, row_shift(grad, 1, inner)]
-        for tap_z, ref in enumerate((up, tok, down)):
+        found = []
+        for ref in (near, tok, far):
             plane = as_f32(ref[:, cols])
+            lines = []
             for tap_y in range(3):
                 low, high = max(0, 1 - tap_y), max(0, tap_y - 1)
                 for tap_x in range(3):
-                    index = 9 * tap_z + 3 * tap_y + tap_x
                     prod = (
                         plane[high * inner : rows - low * inner]
                         * moved[tap_x][low * inner : rows - high * inner]
                     )
                     prod = jnp.sum(prod.reshape(-1, 8, step), axis=0)
-                    terms[index : index + 1, cols] = jnp.sum(prod, axis=0, keepdims=True)
+                    lines.append(jnp.sum(prod, axis=0, keepdims=True))
+            found.append(lines)
+        for i in range(9):
+            by_near, by_far = found[0][i], found[2][i]
+            terms[i : i + 1, cols] = jnp.where(odd, by_near, by_far)
+            terms[9 + i : 10 + i, cols] = found[1][i]
+            terms[18 + i : 19 + i, cols] = jnp.where(odd, by_far, by_near)
 
 
 def out_body(slots, ids, *refs):
-    attns = refs[:slots]
+    backs = refs[:slots]
     resid, mod, wo_own, wo_oth, out, by_group = refs[slots:]
     me, half = ids[0], ids[1]
-    lanes = attns[0].shape[1]
+    lanes = backs[0].shape[1] // 4
     per_half = wo_own.shape[0] // lanes
-    for k in range(slots):
-        by_group[lax.bitwise_xor(me, k)] = attns[k][...]
+    for k, gap in enumerate(distances(slots)):
+        by_group[lax.bitwise_xor(me, gap)] = backs[k][:, 3 * lanes :]
     total = None
     for weight, part in ((wo_own, half), (wo_oth, 1 - half)):
         for j in range(per_half):
@@ -536,41 +563,51 @@
     out[...] = (as_f32(resid[...]) + mod[2:3, :] * total).astype(jnp.bfloat16)
 
 
-def back_conv_body(inner, grad, up, down, taps, out):
+def back_conv_body(inner, ids, grad, near, far, taps, out):
+    odd = lax.rem(ids[0], 2) == 1
     width = grad.shape[1]
     step = 128
     for start in range(0, width, step):
         cols = slice(start, start + step)
-        planes = [as_f32(ref[:, cols]) for ref in (up, grad, down)]
-        mixed = conv_lanes(planes, taps[:, cols], True, inner)
+        planes = [as_f32(ref[:, cols]) for ref in (near, grad, far)]
+        lines = taps[:, cols]
+        turned = [jnp.concatenate([lines[r : r + 1] for r in range(26, -1, -1)], axis=0)]
+        mixed = conv_lanes(planes, sided_taps(turned[0], odd), inner)
         out[:, cols] = (planes[1] + mixed).astype(jnp.bfloat16)
 
 
-def pair_body(last, left, right, out):
+def pair_body(left, right, out):
     total = as_f32(left[...]) + as_f32(right[...])
     out[...] = total.astype(out.dtype)
 
 
 def final_body(factor, slots, *refs):
-    values = [as_f32(ref[...]) for ref in refs[:slots]]
+    gaps = distances(slots)
+    values = [as_f32(refs[gaps.index(gap)][...]) for gap in range(slots)]
     while len(values) > 1:
         values = [values[i] + values[i + 1] for i in range(0, len(values), 2)]
     refs[slots][...] = values[0] * factor
 
 
-def call(body, name, outs, args, scratch=(), flops=0, scalars=False):
+def call(body, name, outs, args, scratch=(), flops=0, scalars=False, far_args=(), vmem=16):
     whole = pl.BlockSpec(memory_space=pltpu.VMEM)
     specs = [whole] * len(args)
     if scalars:
         specs[0] = pl.BlockSpec(memory_space=pltpu.SMEM)
+    for i in far_args:
+        specs[i] = pl.BlockSpec(memory_space=pltpu.HBM)
     sizes = [math.prod(a.shape) * a.dtype.itemsize for a in list(args) + list(outs)]
+    args = [
+        pltpu.with_memory_space_constraint(a, pltpu.HBM) if i in far_args else a
+        for i, a in enumerate(args)
+    ]
     return pl.pallas_call(
         body,
         out_shape=tuple(outs),
         in_specs=specs,
         out_specs=(whole,) * len(outs),
         scratch_shapes=list(scratch),
-        compiler_params=pltpu.CompilerParams(vmem_limit_bytes=40 * 2**20),
+        compiler_params=pltpu.CompilerParams(vmem_limit_bytes=vmem * 2**20),
         cost_estimate=pl.CostEstimate(flops=flops, bytes_accessed=sum(sizes), transcendentals=0),
         name=name,
     )(*args)
@@ -581,15 +618,22 @@
     return lax.ppermute(value, axis, [(i, i ^ distance) for i in range(count)])
 
 
+def distances(slots):
+    return (0, 2, 3, 1) if slots == 4 else (0, 1)
+
+
 def exchanged(pieces):
-    return [pieces[0]] + [swapped(pieces[k], "seq", k) for k in range(1, len(pieces))]
+    pairs = list(zip(pieces, distances(len(pieces))))
+    return [pieces[0]] + [swapped(piece, "seq", k) for piece, k in pairs[1:]]
 
 
 def neighbours(value):
     count = lax.axis_size("seq")
-    up = [(i, i + 1) for i in range(count - 1)]
-    down = [(i + 1, i) for i in range(count - 1)]
-    return lax.ppermute(value, "seq", up), lax.ppermute(value, "seq", down)
+    near = swapped(value, "seq", 1)
+    if count == 2:
+        return near, jnp.zeros_like(value)
+    middle = [(i, i + 1) for i in range(1, count - 1, 2)]
+    return near, lax.ppermute(value, "seq", middle + [(j, i) for i, j in middle])
 
 
 def slab_shards(
@@ -609,7 +653,7 @@
 
     wo_oth = swapped(out_weight, "fsdp", 1)
     wt_oth = swapped(time_weight, "fsdp", 1)
-    up, down = neighbours(tok)
+    near, far = neighbours(tok)
     wq_oth = swapped(qkv_weight, "fsdp", 1)
 
     freq = 2 * time_weight.shape[0]
@@ -621,8 +665,13 @@
         functools.partial(front_body, slots),
         "front",
         [shape((3, width), f32)] + [shape((rows, lanes), bf16)] * slots,
-        (ids, feats, pxrd_mod[0], time_weight, wt_oth, cot, out_weight, wo_oth),
-        [pltpu.VMEM((slots, rows, lanes), bf16)],
+        (ids, feats, time_weight, wt_oth, pxrd_mod[0], out_weight, wo_oth, cot),
+        [pltpu.VMEM((slots, rows, lanes), bf16)]
+        + [pltpu.VMEM(time_weight.shape, bf16)] * 2
+        + [pltpu.VMEM(pxrd_mod.shape[1:], f32)]
+        + [pltpu.VMEM(out_weight.shape, bf16)] * 2
+        + [pltpu.VMEM((rows, width), bf16), pltpu.SemaphoreType.DMA((6,))],
+        far_args=range(2, 8),
         flops=2 * rows * width * H * HD,
         scalars=True,
     )
@@ -634,35 +683,34 @@
         "mix",
         [shape((rows, width), bf16), shape((rows, 2 * H * HD), f32)]
         + [shape((rows, 3 * lanes), bf16)] * slots,
-        (ids, tok, up, down, conv_kernel, mod, qkv_weight, wq_oth),
+        (ids, tok, near, far, conv_kernel, mod, qkv_weight, wq_oth),
         [pltpu.VMEM((2, rows, width // 2), bf16), pltpu.VMEM((slots, rows, 3 * lanes), bf16)],
         flops=2 * rows * width * 3 * H * HD,
         scalars=True,
     )
     resid, sections = mixed[:2]
-    qkv_in = exchanged(mixed[2:])
+    sends, grads_in = lax.optimization_barrier((mixed[2:], grads_in))
+    qkv_in = exchanged(sends)
     count = slots * rows
     attended = call(
         functools.partial(attend_body, slots),
         "attend",
-        [shape((rows, 3 * lanes), bf16)] * slots + [shape((rows, lanes), bf16)] * slots,
+        [shape((rows, 4 * lanes), bf16)] * slots,
         (*qkv_in, *grads_in),
         [pltpu.VMEM((count, lanes), bf16)] * 2
         + [pltpu.VMEM((lanes // HD, count, count), bf16)] * 2,
         flops=12 * count * count * lanes,
     )
-    backs = exchanged(attended[:slots])
-    attns = exchanged(attended[slots:])
+    backs = exchanged(attended)
     dresid, terms = call(
         functools.partial(tail_body, slots, inner),
         "tail",
         [shape((rows, width), bf16), shape((27, width), f32)],
-        (ids, *backs, sections, resid, cot, mod, qkv_weight, wq_oth, tok, up, down),
+        (ids, *backs, sections, resid, cot, mod, qkv_weight, wq_oth, tok, near, far),
         [
             pltpu.VMEM((slots, 3, rows, lanes), bf16),
             pltpu.VMEM((rows, 3 * H * HD), bf16),
             pltpu.VMEM((2, rows, width // 2), f32),
-            pltpu.VMEM((8, width), f32),
         ],
         flops=2 * rows * width * 3 * H * HD,
         scalars=True,
@@ -671,36 +719,30 @@
         functools.partial(out_body, slots),
         "out",
         [shape((rows, width), bf16)],
-        (ids, *attns, resid, mod, out_weight, wo_oth),
+        (ids, *backs, resid, mod, out_weight, wo_oth),
         [pltpu.VMEM((slots, rows, lanes), bf16)],
         flops=2 * rows * width * H * HD,
         scalars=True,
     )
-    (terms,) = call(
-        functools.partial(pair_body, False),
-        "add_fsdp",
-        [shape((27, width), bf16)],
-        (terms, swapped(terms, "fsdp", 1)),
-    )
-    (terms,) = call(
-        functools.partial(pair_body, False),
-        "add_dp",
-        [shape((27, width), bf16)],
-        (terms, swapped(terms, "dp", 1)),
-    )
-    factor = 1.0 / math.sqrt(lax.axis_size("dp") * lax.axis_size("fsdp") * slots * rows)
-    (kernel_grad,) = call(
-        functools.partial(final_body, factor, slots),
-        "add_seq",
-        [shape((27, width), f32)],
-        exchanged([terms] * slots),
-    )
-    grad_up, grad_down = neighbours(dresid)
+    shape_terms = [shape((27, width), bf16)]
+    other = swapped(terms, "fsdp", 1)
+    grad_near, grad_far = neighbours(dresid)
+    (terms,) = call(pair_body, "add_fsdp", shape_terms, (terms, other))
+    other = swapped(terms, "dp", 1)
+    other, out = lax.optimization_barrier((other, out))
+    (terms,) = call(pair_body, "add_dp", shape_terms, (terms, other))
     (token_grad,) = call(
         functools.partial(back_conv_body, inner),
         "back_conv",
         [shape((rows, width), bf16)],
-        (dresid, grad_up, grad_down, conv_kernel),
+        (ids, dresid, grad_near, grad_far, conv_kernel),
+        scalars=True,
+    )
+    factor = 1.0 / math.sqrt(lax.axis_size("dp") * lax.axis_size("fsdp") * slots * rows)
+    pieces = exchanged([terms] * slots)
+    pieces[-1], token_grad = lax.optimization_barrier((pieces[-1], token_grad))
+    (kernel_grad,) = call(
+        functools.partial(final_body, factor, slots), "add_seq", [shape((27, width), f32)], pieces
     )
     return out.reshape(tokens.shape), token_grad.reshape(tokens.shape), kernel_grad
 

time: 79 us -> 70.8 us (0.90)
  starting transfers between devices: 40.5 us -> 28.2 us
  waiting for transfers between devices: 14.2 us -> 19.5 us
  local copies, waits for them, and re-layouts: 3.86 us -> 1.36 us
  Pallas kernels: 18.3 us -> 19.8 us
    ppermute x4 -> x2, starting transfers between devices: 13 us -> 2.06 us  [neighbours(): lax.ppermute(value, 'seq', middle + [(j, i) for i, j in middle])]
    ppermute x20 -> x19, waiting for transfers between devices: 14.2 us -> 19.5 us  [swapped(): return lax.ppermute(value, axis, [(i, i ^ distance) for i in range(count)])]
    unnamed x14 -> x12, local copies, waits for them, and re-layouts: 3.85 us -> 1.34 us
    pallas_call x9, Pallas kernels: 18.3 us -> 19.8 us  [call(): pl.pallas_call(body, out_shape=tuple(outs), in_specs=specs, out_specs=(wh...]
    ppermute x20 -> x19, starting transfers between devices: 27.5 us -> 26.1 us  [swapped(): return lax.ppermute(value, axis, [(i, i ^ distance) for i in range(count)])]
  transfers between devices with their start and end apart: 24 -> 21, of which waited for: 11 -> 8; matrix products, arithmetic and copies ran while one was open for 1% -> 2% of each run, Pallas kernels for 6% -> 15%
where the time goes in v2:
time: 70.8 us; the launch traced here: 70.5 us
  starting transfers between devices  28.2 us (40%)
  Pallas kernels  19.8 us (28%)
  waiting for transfers between devices  19.5 us (28%)
  between operations  1.46 us (2%)
  local copies, waits for them, and re-layouts  1.36 us (2%)
    ppermute x19, starting transfers between devices, swapped(): return lax.ppermute(value, axis, [(i, i ^ distance) for i in range(count)])  26.1 us
    pallas_call x9, Pallas kernels, call(): pl.pallas_call(body, out_shape=tuple(outs), in_specs=specs, out_specs=(wh...  19.8 us
    ppermute x19, waiting for transfers between devices, swapped(): return lax.ppermute(value, axis, [(i, i ^ distance) for i in range(count)])  19.5 us
    ppermute x2, starting transfers between devices, neighbours(): lax.ppermute(value, 'seq', middle + [(j, i) for i, j in middle])  2.06 us
  transfers between devices with their start and end apart: 21, of which 8 were waited for; matrix products, arithmetic and copies ran while one was open for 2% of the time, Pallas kernels for 15%

profile of v2, /device:TPU:0, one launch (start us, length us, event | category | flops | bytes accessed | tf_op | source)
XLA Modules:
  0.0 70.5 jit_solution(15971119563830314904)
XLA Ops:
  0.7 0.5 collective-permute-start.4
  1.3 0.4 collective-permute-start.3
  1.7 1.4 %collective-permute-start.1 = (bf16[128,1024]{1,0:T(8,128)(2,1)}, bf16[128,1024]{1,0:T(8,128)(2,1)}, u32[]{:S(2)}, u32[]{:S(2)}) collective-permute-start(bf16[128,1024]{1,0:T(8,128)(2,1)} %bitcast.18), channel_id=1, source_target_pairs={{4,8},{8,4},{5,9},{9,5},{6,10},{10,6},{7,11},{11,7},{20,24},{24,20... | collective-permute-start | bytes 786440 | tf_op jit(solution)/shard_map/ppermute | solution.py:636
  3.1 4.8 %collective-permute-start = (bf16[128,1024]{1,0:T(8,128)(2,1)}, bf16[128,1024]{1,0:T(8,128)(2,1)}, u32[]{:S(2)}, u32[]{:S(2)}) collective-permute-start(bf16[128,1024]{1,0:T(8,128)(2,1)} %bitcast.19), channel_id=1, source_target_pairs={{0,4},{4,0},{8,12},{12,8},{1,5},{5,1},{9,13},{13,9},{2,6},{6,2},{1... | collective-permute-start | bytes 786440 | tf_op jit(solution)/shard_map/ppermute | solution.py:618
  8.7 1.3 %copy.15 = f32[1,3,1024]{2,1,0:T(4,128)} copy(f32[1,3,1024]{2,0,1:T(1,128)} %param.10) | data formatting | bytes 24576
  10.1 2.9 %front.1 = (f32[3,1024]{1,0:T(4,128)S(1)}, bf16[128,128]{1,0:T(8,128)(2,1)S(1)}, bf16[128,128]{1,0:T(8,128)(2,1)S(1)}, bf16[128,128]{1,0:T(8,128)(2,1)S(1)}, bf16[128,128]{1,0:T(8,128)(2,1)S(1)}) custom-call(s32[2]{0:T(128)S(1)} %pad_add_fusion.ids, bf16[2,8,128]{2,1,0:T(8,128)(2,1)S(1)} %broadcast_in_dim.10.feats, bf16[128,3072]{1,0:T(8,128)(2,1)} %rest_0_.1, ...), custom_call_target="tpu_custom_call" | custom-call | flops 134217728 | bytes 3043336 | tf_op jit(solution)/shard_map/front/pallas_call | solution.py:604
  12.9 0.5 collective-permute-start.5
  13.4 2.0 %collective-permute-start.6 = (bf16[128,128]{1,0:T(8,128)(2,1)S(1)}, bf16[128,128]{1,0:T(8,128)(2,1)S(1)}, u32[]{:S(2)}, u32[]{:S(2)}) collective-permute-start(bf16[128,128]{1,0:T(8,128)(2,1)S(1)} %get-tuple-element.39), channel_id=1, source_target_pairs={{0,12},{4,8},{8,4},{12,0},{1,13},{5,9},{9,5},{13,1},{2,14},{6,10},... | collective-permute-start | bytes 98312 | tf_op jit(solution)/shard_map/ppermute | solution.py:618
  15.4 1.1 %collective-permute-start.7 = (bf16[128,128]{1,0:T(8,128)(2,1)S(1)}, bf16[128,128]{1,0:T(8,128)(2,1)S(1)}, u32[]{:S(2)}, u32[]{:S(2)}) collective-permute-start(bf16[128,128]{1,0:T(8,128)(2,1)S(1)} %get-tuple-element.40), channel_id=1, source_target_pairs={{0,4},{4,0},{8,12},{12,8},{1,5},{5,1},{9,13},{13,9},{2,6},{6,2},{1... | collective-permute-start | bytes 98312 | tf_op jit(solution)/shard_map/ppermute | solution.py:618
  16.5 3.1 %mix.1 = (bf16[128,1024]{1,0:T(8,128)(2,1)S(1)}, f32[128,1024]{1,0:T(8,128)S(1)}, bf16[128,384]{1,0:T(8,128)(2,1)S(1)}, bf16[128,384]{1,0:T(8,128)(2,1)S(1)}, bf...) custom-call(s32[2]{0:T(128)S(1)} %pad_add_fusion.ids, bf16[128,1024]{1,0:T(8,128)(2,1)S(1)} %bitcast.20, ...), custom_call_target="tpu_custom_call" | custom-call | flops 402653184 | bytes 5234696 | tf_op jit(solution)/shard_map/mix/pallas_call | solution.py:604
  19.7 1.4 %collective-permute-start.8 = (bf16[128,384]{1,0:T(8,128)(2,1)S(1)}, bf16[128,384]{1,0:T(8,128)(2,1)S(1)}, u32[]{:S(2)}, u32[]{:S(2)}) collective-permute-start(bf16[128,384]{1,0:T(8,128)(2,1)S(1)} %get-tuple-element.42), channel_id=1, source_target_pairs={{0,8},{4,12},{8,0},{12,4},{1,9},{5,13},{9,1},{13,5},{2,10},{6,14},... | collective-permute-start | bytes 294920 | tf_op jit(solution)/shard_map/ppermute | solution.py:618
  21.1 1.9 %collective-permute-start.9 = (bf16[128,384]{1,0:T(8,128)(2,1)S(1)}, bf16[128,384]{1,0:T(8,128)(2,1)S(1)}, u32[]{:S(2)}, u32[]{:S(2)}) collective-permute-start(bf16[128,384]{1,0:T(8,128)(2,1)S(1)} %get-tuple-element.43), channel_id=1, source_target_pairs={{0,12},{4,8},{8,4},{12,0},{1,13},{5,9},{9,5},{13,1},{2,14},{6,10},... | collective-permute-start | bytes 294920 | tf_op jit(solution)/shard_map/ppermute | solution.py:618
  23.0 0.2 collective-permute-start.10
  23.2 6.3 %collective-permute-done.8.refs_1_ = bf16[128,384]{1,0:T(8,128)(2,1)S(1)} collective-permute-done((bf16[128,384]{1,0:T(8,128)(2,1)S(1)}, bf16[128,384]{1,0:T(8,128)(2,1)S(1)}, u32[]{:S(2)}, u32[]{:S(2)}) %collective-permute-start.8) | collective-permute-done | bytes 98336 | tf_op jit(solution)/shard_map/ppermute | solution.py:618
  29.7 4.4 %attend.1 = (bf16[128,512]{1,0:T(8,128)(2,1)S(1)}, bf16[128,512]{1,0:T(8,128)(2,1)S(1)}, bf16[128,512]{1,0:T(8,128)(2,1)S(1)}, bf16[128,512]{1,0:T(8,128)(2,1)S(1)}) custom-call(bf16[128,384]{1,0:T(8,128)(2,1)S(1)} %get-tuple-element.41.refs_0_, bf16[128,384]{1,0:T(8,128)(2,1)S(1)} %collective-permute-done.8.refs_1_, ...), custom_call_target="tpu_custom_call" | custom-call | flops 402653184 | bytes 1048576 | tf_op jit(solution)/shard_map/attend/pallas_call | solution.py:604
  34.1 1.9 %collective-permute-start.11 = (bf16[128,512]{1,0:T(8,128)(2,1)S(1)}, bf16[128,512]{1,0:T(8,128)(2,1)S(1)}, u32[]{:S(2)}, u32[]{:S(2)}) collective-permute-start(bf16[128,512]{1,0:T(8,128)(2,1)S(1)} %get-tuple-element.50), channel_id=1, source_target_pairs={{0,8},{4,12},{8,0},{12,4},{1,9},{5,13},{9,1},{13,5},{2,10},{6,14},... | collective-permute-start | bytes 393224 | tf_op jit(solution)/shard_map/ppermute | solution.py:618
  35.9 2.2 %collective-permute-start.12 = (bf16[128,512]{1,0:T(8,128)(2,1)S(1)}, bf16[128,512]{1,0:T(8,128)(2,1)S(1)}, u32[]{:S(2)}, u32[]{:S(2)}) collective-permute-start(bf16[128,512]{1,0:T(8,128)(2,1)S(1)} %get-tuple-element.51), channel_id=1, source_target_pairs={{0,12},{4,8},{8,4},{12,0},{1,13},{5,9},{9,5},{13,1},{2,14},{6,10},... | collective-permute-start | bytes 393224 | tf_op jit(solution)/shard_map/ppermute | solution.py:618
  38.1 7.6 %collective-permute-done.11.refs_1_ = bf16[128,512]{1,0:T(8,128)(2,1)S(1)} collective-permute-done((bf16[128,512]{1,0:T(8,128)(2,1)S(1)}, bf16[128,512]{1,0:T(8,128)(2,1)S(1)}, u32[]{:S(2)}, u32[]{:S(2)}) %collective-permute-start.11) | collective-permute-done | bytes 131104 | tf_op jit(solution)/shard_map/ppermute | solution.py:618
  45.8 0.6 collective-permute-done.13.refs_3_
  46.4 4.2 %tail.1 = (bf16[128,1024]{1,0:T(8,128)(2,1)S(1)}, f32[27,1024]{1,0:T(8,128)S(1)}) custom-call(s32[2]{0:T(128)S(1)} %pad_add_fusion.ids, bf16[128,512]{1,0:T(8,128)(2,1)S(1)} %get-tuple-element.49.refs_0_, bf16[128,512]{1,0:T(8,128)(2,1)S(1)} %collective-permute-done.11.refs_1_, bf16[128,512]{1,0:T(8,128)(2,1)S(1)} %collective-permute-done.12.refs_2_, ...), custom_call_target="tpu_custom_call" | custom-call | flops 402653184 | bytes 5890056 | tf_op jit(solution)/shard_map/tail/pallas_call | solution.py:604
  50.5 0.7 collective-permute-start.18
  51.2 4.0 %collective-permute-start.17 = (bf16[128,1024]{1,0:T(8,128)(2,1)S(1)}, bf16[128,1024]{1,0:T(8,128)(2,1)S(1)}, u32[]{:S(2)}, u32[]{:S(2)}) collective-permute-start(bf16[128,1024]{1,0:T(8,128)(2,1)S(1)} %get-tuple-element.58.grad), channel_id=1, source_target_pairs={{0,4},{4,0},{8,12},{12,8},{1,5},{5,1},{9,13},{13,9},{2,6},{6,2},{1... | collective-permute-start | bytes 786440 | tf_op jit(solution)/shard_map/ppermute | solution.py:618
  55.2 1.3 %collective-permute-done.14.right = f32[27,1024]{1,0:T(8,128)S(1)} collective-permute-done((f32[27,1024]{1,0:T(8,128)S(1)}, f32[27,1024]{1,0:T(8,128)S(1)}, u32[]{:S(2)}, u32[]{:S(2)}) %collective-permute-start.14) | collective-permute-done | bytes 110624 | tf_op jit(solution)/shard_map/ppermute | solution.py:618
  56.6 1.6 %collective-permute-start.15 = (bf16[27,1024]{1,0:T(8,128)(2,1)S(1)}, bf16[27,1024]{1,0:T(8,128)(2,1)S(1)}, u32[]{:S(2)}, u32[]{:S(2)}) collective-permute-start(bf16[27,1024]{1,0:T(8,128)(2,1)S(1)} %add_fsdp.1.left), channel_id=1, source_target_pairs={{0,2},{2,0},{1,3},{3,1},{4,6},{6,4},{5,7},{7,5},{8,10},{10,8},{9,1... | collective-permute-start | bytes 165896 | tf_op jit(solution)/shard_map/ppermute | solution.py:618
  58.1 2.2 %out.1 = bf16[128,1024]{1,0:T(8,128)(2,1)} custom-call(s32[2]{0:T(128)S(1)} %pad_add_fusion.ids, bf16[128,512]{1,0:T(8,128)(2,1)S(1)} %get-tuple-element.49.refs_0_, bf16[128,512]{1,0:T(8,128)(2,1)S(1)} %collective-permute-done.11.refs_1_, bf16[128,512]{1,0:T(8,128)(2,1)S(1)} %collective-permute-done.12.refs_2_, ...), custom_call_target="tpu_custom_call" | custom-call | flops 134217728 | bytes 2109448 | tf_op jit(solution)/shard_map/out/pallas_call | solution.py:604
  60.3 0.6 collective-permute-done.15.right
  61.1 1.5 %collective-permute-start.20 = (bf16[27,1024]{1,0:T(8,128)(2,1)S(1)}, bf16[27,1024]{1,0:T(8,128)(2,1)S(1)}, u32[]{:S(2)}, u32[]{:S(2)}) collective-permute-start(bf16[27,1024]{1,0:T(8,128)(2,1)S(1)} %add_dp.1.refs_0_), channel_id=1, source_target_pairs={{0,12},{4,8},{8,4},{12,0},{1,13},{5,9},{9,5},{13,1},{2,14},{6,10},... | collective-permute-start | bytes 165896 | tf_op jit(solution)/shard_map/ppermute | solution.py:618
  62.6 1.9 %collective-permute-start.19 = (bf16[27,1024]{1,0:T(8,128)(2,1)S(1)}, bf16[27,1024]{1,0:T(8,128)(2,1)S(1)}, u32[]{:S(2)}, u32[]{:S(2)}) collective-permute-start(bf16[27,1024]{1,0:T(8,128)(2,1)S(1)} %add_dp.1.refs_0_), channel_id=1, source_target_pairs={{0,8},{4,12},{8,0},{12,4},{1,9},{5,13},{9,1},{13,5},{2,10},{6,14},... | collective-permute-start | bytes 165896 | tf_op jit(solution)/shard_map/ppermute | solution.py:618
  64.5 2.4 %back_conv.1 = bf16[128,1024]{1,0:T(8,128)(2,1)} custom-call(s32[2]{0:T(128)S(1)} %pad_add_fusion.ids, bf16[128,1024]{1,0:T(8,128)(2,1)S(1)} %get-tuple-element.58.grad, bf16[128,1024]{1,0:T(8,128)(2,1)S(1)} %collective-permute-done.17.near, bf16[128,1024]{1,0:T(8,128)(2,1)S(1)} %collective-permute-done.18.far, f32[27,1024]{1,0:T(8,128)S(1)} %copy-done.4), custom_call_target="tpu_custom_call" | custom-call | bytes 1159176 | tf_op jit(solution)/shard_map/back_conv/pallas_call | solution.py:604
  66.9 0.3 collective-permute-done.20.refs_2_
  67.2 2.6 %collective-permute-done.19.refs_1_ = bf16[27,1024]{1,0:T(8,128)(2,1)S(1)} collective-permute-done((bf16[27,1024]{1,0:T(8,128)(2,1)S(1)}, bf16[27,1024]{1,0:T(8,128)(2,1)S(1)}, u32[]{:S(2)}, u32[]{:S(2)}) %collective-permute-start.19) | collective-permute-done | bytes 55328 | tf_op jit(solution)/shard_map/ppermute | solution.py:618
  69.8 0.7 add_seq.1
  (37 shorter events, 0.6 us)
Async XLA Ops:
  0.6 15.9 %copy-start = (bf16[512,1536]{1,0:T(8,128)(2,1)S(1)}, bf16[512,1536]{1,0:T(8,128)(2,1)}, u32[]{:S(2)}) copy-start(bf16[512,1536]{1,0:T(8,128)(2,1)} %refs_8_.1) | copy-start | bytes 4718596
  0.6 15.9 %copy-start.2 = (bf16[1,1,8,16,1024]{4,3,2,1,0:T(8,128)(2,1)S(1)}, bf16[1,1,8,16,1024]{4,3,2,1,0:T(8,128)(2,1)}, u32[]{:S(2)}) copy-start(bf16[1,1,8,16,1024]{4,3,2,1,0:T(8,128)(2,1)} %param.8) | copy-start | bytes 786436
  0.7 15.9 %copy-start.4 = (f32[27,1024]{1,0:T(8,128)S(1)}, f32[27,1024]{1,0:T(8,128)}, u32[]{:S(2)}) copy-start(f32[27,1024]{1,0:T(8,128)} %taps.3) | copy-start | bytes 331780
  0.7 15.8 %collective-permute-start.4 = (bf16[512,1536]{1,0:T(8,128)(2,1)}, bf16[512,1536]{1,0:T(8,128)(2,1)S(1)}, u32[]{:S(2)}, u32[]{:S(2)}) collective-permute-start(bf16[512,1536]{1,0:T(8,128)(2,1)} %refs_8_.1), channel_id=1, source_target_pairs={{0,1},{1,0},{2,3},{3,2},{4,5},{5,4},{6,7},{7,6},{8,9},{9,8},{10,11... | collective-permute-start | bytes 4718600 | tf_op jit(solution)/shard_map/ppermute | solution.py:618
  1.2 8.9 %collective-permute-start.2 = (bf16[128,3072]{1,0:T(8,128)(2,1)}, bf16[128,3072]{1,0:T(8,128)(2,1)}, u32[]{:S(2)}, u32[]{:S(2)}) collective-permute-start(bf16[128,3072]{1,0:T(8,128)(2,1)} %rest_0_.1), channel_id=1, source_target_pairs={{0,1},{1,0},{2,3},{3,2},{4,5},{5,4},{6,7},{7,6},{8,9},{9,8},{10,11... | collective-permute-start | bytes 2359304 | tf_op jit(solution)/shard_map/ppermute | solution.py:618
  1.3 8.8 %collective-permute-start.3 = (bf16[256,1024]{1,0:T(8,128)(2,1)}, bf16[256,1024]{1,0:T(8,128)(2,1)}, u32[]{:S(2)}, u32[]{:S(2)}) collective-permute-start(bf16[256,1024]{1,0:T(8,128)(2,1)} %refs_6_.1), channel_id=1, source_target_pairs={{0,1},{1,0},{2,3},{3,2},{4,5},{5,4},{6,7},{7,6},{8,9},{9,8},{10,11... | collective-permute-start | bytes 1572872 | tf_op jit(solution)/shard_map/ppermute | solution.py:618
  1.7 13.7 %collective-permute-start.1 = (bf16[128,1024]{1,0:T(8,128)(2,1)}, bf16[128,1024]{1,0:T(8,128)(2,1)}, u32[]{:S(2)}, u32[]{:S(2)}) collective-permute-start(bf16[128,1024]{1,0:T(8,128)(2,1)} %bitcast.18), channel_id=1, source_target_pairs={{4,8},{8,4},{5,9},{9,5},{6,10},{10,6},{7,11},{11,7},{20,24},{24,20... | collective-permute-start | bytes 786440 | tf_op jit(solution)/shard_map/ppermute | solution.py:636
  3.1 13.4 %collective-permute-start = (bf16[128,1024]{1,0:T(8,128)(2,1)}, bf16[128,1024]{1,0:T(8,128)(2,1)}, u32[]{:S(2)}, u32[]{:S(2)}) collective-permute-start(bf16[128,1024]{1,0:T(8,128)(2,1)} %bitcast.19), channel_id=1, source_target_pairs={{0,4},{4,0},{8,12},{12,8},{1,5},{5,1},{9,13},{13,9},{2,6},{6,2},{1... | collective-permute-start | bytes 786440 | tf_op jit(solution)/shard_map/ppermute | solution.py:618
  12.9 6.7 %collective-permute-start.5 = (bf16[128,128]{1,0:T(8,128)(2,1)S(1)}, bf16[128,128]{1,0:T(8,128)(2,1)S(1)}, u32[]{:S(2)}, u32[]{:S(2)}) collective-permute-start(bf16[128,128]{1,0:T(8,128)(2,1)S(1)} %get-tuple-element.38), channel_id=1, source_target_pairs={{0,8},{4,12},{8,0},{12,4},{1,9},{5,13},{9,1},{13,5},{2,10},{6,14},... | collective-permute-start | bytes 98312 | tf_op jit(solution)/shard_map/ppermute | solution.py:618
  13.4 6.3 %collective-permute-start.6 = (bf16[128,128]{1,0:T(8,128)(2,1)S(1)}, bf16[128,128]{1,0:T(8,128)(2,1)S(1)}, u32[]{:S(2)}, u32[]{:S(2)}) collective-permute-start(bf16[128,128]{1,0:T(8,128)(2,1)S(1)} %get-tuple-element.39), channel_id=1, source_target_pairs={{0,12},{4,8},{8,4},{12,0},{1,13},{5,9},{9,5},{13,1},{2,14},{6,10},... | collective-permute-start | bytes 98312 | tf_op jit(solution)/shard_map/ppermute | solution.py:618
  15.4 4.3 %collective-permute-start.7 = (bf16[128,128]{1,0:T(8,128)(2,1)S(1)}, bf16[128,128]{1,0:T(8,128)(2,1)S(1)}, u32[]{:S(2)}, u32[]{:S(2)}) collective-permute-start(bf16[128,128]{1,0:T(8,128)(2,1)S(1)} %get-tuple-element.40), channel_id=1, source_target_pairs={{0,4},{4,0},{8,12},{12,8},{1,5},{5,1},{9,13},{13,9},{2,6},{6,2},{1... | collective-permute-start | bytes 98312 | tf_op jit(solution)/shard_map/ppermute | solution.py:618
  19.6 26.7 %copy-start.3 = (bf16[1,1,8,16,1024]{4,3,2,1,0:T(8,128)(2,1)S(1)}, bf16[1,1,8,16,1024]{4,3,2,1,0:T(8,128)(2,1)}, u32[]{:S(2)}) copy-start(bf16[1,1,8,16,1024]{4,3,2,1,0:T(8,128)(2,1)} %param.15) | copy-start | bytes 786436
  19.7 9.9 %collective-permute-start.8 = (bf16[128,384]{1,0:T(8,128)(2,1)S(1)}, bf16[128,384]{1,0:T(8,128)(2,1)S(1)}, u32[]{:S(2)}, u32[]{:S(2)}) collective-permute-start(bf16[128,384]{1,0:T(8,128)(2,1)S(1)} %get-tuple-element.42), channel_id=1, source_target_pairs={{0,8},{4,12},{8,0},{12,4},{1,9},{5,13},{9,1},{13,5},{2,10},{6,14},... | collective-permute-start | bytes 294920 | tf_op jit(solution)/shard_map/ppermute | solution.py:618
  21.1 8.5 %collective-permute-start.9 = (bf16[128,384]{1,0:T(8,128)(2,1)S(1)}, bf16[128,384]{1,0:T(8,128)(2,1)S(1)}, u32[]{:S(2)}, u32[]{:S(2)}) collective-permute-start(bf16[128,384]{1,0:T(8,128)(2,1)S(1)} %get-tuple-element.43), channel_id=1, source_target_pairs={{0,12},{4,8},{8,4},{12,0},{1,13},{5,9},{9,5},{13,1},{2,14},{6,10},... | collective-permute-start | bytes 294920 | tf_op jit(solution)/shard_map/ppermute | solution.py:618
  23.0 6.6 %collective-permute-start.10 = (bf16[128,384]{1,0:T(8,128)(2,1)S(1)}, bf16[128,384]{1,0:T(8,128)(2,1)S(1)}, u32[]{:S(2)}, u32[]{:S(2)}) collective-permute-start(bf16[128,384]{1,0:T(8,128)(2,1)S(1)} %get-tuple-element.44), channel_id=1, source_target_pairs={{0,4},{4,0},{8,12},{12,8},{1,5},{5,1},{9,13},{13,9},{2,6},{6,2},{1... | collective-permute-start | bytes 294920 | tf_op jit(solution)/shard_map/ppermute | solution.py:618
  34.1 11.7 %collective-permute-start.11 = (bf16[128,512]{1,0:T(8,128)(2,1)S(1)}, bf16[128,512]{1,0:T(8,128)(2,1)S(1)}, u32[]{:S(2)}, u32[]{:S(2)}) collective-permute-start(bf16[128,512]{1,0:T(8,128)(2,1)S(1)} %get-tuple-element.50), channel_id=1, source_target_pairs={{0,8},{4,12},{8,0},{12,4},{1,9},{5,13},{9,1},{13,5},{2,10},{6,14},... | collective-permute-start | bytes 393224 | tf_op jit(solution)/shard_map/ppermute | solution.py:618
  35.9 9.8 %collective-permute-start.12 = (bf16[128,512]{1,0:T(8,128)(2,1)S(1)}, bf16[128,512]{1,0:T(8,128)(2,1)S(1)}, u32[]{:S(2)}, u32[]{:S(2)}) collective-permute-start(bf16[128,512]{1,0:T(8,128)(2,1)S(1)} %get-tuple-element.51), channel_id=1, source_target_pairs={{0,12},{4,8},{8,4},{12,0},{1,13},{5,9},{9,5},{13,1},{2,14},{6,10},... | collective-permute-start | bytes 393224 | tf_op jit(solution)/shard_map/ppermute | solution.py:618
  38.1 8.2 %collective-permute-start.13 = (bf16[128,512]{1,0:T(8,128)(2,1)S(1)}, bf16[128,512]{1,0:T(8,128)(2,1)S(1)}, u32[]{:S(2)}, u32[]{:S(2)}) collective-permute-start(bf16[128,512]{1,0:T(8,128)(2,1)S(1)} %get-tuple-element.52), channel_id=1, source_target_pairs={{0,4},{4,0},{8,12},{12,8},{1,5},{5,1},{9,13},{13,9},{2,6},{6,2},{1... | collective-permute-start | bytes 393224 | tf_op jit(solution)/shard_map/ppermute | solution.py:618
  46.4 11.8 %copy-start.1 = (bf16[256,1024]{1,0:T(8,128)(2,1)S(1)}, bf16[256,1024]{1,0:T(8,128)(2,1)}, u32[]{:S(2)}) copy-start(bf16[256,1024]{1,0:T(8,128)(2,1)} %refs_6_.1) | copy-start | bytes 1572868
  50.5 14.0 %collective-permute-start.18 = (bf16[128,1024]{1,0:T(8,128)(2,1)S(1)}, bf16[128,1024]{1,0:T(8,128)(2,1)S(1)}, u32[]{:S(2)}, u32[]{:S(2)}) collective-permute-start(bf16[128,1024]{1,0:T(8,128)(2,1)S(1)} %get-tuple-element.58.grad), channel_id=1, source_target_pairs={{4,8},{8,4},{5,9},{9,5},{6,10},{10,6},{7,11},{11,7},{20,24},{24,20... | collective-permute-start | bytes 786440 | tf_op jit(solution)/shard_map/ppermute | solution.py:636
  51.2 13.3 %collective-permute-start.17 = (bf16[128,1024]{1,0:T(8,128)(2,1)S(1)}, bf16[128,1024]{1,0:T(8,128)(2,1)S(1)}, u32[]{:S(2)}, u32[]{:S(2)}) collective-permute-start(bf16[128,1024]{1,0:T(8,128)(2,1)S(1)} %get-tuple-element.58.grad), channel_id=1, source_target_pairs={{0,4},{4,0},{8,12},{12,8},{1,5},{5,1},{9,13},{13,9},{2,6},{6,2},{1... | collective-permute-start | bytes 786440 | tf_op jit(solution)/shard_map/ppermute | solution.py:618
  55.2 1.3 %collective-permute-start.14 = (f32[27,1024]{1,0:T(8,128)S(1)}, f32[27,1024]{1,0:T(8,128)S(1)}, u32[]{:S(2)}, u32[]{:S(2)}) collective-permute-start(f32[27,1024]{1,0:T(8,128)S(1)} %get-tuple-element.55.left), channel_id=1, source_target_pairs={{0,1},{1,0},{2,3},{3,2},{4,5},{5,4},{6,7},{7,6},{8,9},{9,8},{10,11... | collective-permute-start | bytes 331784 | tf_op jit(solution)/shard_map/ppermute | solution.py:618
  56.6 4.3 %collective-permute-start.15 = (bf16[27,1024]{1,0:T(8,128)(2,1)S(1)}, bf16[27,1024]{1,0:T(8,128)(2,1)S(1)}, u32[]{:S(2)}, u32[]{:S(2)}) collective-permute-start(bf16[27,1024]{1,0:T(8,128)(2,1)S(1)} %add_fsdp.1.left), channel_id=1, source_target_pairs={{0,2},{2,0},{1,3},{3,1},{4,6},{6,4},{5,7},{7,5},{8,10},{10,8},{9,1... | collective-permute-start | bytes 165896 | tf_op jit(solution)/shard_map/ppermute | solution.py:618
  60.9 5.9 %collective-permute-start.16 = (bf16[27,1024]{1,0:T(8,128)(2,1)S(1)}, bf16[27,1024]{1,0:T(8,128)(2,1)S(1)}, u32[]{:S(2)}, u32[]{:S(2)}) collective-permute-start(bf16[27,1024]{1,0:T(8,128)(2,1)S(1)} %add_dp.1.refs_0_), channel_id=1, source_target_pairs={{0,4},{4,0},{8,12},{12,8},{1,5},{5,1},{9,13},{13,9},{2,6},{6,2},{1... | collective-permute-start | bytes 165896 | tf_op jit(solution)/shard_map/ppermute | solution.py:618
  61.1 6.1 %collective-permute-start.20 = (bf16[27,1024]{1,0:T(8,128)(2,1)S(1)}, bf16[27,1024]{1,0:T(8,128)(2,1)S(1)}, u32[]{:S(2)}, u32[]{:S(2)}) collective-permute-start(bf16[27,1024]{1,0:T(8,128)(2,1)S(1)} %add_dp.1.refs_0_), channel_id=1, source_target_pairs={{0,12},{4,8},{8,4},{12,0},{1,13},{5,9},{9,5},{13,1},{2,14},{6,10},... | collective-permute-start | bytes 165896 | tf_op jit(solution)/shard_map/ppermute | solution.py:618
  62.6 7.2 %collective-permute-start.19 = (bf16[27,1024]{1,0:T(8,128)(2,1)S(1)}, bf16[27,1024]{1,0:T(8,128)(2,1)S(1)}, u32[]{:S(2)}, u32[]{:S(2)}) collective-permute-start(bf16[27,1024]{1,0:T(8,128)(2,1)S(1)} %add_dp.1.refs_0_), channel_id=1, source_target_pairs={{0,8},{4,12},{8,0},{12,4},{1,9},{5,13},{9,1},{13,5},{2,10},{6,14},... | collective-permute-start | bytes 165896 | tf_op jit(solution)/shard_map/ppermute | solution.py:618

commit v3 on v2

--- a/solution.py
+++ b/solution.py
@@ -286,20 +286,18 @@
     return jnp.concatenate([value[inner:], empty], axis=0)
 
 
-def sided_taps(taps, odd):
-    before, after = taps[0:9], taps[18:27]
-    return jnp.where(odd, before, after), taps[9:18], jnp.where(odd, after, before)
-
-
-def conv_lanes(planes, taps, inner):
+def conv_lanes(planes, taps, odd, flipped, inner):
+    before, after = (taps[18:27], taps[0:9]) if flipped else (taps[0:9], taps[18:27])
+    sided = (jnp.where(odd, before, after), taps[9:18], jnp.where(odd, after, before))
     by_x = []
     for tap_x in range(3):
         total = None
         for tap_y in range(3):
             part = None
-            for tap_z in range(3):
-                index = 3 * tap_y + tap_x
-                term = taps[tap_z][index : index + 1] * planes[tap_z]
+            index = 3 * tap_y + tap_x
+            index = 8 - index if flipped else index
+            for plane, lines in zip(planes, sided):
+                term = lines[index : index + 1] * plane
                 part = term if part is None else part + term
             part = slab_shift(part, 1 - tap_y, inner)
             total = part if total is None else total + part
@@ -353,7 +351,7 @@
     projected = nn_dot(feats[0], wt_own[...]) + nn_dot(feats[1], wt_oth[...])
     for row in range(3):
         cols = slice(row * width, (row + 1) * width)
-        mod[row : row + 1, :] = projected[0:1, cols] + pxrd[row : row + 1, :]
+        mod[row : row + 1, :] = projected[0:1, cols] + pxrd[row]
     for copy in copies[3:]:
         copy.wait()
     gated = (mod[2:3, :] * as_f32(cot[...])).astype(jnp.bfloat16)
@@ -379,7 +377,7 @@
     for start in range(0, width, step):
         cols = slice(start, start + step)
         planes = [as_f32(ref[:, cols]) for ref in (near, tok, far)]
-        mixed = conv_lanes(planes, sided_taps(taps[:, cols], odd), inner)
+        mixed = conv_lanes(planes, taps[:, cols], odd, False, inner)
         rounded = (planes[1] + mixed).astype(jnp.bfloat16)
         resid[:, cols] = rounded
         sums = sums + as_f32(rounded)
@@ -413,66 +411,62 @@
 
 def attend_body(slots, *refs):
     qkv_in, grads_in = refs[:slots], refs[slots : 2 * slots]
-    backs = refs[2 * slots : 3 * slots]
-    keys, values, probs_all, dscore_all = refs[3 * slots :]
+    backs, attns = refs[2 * slots : 3 * slots], refs[3 * slots : 4 * slots]
+    weights, probs, dscore = refs[4 * slots :]
     rows, lanes = grads_in[0].shape
     heads = lanes // HD
+    count = slots * rows
     scale = 1.0 / math.sqrt(HD)
+    step = 64
+    zero = jnp.zeros((count, lanes), jnp.bfloat16)
+    owner = lax.broadcasted_iota(jnp.int32, (count, lanes), 1) // HD
+    masks = [owner == head for head in range(heads)]
+    query = jnp.concatenate([ref[:, :lanes] for ref in qkv_in], axis=0)
+    key = jnp.concatenate([ref[:, lanes : 2 * lanes] for ref in qkv_in], axis=0)
+    value = jnp.concatenate([ref[:, 2 * lanes :] for ref in qkv_in], axis=0)
+    grad = jnp.concatenate([ref[...] for ref in grads_in], axis=0)
+    scaled = query * jnp.asarray(scale, jnp.bfloat16)
+    for head in range(heads):
+        weights[head] = nt_dot(jnp.where(masks[head], scaled, zero), key)
+    for head in range(heads):
+        for start in range(0, count, step):
+            span = slice(start, start + step)
+            expo = jnp.exp(weights[head, span, :])
+            expo = expo * (1.0 / jnp.sum(expo, axis=1, keepdims=True))
+            weights[head, span, :] = expo
+            probs[span, head * count : (head + 1) * count] = expo.astype(jnp.bfloat16)
+    values = jnp.concatenate([jnp.where(mask, value, zero) for mask in masks], axis=0)
+    keys = jnp.concatenate([jnp.where(mask, key, zero) for mask in masks], axis=0)
+    attn = nn_dot(probs[...], values).astype(jnp.bfloat16)
     for k in range(slots):
-        keys[k * rows : (k + 1) * rows, :] = qkv_in[k][:, lanes : 2 * lanes]
-        values[k * rows : (k + 1) * rows, :] = qkv_in[k][:, 2 * lanes :]
-    owner = lax.broadcasted_iota(jnp.int32, (rows, lanes), 1) // HD
-    for k in range(slots):
-        query = qkv_in[k][:, :lanes]
-        grad = grads_in[k][...]
-        attn_total = None
-        pieces = []
-        for head in range(heads):
-            mine = owner == head
-            scores = nt_dot(jnp.where(mine, query, jnp.zeros_like(query)), keys[...]) * scale
-            expo = jnp.exp(scores)
-            weights = expo * (1.0 / jnp.sum(expo, axis=1, keepdims=True))
-            probs = weights.astype(jnp.bfloat16)
-            probs_all[head, k * rows : (k + 1) * rows, :] = probs
-            attn = jnp.where(mine, nn_dot(probs, values[...]), 0.0)
-            attn_total = attn if attn_total is None else attn_total + attn
-            pieces.append(weights)
-        attn_total = attn_total.astype(jnp.bfloat16)
-        backs[k][:, 3 * lanes :] = attn_total
-        product = as_f32(attn_total) * as_f32(grad)
-        dquery = None
-        for head in range(heads):
-            mine = owner == head
-            delta = jnp.sum(jnp.where(mine, product, 0.0), axis=1, keepdims=True)
-            dprob = nt_dot(jnp.where(mine, grad, jnp.zeros_like(grad)), values[...])
-            dscore = (pieces[head] * (dprob - delta) * scale).astype(jnp.bfloat16)
-            dscore_all[head, k * rows : (k + 1) * rows, :] = dscore
-            part = jnp.where(mine, nn_dot(dscore, keys[...]), 0.0)
-            dquery = part if dquery is None else dquery + part
-        backs[k][:, :lanes] = dquery.astype(jnp.bfloat16)
-    queries = jnp.concatenate([ref[:, :lanes] for ref in qkv_in], axis=0)
-    grads = jnp.concatenate([ref[...] for ref in grads_in], axis=0)
-    owner_all = lax.broadcasted_iota(jnp.int32, queries.shape, 1) // HD
-    dkeys = None
-    dvalues = None
+        attns[k][...] = attn[k * rows : (k + 1) * rows]
+    product = as_f32(attn) * as_f32(grad)
     for head in range(heads):
-        mine = owner_all == head
-        dkey = jnp.where(mine, tn_dot(dscore_all[head], queries), 0.0)
-        dvalue = jnp.where(mine, tn_dot(probs_all[head], grads), 0.0)
+        delta = jnp.sum(jnp.where(masks[head], product, 0.0), axis=1, keepdims=True)
+        dprob = nt_dot(jnp.where(masks[head], grad, zero), value)
+        for start in range(0, count, step):
+            span = slice(start, start + step)
+            part = weights[head, span, :] * (dprob[span] - delta[span])
+            dscore[span, head * count : (head + 1) * count] = part.astype(jnp.bfloat16)
+    dquery = nn_dot(dscore[...], keys) * scale
+    dkeys, dvalues = None, None
+    for head in range(heads):
+        span = slice(head * count, (head + 1) * count)
+        dkey = jnp.where(masks[head], tn_dot(dscore[:, span], scaled), 0.0)
+        dvalue = jnp.where(masks[head], tn_dot(probs[:, span], grad), 0.0)
         dkeys = dkey if dkeys is None else dkeys + dkey
         dvalues = dvalue if dvalues is None else dvalues + dvalue
     for k in range(slots):
-        backs[k][:, lanes : 2 * lanes] = dkeys[k * rows : (k + 1) * rows].astype(jnp.bfloat16)
-        backs[k][:, 2 * lanes : 3 * lanes] = dvalues[k * rows : (k + 1) * rows].astype(jnp.bfloat16)
-
-
-def tail_body(slots, inner, ids, *refs):
+        span = slice(k * rows, (k + 1) * rows)
+        for part, found in enumerate((dquery, dkeys, dvalues)):
+            backs[k][:, part * lanes : (part + 1) * lanes] = found[span].astype(jnp.bfloat16)
+
+
+def tail_body(slots, ids, *refs):
     backs = refs[:slots]
-    sections, resid, cot, mod, w_own, w_oth, tok, near, far = refs[slots : slots + 9]
-    dresid, terms = refs[slots + 9 : slots + 11]
-    by_group, dproj, dnormed = refs[slots + 11 :]
+    sections, resid, cot, mod, w_own, w_oth, dresid = refs[slots : slots + 7]
+    by_group, dproj, dnormed = refs[slots + 7 :]
     me, half = ids[0], ids[1]
-    odd = lax.rem(me, 2) == 1
     rows, width = resid.shape
     lanes = by_group.shape[3]
     inner_width = H * HD
@@ -522,6 +516,12 @@
         unit = (as_f32(resid[:, cols]) - mean) * inverse
         stream = as_f32(cot[:, cols]) + inverse * (grad - plain - unit * crossed)
         dresid[:, cols] = stream.astype(jnp.bfloat16)
+
+
+def terms_body(inner, ids, dresid, tok, near, far, terms, partial):
+    odd = lax.rem(ids[0], 2) == 1
+    rows, width = dresid.shape
+    step = 128
     for start in range(0, width, step):
         cols = slice(start, start + step)
         grad = as_f32(dresid[:, cols])
@@ -537,24 +537,30 @@
                         plane[high * inner : rows - low * inner]
                         * moved[tap_x][low * inner : rows - high * inner]
                     )
-                    prod = jnp.sum(prod.reshape(-1, 8, step), axis=0)
-                    lines.append(jnp.sum(prod, axis=0, keepdims=True))
+                    lines.append(jnp.sum(prod.reshape(-1, 8, step), axis=0))
             found.append(lines)
+        base = 27 * (start // step)
         for i in range(9):
             by_near, by_far = found[0][i], found[2][i]
-            terms[i : i + 1, cols] = jnp.where(odd, by_near, by_far)
-            terms[9 + i : 10 + i, cols] = found[1][i]
-            terms[18 + i : 19 + i, cols] = jnp.where(odd, by_far, by_near)
+            lines = (jnp.where(odd, by_near, by_far), found[1][i], jnp.where(odd, by_far, by_near))
+            for tap_z, line in enumerate(lines):
+                row = 8 * (base + 9 * tap_z + i)
+                partial[row : row + 8, :] = line
+    count = terms.shape[0]
+    total = partial[pl.ds(0, count, stride=8), :]
+    for i in range(1, 8):
+        total = total + partial[pl.ds(i, count, stride=8), :]
+    terms[...] = total.astype(terms.dtype)
 
 
 def out_body(slots, ids, *refs):
-    backs = refs[:slots]
+    attns = refs[:slots]
     resid, mod, wo_own, wo_oth, out, by_group = refs[slots:]
     me, half = ids[0], ids[1]
-    lanes = backs[0].shape[1] // 4
+    lanes = attns[0].shape[1]
     per_half = wo_own.shape[0] // lanes
     for k, gap in enumerate(distances(slots)):
-        by_group[lax.bitwise_xor(me, gap)] = backs[k][:, 3 * lanes :]
+        by_group[lax.bitwise_xor(me, gap)] = attns[k][...]
     total = None
     for weight, part in ((wo_own, half), (wo_oth, 1 - half)):
         for j in range(per_half):
@@ -570,23 +576,28 @@
     for start in range(0, width, step):
         cols = slice(start, start + step)
         planes = [as_f32(ref[:, cols]) for ref in (near, grad, far)]
-        lines = taps[:, cols]
-        turned = [jnp.concatenate([lines[r : r + 1] for r in range(26, -1, -1)], axis=0)]
-        mixed = conv_lanes(planes, sided_taps(turned[0], odd), inner)
+        mixed = conv_lanes(planes, taps[:, cols], odd, True, inner)
         out[:, cols] = (planes[1] + mixed).astype(jnp.bfloat16)
 
 
-def pair_body(left, right, out):
-    total = as_f32(left[...]) + as_f32(right[...])
-    out[...] = total.astype(out.dtype)
+def tree_sum(values):
+    while len(values) > 1:
+        values = [values[i] + values[i + 1] for i in range(0, len(values), 2)]
+    return values[0]
+
+
+def sum_body(*refs):
+    out = refs[-1]
+    out[...] = tree_sum([as_f32(ref[...]) for ref in refs[:-1]]).astype(out.dtype)
 
 
 def final_body(factor, slots, *refs):
     gaps = distances(slots)
-    values = [as_f32(refs[gaps.index(gap)][...]) for gap in range(slots)]
-    while len(values) > 1:
-        values = [values[i] + values[i + 1] for i in range(0, len(values), 2)]
-    refs[slots][...] = values[0] * factor
+    out = refs[slots]
+    total = tree_sum([as_f32(refs[gaps.index(gap)][...]) for gap in range(slots)]) * factor
+    lanes = total.shape[1]
+    for block in range(out.shape[1] // lanes):
+        out[:, block * lanes : (block + 1) * lanes] = total[27 * block : 27 * (block + 1)]
 
 
 def call(body, name, outs, args, scratch=(), flops=0, scalars=False, far_args=(), vmem=16):
@@ -653,7 +664,7 @@
 
     wo_oth = swapped(out_weight, "fsdp", 1)
     wt_oth = swapped(time_weight, "fsdp", 1)
-    near, far = neighbours(tok)
+    near, far = (pltpu.with_memory_space_constraint(v, pltpu.VMEM) for v in neighbours(tok))
     wq_oth = swapped(qkv_weight, "fsdp", 1)
 
     freq = 2 * time_weight.shape[0]
@@ -661,14 +672,15 @@
     own = lax.dynamic_slice_in_dim(feats, half, 1, axis=0)
     oth = lax.dynamic_slice_in_dim(feats, 1 - half, 1, axis=0)
     feats = jnp.broadcast_to(jnp.stack([own, oth]), (2, 8, freq // 2))
+    pxrd_rows = pxrd_mod.transpose(1, 0, 2)
     front = call(
         functools.partial(front_body, slots),
         "front",
         [shape((3, width), f32)] + [shape((rows, lanes), bf16)] * slots,
-        (ids, feats, time_weight, wt_oth, pxrd_mod[0], out_weight, wo_oth, cot),
+        (ids, feats, time_weight, wt_oth, pxrd_rows, out_weight, wo_oth, cot),
         [pltpu.VMEM((slots, rows, lanes), bf16)]
         + [pltpu.VMEM(time_weight.shape, bf16)] * 2
-        + [pltpu.VMEM(pxrd_mod.shape[1:], f32)]
+        + [pltpu.VMEM(pxrd_rows.shape, f32)]
         + [pltpu.VMEM(out_weight.shape, bf16)] * 2
         + [pltpu.VMEM((rows, width), bf16), pltpu.SemaphoreType.DMA((6,))],
         far_args=range(2, 8),
@@ -695,18 +707,22 @@
     attended = call(
         functools.partial(attend_body, slots),
         "attend",
-        [shape((rows, 4 * lanes), bf16)] * slots,
+        [shape((rows, 3 * lanes), bf16)] * slots + [shape((rows, lanes), bf16)] * slots,
         (*qkv_in, *grads_in),
-        [pltpu.VMEM((count, lanes), bf16)] * 2
-        + [pltpu.VMEM((lanes // HD, count, count), bf16)] * 2,
+        [
+            pltpu.VMEM((lanes // HD, count, count), f32),
+            pltpu.VMEM((count, lanes // HD * count), bf16),
+            pltpu.VMEM((count, lanes // HD * count), bf16),
+        ],
         flops=12 * count * count * lanes,
     )
-    backs = exchanged(attended)
-    dresid, terms = call(
-        functools.partial(tail_body, slots, inner),
+    backs = exchanged(attended[:slots])
+    attns = exchanged(attended[slots:])
+    (dresid,) = call(
+        functools.partial(tail_body, slots),
         "tail",
-        [shape((rows, width), bf16), shape((27, width), f32)],
-        (ids, *backs, sections, resid, cot, mod, qkv_weight, wq_oth, tok, near, far),
+        [shape((rows, width), bf16)],
+        (ids, *backs, sections, resid, cot, mod, qkv_weight, wq_oth),
         [
             pltpu.VMEM((slots, 3, rows, lanes), bf16),
             pltpu.VMEM((rows, 3 * H * HD), bf16),
@@ -715,22 +731,31 @@
         flops=2 * rows * width * 3 * H * HD,
         scalars=True,
     )
+    dresid, attns = lax.optimization_barrier((dresid, attns))
+    (terms,) = call(
+        functools.partial(terms_body, inner),
+        "terms",
+        [shape((27 * width // 128, 128), bf16)],
+        (ids, dresid, tok, near, far),
+        [pltpu.VMEM((8 * 27 * width // 128, 128), f32)],
+        scalars=True,
+    )
     (out,) = call(
         functools.partial(out_body, slots),
         "out",
         [shape((rows, width), bf16)],
-        (ids, *backs, resid, mod, out_weight, wo_oth),
+        (ids, *attns, resid, mod, out_weight, wo_oth),
         [pltpu.VMEM((slots, rows, lanes), bf16)],
         flops=2 * rows * width * H * HD,
         scalars=True,
     )
-    shape_terms = [shape((27, width), bf16)]
-    other = swapped(terms, "fsdp", 1)
     grad_near, grad_far = neighbours(dresid)
-    (terms,) = call(pair_body, "add_fsdp", shape_terms, (terms, other))
-    other = swapped(terms, "dp", 1)
-    other, out = lax.optimization_barrier((other, out))
-    (terms,) = call(pair_body, "add_dp", shape_terms, (terms, other))
+    pair = ("dp", "fsdp")
+    others = [lax.ppermute(terms, pair, [(i, i ^ gap) for i in range(4)]) for gap in (1, 2, 3)]
+    others[-1], out = lax.optimization_barrier((others[-1], out))
+    (terms,) = call(
+        sum_body, "add_dp", [shape((27 * width // 128, 128), bf16)], (terms, *others)
+    )
     (token_grad,) = call(
         functools.partial(back_conv_body, inner),
         "back_conv",

time: 70.8 us -> 67.6 us (0.955)
  waiting for transfers between devices: 19.5 us -> 15.5 us
  starting transfers between devices: 28.2 us -> 32.1 us
  Pallas kernels: 19.8 us -> 18 us
  local copies, waits for them, and re-layouts: 1.36 us -> 0.04 us
    ppermute x19 -> x20, waiting for transfers between devices: 19.5 us -> 14.3 us  [swapped(): return lax.ppermute(value, axis, [(i, i ^ distance) for i in range(count)])]
    ppermute x19 -> x20, starting transfers between devices: 26.1 us -> 28.1 us  [swapped(): return lax.ppermute(value, axis, [(i, i ^ distance) for i in range(count)])]
    ppermute x0 -> x3, starting transfers between devices: none -> 1.92 us  [slab_shards(): lax.ppermute(terms, pair, [(i, i ^ gap) for i in range(4)])]
    pallas_call x9, Pallas kernels: 19.8 us -> 18 us  [call(): pl.pallas_call(body, out_shape=tuple(outs), in_specs=specs, out_specs=(wh...]
    unnamed x12 -> x11, local copies, waits for them, and re-layouts: 1.34 us -> 0.03 us
    ppermute x0 -> x3, waiting for transfers between devices: none -> 1.27 us  [slab_shards(): lax.ppermute(terms, pair, [(i, i ^ gap) for i in range(4)])]
  transfers between devices with their start and end apart: 21 -> 25, of which waited for: 8 -> 10; matrix products, arithmetic and copies ran while one was open for 2% -> 0% of each run, Pallas kernels for 15% -> 23%
where the time goes in v3:
time: 67.6 us; the launch traced here: 67.3 us
  starting transfers between devices  32.1 us (47%)
  Pallas kernels  18 us (27%)
  waiting for transfers between devices  15.5 us (23%)
  between operations  1.45 us (2%)
    ppermute x20, starting transfers between devices, swapped(): return lax.ppermute(value, axis, [(i, i ^ distance) for i in range(count)])  28.1 us
    pallas_call x9, Pallas kernels, call(): pl.pallas_call(body, out_shape=tuple(outs), in_specs=specs, out_specs=(wh...  18 us
    ppermute x20, waiting for transfers between devices, swapped(): return lax.ppermute(value, axis, [(i, i ^ distance) for i in range(count)])  14.3 us
    ppermute x2, starting transfers between devices, neighbours(): lax.ppermute(value, 'seq', middle + [(j, i) for i, j in middle])  2.06 us
    ppermute x3, starting transfers between devices, slab_shards(): lax.ppermute(terms, pair, [(i, i ^ gap) for i in range(4)])  1.92 us
  transfers between devices with their start and end apart: 25, of which 10 were waited for; matrix products, arithmetic and copies ran while one was open for 0% of the time, Pallas kernels for 23%

profile of v3, /device:TPU:0, one launch (start us, length us, event | category | flops | bytes accessed | tf_op | source)
XLA Modules:
  0.0 67.3 jit_solution(13219076133940021086)
XLA Ops:
  0.7 0.5 collective-permute-start.4
  1.7 1.4 %collective-permute-start.1 = (bf16[128,1024]{1,0:T(8,128)(2,1)}, bf16[128,1024]{1,0:T(8,128)(2,1)}, u32[]{:S(2)}, u32[]{:S(2)}) collective-permute-start(bf16[128,1024]{1,0:T(8,128)(2,1)} %bitcast.18), channel_id=1, source_target_pairs={{4,8},{8,4},{5,9},{9,5},{6,10},{10,6},{7,11},{11,7},{20,24},{24,20... | collective-permute-start | bytes 786440 | tf_op jit(solution)/shard_map/ppermute | solution.py:647
  3.1 4.8 %collective-permute-start = (bf16[128,1024]{1,0:T(8,128)(2,1)}, bf16[128,1024]{1,0:T(8,128)(2,1)}, u32[]{:S(2)}, u32[]{:S(2)}) collective-permute-start(bf16[128,1024]{1,0:T(8,128)(2,1)} %bitcast.19), channel_id=1, source_target_pairs={{0,4},{4,0},{8,12},{12,8},{1,5},{5,1},{9,13},{13,9},{2,6},{6,2},{1... | collective-permute-start | bytes 786440 | tf_op jit(solution)/shard_map/ppermute | solution.py:629
  8.8 2.9 %front.1 = (f32[3,1024]{1,0:T(4,128)S(1)}, bf16[128,128]{1,0:T(8,128)(2,1)S(1)}, bf16[128,128]{1,0:T(8,128)(2,1)S(1)}, bf16[128,128]{1,0:T(8,128)(2,1)S(1)}, bf16[128,128]{1,0:T(8,128)(2,1)S(1)}) custom-call(s32[2]{0:T(128)S(1)} %pad_add_fusion.ids, bf16[2,8,128]{2,1,0:T(8,128)(2,1)S(1)} %broadcast_in_dim.10.feats, bf16[128,3072]{1,0:T(8,128)(2,1)} %rest_0_.1, ...), custom_call_target="tpu_custom_call" | custom-call | flops 134217728 | bytes 3043336 | tf_op jit(solution)/shard_map/front/pallas_call | solution.py:615
  11.6 1.7 %collective-permute-start.5 = (bf16[128,128]{1,0:T(8,128)(2,1)S(1)}, bf16[128,128]{1,0:T(8,128)(2,1)S(1)}, u32[]{:S(2)}, u32[]{:S(2)}) collective-permute-start(bf16[128,128]{1,0:T(8,128)(2,1)S(1)} %get-tuple-element.45), channel_id=1, source_target_pairs={{0,8},{4,12},{8,0},{12,4},{1,9},{5,13},{9,1},{13,5},{2,10},{6,14},... | collective-permute-start | bytes 98312 | tf_op jit(solution)/shard_map/ppermute | solution.py:629
  13.3 1.3 %collective-permute-start.6 = (bf16[128,128]{1,0:T(8,128)(2,1)S(1)}, bf16[128,128]{1,0:T(8,128)(2,1)S(1)}, u32[]{:S(2)}, u32[]{:S(2)}) collective-permute-start(bf16[128,128]{1,0:T(8,128)(2,1)S(1)} %get-tuple-element.46), channel_id=1, source_target_pairs={{0,12},{4,8},{8,4},{12,0},{1,13},{5,9},{9,5},{13,1},{2,14},{6,10},... | collective-permute-start | bytes 98312 | tf_op jit(solution)/shard_map/ppermute | solution.py:629
  14.7 0.5 collective-permute-start.7
  15.2 3.1 %mix.1 = (bf16[128,1024]{1,0:T(8,128)(2,1)S(1)}, f32[128,1024]{1,0:T(8,128)S(1)}, bf16[128,384]{1,0:T(8,128)(2,1)S(1)}, bf16[128,384]{1,0:T(8,128)(2,1)S(1)}, bf...) custom-call(s32[2]{0:T(128)S(1)} %pad_add_fusion.ids, bf16[128,1024]{1,0:T(8,128)(2,1)S(1)} %bitcast.20, ...), custom_call_target="tpu_custom_call" | custom-call | flops 402653184 | bytes 5234696 | tf_op jit(solution)/shard_map/mix/pallas_call | solution.py:615
  18.4 0.7 collective-permute-done.6.refs_6_
  19.0 1.9 %collective-permute-start.8 = (bf16[128,384]{1,0:T(8,128)(2,1)S(1)}, bf16[128,384]{1,0:T(8,128)(2,1)S(1)}, u32[]{:S(2)}, u32[]{:S(2)}) collective-permute-start(bf16[128,384]{1,0:T(8,128)(2,1)S(1)} %get-tuple-element.49), channel_id=1, source_target_pairs={{0,8},{4,12},{8,0},{12,4},{1,9},{5,13},{9,1},{13,5},{2,10},{6,14},... | collective-permute-start | bytes 294920 | tf_op jit(solution)/shard_map/ppermute | solution.py:629
  21.0 1.6 %collective-permute-start.9 = (bf16[128,384]{1,0:T(8,128)(2,1)S(1)}, bf16[128,384]{1,0:T(8,128)(2,1)S(1)}, u32[]{:S(2)}, u32[]{:S(2)}) collective-permute-start(bf16[128,384]{1,0:T(8,128)(2,1)S(1)} %get-tuple-element.50), channel_id=1, source_target_pairs={{0,12},{4,8},{8,4},{12,0},{1,13},{5,9},{9,5},{13,1},{2,14},{6,10},... | collective-permute-start | bytes 294920 | tf_op jit(solution)/shard_map/ppermute | solution.py:629
  22.6 6.2 %collective-permute-done.8.refs_1_ = bf16[128,384]{1,0:T(8,128)(2,1)S(1)} collective-permute-done((bf16[128,384]{1,0:T(8,128)(2,1)S(1)}, bf16[128,384]{1,0:T(8,128)(2,1)S(1)}, u32[]{:S(2)}, u32[]{:S(2)}) %collective-permute-start.8) | collective-permute-done | bytes 98336 | tf_op jit(solution)/shard_map/ppermute | solution.py:629
  29.1 2.1 %attend.1 = (bf16[128,384]{1,0:T(8,128)(2,1)S(1)}, bf16[128,384]{1,0:T(8,128)(2,1)S(1)}, bf16[128,384]{1,0:T(8,128)(2,1)S(1)}, bf16[128,384]{1,0:T(8,128)(2,1)S(...) custom-call(bf16[128,384]{1,0:T(8,128)(2,1)S(1)} %get-tuple-element., ...), custom_call_target="tpu_custom_call" | custom-call | flops 402653184 | bytes 1048576 | tf_op jit(solution)/shard_map/attend/pallas_call | solution.py:615
  31.2 2.4 %collective-permute-start.11 = (bf16[128,384]{1,0:T(8,128)(2,1)S(1)}, bf16[128,384]{1,0:T(8,128)(2,1)S(1)}, u32[]{:S(2)}, u32[]{:S(2)}) collective-permute-start(bf16[128,384]{1,0:T(8,128)(2,1)S(1)} %get-tuple-element.57), channel_id=1, source_target_pairs={{0,8},{4,12},{8,0},{12,4},{1,9},{5,13},{9,1},{13,5},{2,10},{6,14},... | collective-permute-start | bytes 294920 | tf_op jit(solution)/shard_map/ppermute | solution.py:629
  33.7 1.2 %collective-permute-start.12 = (bf16[128,384]{1,0:T(8,128)(2,1)S(1)}, bf16[128,384]{1,0:T(8,128)(2,1)S(1)}, u32[]{:S(2)}, u32[]{:S(2)}) collective-permute-start(bf16[128,384]{1,0:T(8,128)(2,1)S(1)} %get-tuple-element.58), channel_id=1, source_target_pairs={{0,12},{4,8},{8,4},{12,0},{1,13},{5,9},{9,5},{13,1},{2,14},{6,10},... | collective-permute-start | bytes 294920 | tf_op jit(solution)/shard_map/ppermute | solution.py:629
  34.9 3.2 %collective-permute-start.14 = (bf16[128,128]{1,0:T(8,128)(2,1)S(1)}, bf16[128,128]{1,0:T(8,128)(2,1)S(1)}, u32[]{:S(2)}, u32[]{:S(2)}) collective-permute-start(bf16[128,128]{1,0:T(8,128)(2,1)S(1)} %get-tuple-element.63), channel_id=1, source_target_pairs={{0,8},{4,12},{8,0},{12,4},{1,9},{5,13},{9,1},{13,5},{2,10},{6,14},... | collective-permute-start | bytes 98312 | tf_op jit(solution)/shard_map/ppermute | solution.py:629
  38.1 1.2 %collective-permute-start.15 = (bf16[128,128]{1,0:T(8,128)(2,1)S(1)}, bf16[128,128]{1,0:T(8,128)(2,1)S(1)}, u32[]{:S(2)}, u32[]{:S(2)}) collective-permute-start(bf16[128,128]{1,0:T(8,128)(2,1)S(1)} %get-tuple-element.64), channel_id=1, source_target_pairs={{0,12},{4,8},{8,4},{12,0},{1,13},{5,9},{9,5},{13,1},{2,14},{6,10},... | collective-permute-start | bytes 98312 | tf_op jit(solution)/shard_map/ppermute | solution.py:629
  39.3 2.6 %collective-permute-done.11.refs_1_ = bf16[128,384]{1,0:T(8,128)(2,1)S(1)} collective-permute-done((bf16[128,384]{1,0:T(8,128)(2,1)S(1)}, bf16[128,384]{1,0:T(8,128)(2,1)S(1)}, u32[]{:S(2)}, u32[]{:S(2)}) %collective-permute-start.11) | collective-permute-done | bytes 98336 | tf_op jit(solution)/shard_map/ppermute | solution.py:629
  41.8 0.5 collective-permute-done.13.refs_3_
  42.3 2.3 %tail.1.dresid.grad = bf16[128,1024]{1,0:T(8,128)(2,1)S(1)} custom-call(s32[2]{0:T(128)S(1)} %pad_add_fusion.ids, bf16[128,384]{1,0:T(8,128)(2,1)S(1)} %get-tuple-element.56.refs_0_, bf16[128,384]{1,0:T(8,128)(2,1)S(1)} %collective-permute-done.11.refs_1_, bf16[128,384]{1,0:T(8,128)(2,1)S(1)} %collective-permute-done.12.refs_2_, ...), custom_call_target="tpu_custom_call" | custom-call | flops 402653184 | bytes 4861960 | tf_op jit(solution)/shard_map/tail/pallas_call | solution.py:615
  44.7 1.0 %collective-permute-done.16.refs_3_ = bf16[128,128]{1,0:T(8,128)(2,1)S(1)} collective-permute-done((bf16[128,128]{1,0:T(8,128)(2,1)S(1)}, bf16[128,128]{1,0:T(8,128)(2,1)S(1)}, u32[]{:S(2)}, u32[]{:S(2)}) %collective-permute-start.16) | collective-permute-done | bytes 32800 | tf_op jit(solution)/shard_map/ppermute | solution.py:629
  45.7 0.7 collective-permute-start.22
  46.4 3.7 %collective-permute-start.21 = (bf16[128,1024]{1,0:T(8,128)(2,1)S(1)}, bf16[128,1024]{1,0:T(8,128)(2,1)S(1)}, u32[]{:S(2)}, u32[]{:S(2)}) collective-permute-start(bf16[128,1024]{1,0:T(8,128)(2,1)S(1)} %tail.1.dresid.grad), channel_id=1, source_target_pairs={{0,4},{4,0},{8,12},{12,8},{1,5},{5,1},{9,13},{13,9},{2,6},{6,2},{1... | collective-permute-start | bytes 786440 | tf_op jit(solution)/shard_map/ppermute | solution.py:629
  50.1 2.4 %terms.1.refs_0_ = bf16[216,128]{1,0:T(8,128)(2,1)S(1)} custom-call(s32[2]{0:T(128)S(1)} %pad_add_fusion.ids, bf16[128,1024]{1,0:T(8,128)(2,1)S(1)} %tail.1.dresid.grad, bf16[128,1024]{1,0:T(8,128)(2,1)S(1)} %bitcast.21, bf16[128,1024]{1,0:T(8,128)(2,1)} %collective-permute-done.near, bf16[128,1024]{1,0:T(8,128)(2,1)} %collective-permute-done.1.far), custom_call_target="tpu_custom_call" | custom-call | bytes 1103880 | tf_op jit(solution)/shard_map/terms/pallas_call | solution.py:615
  52.5 1.6 %collective-permute-start.19 = (bf16[216,128]{1,0:T(8,128)(2,1)S(1)}, bf16[216,128]{1,0:T(8,128)(2,1)S(1)}, u32[]{:S(2)}, u32[]{:S(2)}) collective-permute-start(bf16[216,128]{1,0:T(8,128)(2,1)S(1)} %terms.1.refs_0_), channel_id=1, source_target_pairs={{0,2},{1,3},{2,0},{3,1},{4,6},{5,7},{6,4},{7,5},{8,10},{9,11},{10,... | collective-permute-start | bytes 165896 | tf_op jit(solution)/shard_map/ppermute | solution.py:754
  54.3 2.2 %out.1 = bf16[128,1024]{1,0:T(8,128)(2,1)} custom-call(s32[2]{0:T(128)S(1)} %pad_add_fusion.ids, bf16[128,128]{1,0:T(8,128)(2,1)S(1)} %get-tuple-element.67.refs_0_, bf16[128,128]{1,0:T(8,128)(2,1)S(1)} %collective-permute-done.14.refs_1_, bf16[128,128]{1,0:T(8,128)(2,1)S(1)} %collective-permute-done.15.refs_2_, ...), custom_call_target="tpu_custom_call" | custom-call | flops 134217728 | bytes 1716232 | tf_op jit(solution)/shard_map/out/pallas_call | solution.py:615
  56.6 1.2 %collective-permute-done.19.refs_2_ = bf16[216,128]{1,0:T(8,128)(2,1)S(1)} collective-permute-done((bf16[216,128]{1,0:T(8,128)(2,1)S(1)}, bf16[216,128]{1,0:T(8,128)(2,1)S(1)}, u32[]{:S(2)}, u32[]{:S(2)}) %collective-permute-start.19) | collective-permute-done | bytes 55328 | tf_op jit(solution)/shard_map/ppermute | solution.py:754
  57.9 2.2 %collective-permute-start.24 = (bf16[216,128]{1,0:T(8,128)(2,1)S(1)}, bf16[216,128]{1,0:T(8,128)(2,1)S(1)}, u32[]{:S(2)}, u32[]{:S(2)}) collective-permute-start(bf16[216,128]{1,0:T(8,128)(2,1)S(1)} %add_dp.1.refs_0_), channel_id=1, source_target_pairs={{0,12},{4,8},{8,4},{12,0},{1,13},{5,9},{9,5},{13,1},{2,14},{6,10},... | collective-permute-start | bytes 165896 | tf_op jit(solution)/shard_map/ppermute | solution.py:629
  60.1 1.3 %collective-permute-start.23 = (bf16[216,128]{1,0:T(8,128)(2,1)S(1)}, bf16[216,128]{1,0:T(8,128)(2,1)S(1)}, u32[]{:S(2)}, u32[]{:S(2)}) collective-permute-start(bf16[216,128]{1,0:T(8,128)(2,1)S(1)} %add_dp.1.refs_0_), channel_id=1, source_target_pairs={{0,8},{4,12},{8,0},{12,4},{1,9},{5,13},{9,1},{13,5},{2,10},{6,14},... | collective-permute-start | bytes 165896 | tf_op jit(solution)/shard_map/ppermute | solution.py:629
  61.4 2.3 %back_conv.1 = bf16[128,1024]{1,0:T(8,128)(2,1)} custom-call(s32[2]{0:T(128)S(1)} %pad_add_fusion.ids, bf16[128,1024]{1,0:T(8,128)(2,1)S(1)} %tail.1.dresid.grad, bf16[128,1024]{1,0:T(8,128)(2,1)S(1)} %collective-permute-done.21.near, bf16[128,1024]{1,0:T(8,128)(2,1)S(1)} %collective-permute-done.22.far, f32[27,1024]{1,0:T(8,128)S(1)} %copy-done.4), custom_call_target="tpu_custom_call" | custom-call | bytes 1159176 | tf_op jit(solution)/shard_map/back_conv/pallas_call | solution.py:615
  64.2 2.4 %collective-permute-done.23.refs_1_ = bf16[216,128]{1,0:T(8,128)(2,1)S(1)} collective-permute-done((bf16[216,128]{1,0:T(8,128)(2,1)S(1)}, bf16[216,128]{1,0:T(8,128)(2,1)S(1)}, u32[]{:S(2)}, u32[]{:S(2)}) %collective-permute-start.23) | collective-permute-done | bytes 55328 | tf_op jit(solution)/shard_map/ppermute | solution.py:629
  66.6 0.7 %add_seq.1 = f32[27,1024]{1,0:T(8,128)} custom-call(bf16[216,128]{1,0:T(8,128)(2,1)S(1)} %add_dp.1.refs_0_, bf16[216,128]{1,0:T(8,128)(2,1)S(1)} %collective-permute-done.23.refs_1_, bf16[216,128]{1,0:T(8,128)(2,1)S(1)} %collective-permute-done.24.refs_2_, bf16[216,128]{1,0:T(8,128)(2,1)S(1)} %collective-permute-done.20.refs_3_), custom_call_target="tpu_custom_call" | custom-call | bytes 331776 | tf_op jit(solution)/shard_map/add_seq/pallas_call | solution.py:615
  (44 shorter events, 2.2 us)
Async XLA Ops:
  0.6 14.6 %copy-start = (bf16[512,1536]{1,0:T(8,128)(2,1)S(1)}, bf16[512,1536]{1,0:T(8,128)(2,1)}, u32[]{:S(2)}) copy-start(bf16[512,1536]{1,0:T(8,128)(2,1)} %refs_8_.1) | copy-start | bytes 4718596
  0.6 14.6 %copy-start.3 = (bf16[1,1,8,16,1024]{4,3,2,1,0:T(8,128)(2,1)S(1)}, bf16[1,1,8,16,1024]{4,3,2,1,0:T(8,128)(2,1)}, u32[]{:S(2)}) copy-start(bf16[1,1,8,16,1024]{4,3,2,1,0:T(8,128)(2,1)} %param.8) | copy-start | bytes 786436
  0.7 14.6 %copy-start.4 = (f32[27,1024]{1,0:T(8,128)S(1)}, f32[27,1024]{1,0:T(8,128)}, u32[]{:S(2)}) copy-start(f32[27,1024]{1,0:T(8,128)} %taps.3) | copy-start | bytes 331780
  0.7 14.5 %collective-permute-start.4 = (bf16[512,1536]{1,0:T(8,128)(2,1)}, bf16[512,1536]{1,0:T(8,128)(2,1)S(1)}, u32[]{:S(2)}, u32[]{:S(2)}) collective-permute-start(bf16[512,1536]{1,0:T(8,128)(2,1)} %refs_8_.1), channel_id=1, source_target_pairs={{0,1},{1,0},{2,3},{3,2},{4,5},{5,4},{6,7},{7,6},{8,9},{9,8},{10,11... | collective-permute-start | bytes 4718600 | tf_op jit(solution)/shard_map/ppermute | solution.py:629
  1.2 7.6 %collective-permute-start.2 = (bf16[128,3072]{1,0:T(8,128)(2,1)}, bf16[128,3072]{1,0:T(8,128)(2,1)}, u32[]{:S(2)}, u32[]{:S(2)}) collective-permute-start(bf16[128,3072]{1,0:T(8,128)(2,1)} %rest_0_.1), channel_id=1, source_target_pairs={{0,1},{1,0},{2,3},{3,2},{4,5},{5,4},{6,7},{7,6},{8,9},{9,8},{10,11... | collective-permute-start | bytes 2359304 | tf_op jit(solution)/shard_map/ppermute | solution.py:629
  1.3 7.5 %collective-permute-start.3 = (bf16[256,1024]{1,0:T(8,128)(2,1)}, bf16[256,1024]{1,0:T(8,128)(2,1)}, u32[]{:S(2)}, u32[]{:S(2)}) collective-permute-start(bf16[256,1024]{1,0:T(8,128)(2,1)} %refs_6_.1), channel_id=1, source_target_pairs={{0,1},{1,0},{2,3},{3,2},{4,5},{5,4},{6,7},{7,6},{8,9},{9,8},{10,11... | collective-permute-start | bytes 1572872 | tf_op jit(solution)/shard_map/ppermute | solution.py:629
  1.7 13.0 %collective-permute-start.1 = (bf16[128,1024]{1,0:T(8,128)(2,1)}, bf16[128,1024]{1,0:T(8,128)(2,1)}, u32[]{:S(2)}, u32[]{:S(2)}) collective-permute-start(bf16[128,1024]{1,0:T(8,128)(2,1)} %bitcast.18), channel_id=1, source_target_pairs={{4,8},{8,4},{5,9},{9,5},{6,10},{10,6},{7,11},{11,7},{20,24},{24,20... | collective-permute-start | bytes 786440 | tf_op jit(solution)/shard_map/ppermute | solution.py:647
  3.1 12.1 %collective-permute-start = (bf16[128,1024]{1,0:T(8,128)(2,1)}, bf16[128,1024]{1,0:T(8,128)(2,1)}, u32[]{:S(2)}, u32[]{:S(2)}) collective-permute-start(bf16[128,1024]{1,0:T(8,128)(2,1)} %bitcast.19), channel_id=1, source_target_pairs={{0,4},{4,0},{8,12},{12,8},{1,5},{5,1},{9,13},{13,9},{2,6},{6,2},{1... | collective-permute-start | bytes 786440 | tf_op jit(solution)/shard_map/ppermute | solution.py:629
  11.6 6.8 %collective-permute-start.5 = (bf16[128,128]{1,0:T(8,128)(2,1)S(1)}, bf16[128,128]{1,0:T(8,128)(2,1)S(1)}, u32[]{:S(2)}, u32[]{:S(2)}) collective-permute-start(bf16[128,128]{1,0:T(8,128)(2,1)S(1)} %get-tuple-element.45), channel_id=1, source_target_pairs={{0,8},{4,12},{8,0},{12,4},{1,9},{5,13},{9,1},{13,5},{2,10},{6,14},... | collective-permute-start | bytes 98312 | tf_op jit(solution)/shard_map/ppermute | solution.py:629
  13.3 5.7 %collective-permute-start.6 = (bf16[128,128]{1,0:T(8,128)(2,1)S(1)}, bf16[128,128]{1,0:T(8,128)(2,1)S(1)}, u32[]{:S(2)}, u32[]{:S(2)}) collective-permute-start(bf16[128,128]{1,0:T(8,128)(2,1)S(1)} %get-tuple-element.46), channel_id=1, source_target_pairs={{0,12},{4,8},{8,4},{12,0},{1,13},{5,9},{9,5},{13,1},{2,14},{6,10},... | collective-permute-start | bytes 98312 | tf_op jit(solution)/shard_map/ppermute | solution.py:629
  14.7 4.4 %collective-permute-start.7 = (bf16[128,128]{1,0:T(8,128)(2,1)S(1)}, bf16[128,128]{1,0:T(8,128)(2,1)S(1)}, u32[]{:S(2)}, u32[]{:S(2)}) collective-permute-start(bf16[128,128]{1,0:T(8,128)(2,1)S(1)} %get-tuple-element.47), channel_id=1, source_target_pairs={{0,4},{4,0},{8,12},{12,8},{1,5},{5,1},{9,13},{13,9},{2,6},{6,2},{1... | collective-permute-start | bytes 98312 | tf_op jit(solution)/shard_map/ppermute | solution.py:629
  18.4 24.0 %copy-start.2 = (bf16[1,1,8,16,1024]{4,3,2,1,0:T(8,128)(2,1)S(1)}, bf16[1,1,8,16,1024]{4,3,2,1,0:T(8,128)(2,1)}, u32[]{:S(2)}) copy-start(bf16[1,1,8,16,1024]{4,3,2,1,0:T(8,128)(2,1)} %param.15) | copy-start | bytes 786436
  19.0 9.7 %collective-permute-start.8 = (bf16[128,384]{1,0:T(8,128)(2,1)S(1)}, bf16[128,384]{1,0:T(8,128)(2,1)S(1)}, u32[]{:S(2)}, u32[]{:S(2)}) collective-permute-start(bf16[128,384]{1,0:T(8,128)(2,1)S(1)} %get-tuple-element.49), channel_id=1, source_target_pairs={{0,8},{4,12},{8,0},{12,4},{1,9},{5,13},{9,1},{13,5},{2,10},{6,14},... | collective-permute-start | bytes 294920 | tf_op jit(solution)/shard_map/ppermute | solution.py:629
  21.0 7.7 %collective-permute-start.9 = (bf16[128,384]{1,0:T(8,128)(2,1)S(1)}, bf16[128,384]{1,0:T(8,128)(2,1)S(1)}, u32[]{:S(2)}, u32[]{:S(2)}) collective-permute-start(bf16[128,384]{1,0:T(8,128)(2,1)S(1)} %get-tuple-element.50), channel_id=1, source_target_pairs={{0,12},{4,8},{8,4},{12,0},{1,13},{5,9},{9,5},{13,1},{2,14},{6,10},... | collective-permute-start | bytes 294920 | tf_op jit(solution)/shard_map/ppermute | solution.py:629
  22.6 6.6 %collective-permute-start.10 = (bf16[128,384]{1,0:T(8,128)(2,1)S(1)}, bf16[128,384]{1,0:T(8,128)(2,1)S(1)}, u32[]{:S(2)}, u32[]{:S(2)}) collective-permute-start(bf16[128,384]{1,0:T(8,128)(2,1)S(1)} %get-tuple-element.51), channel_id=1, source_target_pairs={{0,4},{4,0},{8,12},{12,8},{1,5},{5,1},{9,13},{13,9},{2,6},{6,2},{1... | collective-permute-start | bytes 294920 | tf_op jit(solution)/shard_map/ppermute | solution.py:629
  31.2 10.6 %collective-permute-start.11 = (bf16[128,384]{1,0:T(8,128)(2,1)S(1)}, bf16[128,384]{1,0:T(8,128)(2,1)S(1)}, u32[]{:S(2)}, u32[]{:S(2)}) collective-permute-start(bf16[128,384]{1,0:T(8,128)(2,1)S(1)} %get-tuple-element.57), channel_id=1, source_target_pairs={{0,8},{4,12},{8,0},{12,4},{1,9},{5,13},{9,1},{13,5},{2,10},{6,14},... | collective-permute-start | bytes 294920 | tf_op jit(solution)/shard_map/ppermute | solution.py:629
  33.7 8.1 %collective-permute-start.12 = (bf16[128,384]{1,0:T(8,128)(2,1)S(1)}, bf16[128,384]{1,0:T(8,128)(2,1)S(1)}, u32[]{:S(2)}, u32[]{:S(2)}) collective-permute-start(bf16[128,384]{1,0:T(8,128)(2,1)S(1)} %get-tuple-element.58), channel_id=1, source_target_pairs={{0,12},{4,8},{8,4},{12,0},{1,13},{5,9},{9,5},{13,1},{2,14},{6,10},... | collective-permute-start | bytes 294920 | tf_op jit(solution)/shard_map/ppermute | solution.py:629
  34.9 7.4 %collective-permute-start.13 = (bf16[128,384]{1,0:T(8,128)(2,1)S(1)}, bf16[128,384]{1,0:T(8,128)(2,1)S(1)}, u32[]{:S(2)}, u32[]{:S(2)}) collective-permute-start(bf16[128,384]{1,0:T(8,128)(2,1)S(1)} %get-tuple-element.59), channel_id=1, source_target_pairs={{0,4},{4,0},{8,12},{12,8},{1,5},{5,1},{9,13},{13,9},{2,6},{6,2},{1... | collective-permute-start | bytes 294920 | tf_op jit(solution)/shard_map/ppermute | solution.py:629
  34.9 9.8 %collective-permute-start.14 = (bf16[128,128]{1,0:T(8,128)(2,1)S(1)}, bf16[128,128]{1,0:T(8,128)(2,1)S(1)}, u32[]{:S(2)}, u32[]{:S(2)}) collective-permute-start(bf16[128,128]{1,0:T(8,128)(2,1)S(1)} %get-tuple-element.63), channel_id=1, source_target_pairs={{0,8},{4,12},{8,0},{12,4},{1,9},{5,13},{9,1},{13,5},{2,10},{6,14},... | collective-permute-start | bytes 98312 | tf_op jit(solution)/shard_map/ppermute | solution.py:629
  38.1 6.6 %collective-permute-start.15 = (bf16[128,128]{1,0:T(8,128)(2,1)S(1)}, bf16[128,128]{1,0:T(8,128)(2,1)S(1)}, u32[]{:S(2)}, u32[]{:S(2)}) collective-permute-start(bf16[128,128]{1,0:T(8,128)(2,1)S(1)} %get-tuple-element.64), channel_id=1, source_target_pairs={{0,12},{4,8},{8,4},{12,0},{1,13},{5,9},{9,5},{13,1},{2,14},{6,10},... | collective-permute-start | bytes 98312 | tf_op jit(solution)/shard_map/ppermute | solution.py:629
  41.8 3.9 %collective-permute-start.16 = (bf16[128,128]{1,0:T(8,128)(2,1)S(1)}, bf16[128,128]{1,0:T(8,128)(2,1)S(1)}, u32[]{:S(2)}, u32[]{:S(2)}) collective-permute-start(bf16[128,128]{1,0:T(8,128)(2,1)S(1)} %get-tuple-element.65), channel_id=1, source_target_pairs={{0,4},{4,0},{8,12},{12,8},{1,5},{5,1},{9,13},{13,9},{2,6},{6,2},{1... | collective-permute-start | bytes 98312 | tf_op jit(solution)/shard_map/ppermute | solution.py:629
  42.3 12.0 %copy-start.1 = (bf16[256,1024]{1,0:T(8,128)(2,1)S(1)}, bf16[256,1024]{1,0:T(8,128)(2,1)}, u32[]{:S(2)}) copy-start(bf16[256,1024]{1,0:T(8,128)(2,1)} %refs_6_.1) | copy-start | bytes 1572868
  45.7 15.7 %collective-permute-start.22 = (bf16[128,1024]{1,0:T(8,128)(2,1)S(1)}, bf16[128,1024]{1,0:T(8,128)(2,1)S(1)}, u32[]{:S(2)}, u32[]{:S(2)}) collective-permute-start(bf16[128,1024]{1,0:T(8,128)(2,1)S(1)} %tail.1.dresid.grad), channel_id=1, source_target_pairs={{4,8},{8,4},{5,9},{9,5},{6,10},{10,6},{7,11},{11,7},{20,24},{24,20... | collective-permute-start | bytes 786440 | tf_op jit(solution)/shard_map/ppermute | solution.py:647
  46.4 15.0 %collective-permute-start.21 = (bf16[128,1024]{1,0:T(8,128)(2,1)S(1)}, bf16[128,1024]{1,0:T(8,128)(2,1)S(1)}, u32[]{:S(2)}, u32[]{:S(2)}) collective-permute-start(bf16[128,1024]{1,0:T(8,128)(2,1)S(1)} %tail.1.dresid.grad), channel_id=1, source_target_pairs={{0,4},{4,0},{8,12},{12,8},{1,5},{5,1},{9,13},{13,9},{2,6},{6,2},{1... | collective-permute-start | bytes 786440 | tf_op jit(solution)/shard_map/ppermute | solution.py:629
  52.4 4.2 %collective-permute-start.17 = (bf16[216,128]{1,0:T(8,128)(2,1)S(1)}, bf16[216,128]{1,0:T(8,128)(2,1)S(1)}, u32[]{:S(2)}, u32[]{:S(2)}) collective-permute-start(bf16[216,128]{1,0:T(8,128)(2,1)S(1)} %terms.1.refs_0_), channel_id=1, source_target_pairs={{0,3},{1,2},{2,1},{3,0},{4,7},{5,6},{6,5},{7,4},{8,11},{9,10},{10,... | collective-permute-start | bytes 165896 | tf_op jit(solution)/shard_map/ppermute | solution.py:754
  52.5 5.3 %collective-permute-start.19 = (bf16[216,128]{1,0:T(8,128)(2,1)S(1)}, bf16[216,128]{1,0:T(8,128)(2,1)S(1)}, u32[]{:S(2)}, u32[]{:S(2)}) collective-permute-start(bf16[216,128]{1,0:T(8,128)(2,1)S(1)} %terms.1.refs_0_), channel_id=1, source_target_pairs={{0,2},{1,3},{2,0},{3,1},{4,6},{5,7},{6,4},{7,5},{8,10},{9,11},{10,... | collective-permute-start | bytes 165896 | tf_op jit(solution)/shard_map/ppermute | solution.py:754
  54.0 3.7 %collective-permute-start.18 = (bf16[216,128]{1,0:T(8,128)(2,1)S(1)}, bf16[216,128]{1,0:T(8,128)(2,1)S(1)}, u32[]{:S(2)}, u32[]{:S(2)}) collective-permute-start(bf16[216,128]{1,0:T(8,128)(2,1)S(1)} %terms.1.refs_0_), channel_id=1, source_target_pairs={{0,1},{1,0},{2,3},{3,2},{4,5},{5,4},{6,7},{7,6},{8,9},{9,8},{10,11... | collective-permute-start | bytes 165896 | tf_op jit(solution)/shard_map/ppermute | solution.py:754
  57.8 5.9 %collective-permute-start.20 = (bf16[216,128]{1,0:T(8,128)(2,1)S(1)}, bf16[216,128]{1,0:T(8,128)(2,1)S(1)}, u32[]{:S(2)}, u32[]{:S(2)}) collective-permute-start(bf16[216,128]{1,0:T(8,128)(2,1)S(1)} %add_dp.1.refs_0_), channel_id=1, source_target_pairs={{0,4},{4,0},{8,12},{12,8},{1,5},{5,1},{9,13},{13,9},{2,6},{6,2},{1... | collective-permute-start | bytes 165896 | tf_op jit(solution)/shard_map/ppermute | solution.py:629
  57.9 6.3 %collective-permute-start.24 = (bf16[216,128]{1,0:T(8,128)(2,1)S(1)}, bf16[216,128]{1,0:T(8,128)(2,1)S(1)}, u32[]{:S(2)}, u32[]{:S(2)}) collective-permute-start(bf16[216,128]{1,0:T(8,128)(2,1)S(1)} %add_dp.1.refs_0_), channel_id=1, source_target_pairs={{0,12},{4,8},{8,4},{12,0},{1,13},{5,9},{9,5},{13,1},{2,14},{6,10},... | collective-permute-start | bytes 165896 | tf_op jit(solution)/shard_map/ppermute | solution.py:629
  60.1 6.5 %collective-permute-start.23 = (bf16[216,128]{1,0:T(8,128)(2,1)S(1)}, bf16[216,128]{1,0:T(8,128)(2,1)S(1)}, u32[]{:S(2)}, u32[]{:S(2)}) collective-permute-start(bf16[216,128]{1,0:T(8,128)(2,1)S(1)} %add_dp.1.refs_0_), channel_id=1, source_target_pairs={{0,8},{4,12},{8,0},{12,4},{1,9},{5,13},{9,1},{13,5},{2,10},{6,14},... | collective-permute-start | bytes 165896 | tf_op jit(solution)/shard_map/ppermute | solution.py:629

commit v4 on v3

--- a/solution.py
+++ b/solution.py
@@ -286,23 +286,26 @@
     return jnp.concatenate([value[inner:], empty], axis=0)
 
 
-def conv_lanes(planes, taps, odd, flipped, inner):
-    before, after = (taps[18:27], taps[0:9]) if flipped else (taps[0:9], taps[18:27])
-    sided = (jnp.where(odd, before, after), taps[9:18], jnp.where(odd, after, before))
+def conv_lanes(planes, taps, flipped, inner):
     by_x = []
     for tap_x in range(3):
         total = None
         for tap_y in range(3):
             part = None
-            index = 3 * tap_y + tap_x
-            index = 8 - index if flipped else index
-            for plane, lines in zip(planes, sided):
-                term = lines[index : index + 1] * plane
+            for tap_z, plane in planes.items():
+                index = 9 * tap_z + 3 * tap_y + tap_x
+                index = 26 - index if flipped else index
+                term = taps[index : index + 1] * plane
                 part = term if part is None else part + term
             part = slab_shift(part, 1 - tap_y, inner)
             total = part if total is None else total + part
         by_x.append(total)
     return by_x[1] + row_shift(by_x[0], 1, inner) + row_shift(by_x[2], -1, inner)
+
+
+def sided(odd, near, far, body):
+    pl.when(odd)(lambda: body(near, far))
+    pl.when(jnp.logical_not(odd))(lambda: body(far, near))
 
 
 def head_mean(value):
@@ -335,9 +338,9 @@
 
 def front_body(slots, ids, feats, *rest):
     fetched = rest[:6]
-    mod, sends, by_group = rest[6], rest[7 : 7 + slots], rest[7 + slots]
-    wt_own, wt_oth, pxrd, wo_own, wo_oth, cot = held = rest[8 + slots : 14 + slots]
-    arrive = rest[14 + slots]
+    mod, wo_oth, sends = rest[6], rest[7], rest[8 : 8 + slots]
+    by_group, wt_own, wt_oth, pxrd, wo_own, cot, arrive = rest[8 + slots :]
+    held = (wt_own, wt_oth, pxrd, wo_own, wo_oth, cot)
     me, half = ids[0], ids[1]
     width = cot.shape[1]
     copies = [
@@ -368,19 +371,24 @@
 def mix_body(slots, inner, ids, tok, near, far, taps, mod, w_own, w_oth, *rest):
     resid, sections = rest[0], rest[1]
     sends = rest[2 : 2 + slots]
-    normed, by_group = rest[2 + slots :]
+    normed, by_group, sums_ref = rest[2 + slots :]
     me, half = ids[0], ids[1]
-    odd = lax.rem(me, 2) == 1
     rows, width = tok.shape
     step = 128
-    sums = jnp.zeros((rows, step), jnp.float32)
-    for start in range(0, width, step):
-        cols = slice(start, start + step)
-        planes = [as_f32(ref[:, cols]) for ref in (near, tok, far)]
-        mixed = conv_lanes(planes, taps[:, cols], odd, False, inner)
-        rounded = (planes[1] + mixed).astype(jnp.bfloat16)
-        resid[:, cols] = rounded
-        sums = sums + as_f32(rounded)
+
+    def all_planes(before, after):
+        sums = jnp.zeros((rows, step), jnp.float32)
+        for start in range(0, width, step):
+            cols = slice(start, start + step)
+            planes = {i: as_f32(ref[:, cols]) for i, ref in enumerate((before, tok, after))}
+            rounded = planes[1] + conv_lanes(planes, taps[:, cols], False, inner)
+            rounded = rounded.astype(jnp.bfloat16)
+            resid[:, cols] = rounded
+            sums = sums + as_f32(rounded)
+        sums_ref[...] = sums
+
+    sided(lax.rem(me, 2) == 1, near, far, all_planes)
+    sums = sums_ref[...]
     mean = jnp.sum(sums, axis=1, keepdims=True) * (1.0 / width)
     squares = jnp.zeros((rows, step), jnp.float32)
     for start in range(0, width, step):
@@ -462,11 +470,17 @@
             backs[k][:, part * lanes : (part + 1) * lanes] = found[span].astype(jnp.bfloat16)
 
 
-def tail_body(slots, ids, *refs):
+def tail_body(slots, inner, ids, *refs):
     backs = refs[:slots]
-    sections, resid, cot, mod, w_own, w_oth, dresid = refs[slots : slots + 7]
-    by_group, dproj, dnormed = refs[slots + 7 :]
+    sections, resid, cot, mod, w_own, w_oth, tok, near_far, far_far = refs[slots : slots + 9]
+    dresid, terms, by_group, dproj, dnormed, partial, near, far, arrive = refs[slots + 9 :]
     me, half = ids[0], ids[1]
+    copies = [
+        pltpu.make_async_copy(near_far, near, arrive.at[0]),
+        pltpu.make_async_copy(far_far, far, arrive.at[1]),
+    ]
+    for copy in copies:
+        copy.start()
     rows, width = resid.shape
     lanes = by_group.shape[3]
     inner_width = H * HD
@@ -516,20 +530,27 @@
         unit = (as_f32(resid[:, cols]) - mean) * inverse
         stream = as_f32(cot[:, cols]) + inverse * (grad - plain - unit * crossed)
         dresid[:, cols] = stream.astype(jnp.bfloat16)
-
-
-def terms_body(inner, ids, dresid, tok, near, far, terms, partial):
-    odd = lax.rem(ids[0], 2) == 1
+    for copy in copies:
+        copy.wait()
+    outer = functools.partial(tap_terms, inner, dresid, tok, partial)
+    sided(lax.rem(me, 2) == 1, near, far, outer)
+    count = terms.shape[0]
+    total = partial[pl.ds(0, count, stride=8), :]
+    for i in range(1, 8):
+        total = total + partial[pl.ds(i, count, stride=8), :]
+    terms[...] = total.astype(terms.dtype)
+
+
+def tap_terms(inner, dresid, tok, partial, before, after):
     rows, width = dresid.shape
     step = 128
     for start in range(0, width, step):
         cols = slice(start, start + step)
         grad = as_f32(dresid[:, cols])
         moved = [row_shift(grad, -1, inner), grad, row_shift(grad, 1, inner)]
-        found = []
-        for ref in (near, tok, far):
+        base = 27 * (start // step)
+        for tap_z, ref in enumerate((before, tok, after)):
             plane = as_f32(ref[:, cols])
-            lines = []
             for tap_y in range(3):
                 low, high = max(0, 1 - tap_y), max(0, tap_y - 1)
                 for tap_x in range(3):
@@ -537,20 +558,8 @@
                         plane[high * inner : rows - low * inner]
                         * moved[tap_x][low * inner : rows - high * inner]
                     )
-                    lines.append(jnp.sum(prod.reshape(-1, 8, step), axis=0))
-            found.append(lines)
-        base = 27 * (start // step)
-        for i in range(9):
-            by_near, by_far = found[0][i], found[2][i]
-            lines = (jnp.where(odd, by_near, by_far), found[1][i], jnp.where(odd, by_far, by_near))
-            for tap_z, line in enumerate(lines):
-                row = 8 * (base + 9 * tap_z + i)
-                partial[row : row + 8, :] = line
-    count = terms.shape[0]
-    total = partial[pl.ds(0, count, stride=8), :]
-    for i in range(1, 8):
-        total = total + partial[pl.ds(i, count, stride=8), :]
-    terms[...] = total.astype(terms.dtype)
+                    row = 8 * (base + 9 * tap_z + 3 * tap_y + tap_x)
+                    partial[row : row + 8, :] = jnp.sum(prod.reshape(-1, 8, step), axis=0)
 
 
 def out_body(slots, ids, *refs):
@@ -570,14 +579,17 @@
 
 
 def back_conv_body(inner, ids, grad, near, far, taps, out):
-    odd = lax.rem(ids[0], 2) == 1
     width = grad.shape[1]
     step = 128
-    for start in range(0, width, step):
-        cols = slice(start, start + step)
-        planes = [as_f32(ref[:, cols]) for ref in (near, grad, far)]
-        mixed = conv_lanes(planes, taps[:, cols], odd, True, inner)
-        out[:, cols] = (planes[1] + mixed).astype(jnp.bfloat16)
+
+    def all_planes(before, after):
+        for start in range(0, width, step):
+            cols = slice(start, start + step)
+            planes = {i: as_f32(ref[:, cols]) for i, ref in enumerate((before, grad, after))}
+            mixed = conv_lanes(planes, taps[:, cols], True, inner)
+            out[:, cols] = (planes[1] + mixed).astype(jnp.bfloat16)
+
+    sided(lax.rem(ids[0], 2) == 1, near, far, all_planes)
 
 
 def tree_sum(values):
@@ -630,7 +642,7 @@
 
 
 def distances(slots):
-    return (0, 2, 3, 1) if slots == 4 else (0, 1)
+    return (0, 2, 3, 1)[:slots]
 
 
 def exchanged(pieces):
@@ -641,8 +653,6 @@
 def neighbours(value):
     count = lax.axis_size("seq")
     near = swapped(value, "seq", 1)
-    if count == 2:
-        return near, jnp.zeros_like(value)
     middle = [(i, i + 1) for i in range(1, count - 1, 2)]
     return near, lax.ppermute(value, "seq", middle + [(j, i) for i, j in middle])
 
@@ -664,7 +674,7 @@
 
     wo_oth = swapped(out_weight, "fsdp", 1)
     wt_oth = swapped(time_weight, "fsdp", 1)
-    near, far = (pltpu.with_memory_space_constraint(v, pltpu.VMEM) for v in neighbours(tok))
+    near, far = neighbours(tok)
     wq_oth = swapped(qkv_weight, "fsdp", 1)
 
     freq = 2 * time_weight.shape[0]
@@ -676,19 +686,20 @@
     front = call(
         functools.partial(front_body, slots),
         "front",
-        [shape((3, width), f32)] + [shape((rows, lanes), bf16)] * slots,
+        [shape((3, width), f32), shape(out_weight.shape, bf16)]
+        + [shape((rows, lanes), bf16)] * slots,
         (ids, feats, time_weight, wt_oth, pxrd_rows, out_weight, wo_oth, cot),
         [pltpu.VMEM((slots, rows, lanes), bf16)]
         + [pltpu.VMEM(time_weight.shape, bf16)] * 2
         + [pltpu.VMEM(pxrd_rows.shape, f32)]
-        + [pltpu.VMEM(out_weight.shape, bf16)] * 2
+        + [pltpu.VMEM(out_weight.shape, bf16)]
         + [pltpu.VMEM((rows, width), bf16), pltpu.SemaphoreType.DMA((6,))],
         far_args=range(2, 8),
         flops=2 * rows * width * H * HD,
         scalars=True,
     )
-    mod = front[0]
-    grads_in = exchanged(front[1:])
+    mod, wo_held = front[:2]
+    grads_in = exchanged(front[2:])
 
     mixed = call(
         functools.partial(mix_body, slots, inner),
@@ -696,7 +707,11 @@
         [shape((rows, width), bf16), shape((rows, 2 * H * HD), f32)]
         + [shape((rows, 3 * lanes), bf16)] * slots,
         (ids, tok, near, far, conv_kernel, mod, qkv_weight, wq_oth),
-        [pltpu.VMEM((2, rows, width // 2), bf16), pltpu.VMEM((slots, rows, 3 * lanes), bf16)],
+        [
+            pltpu.VMEM((2, rows, width // 2), bf16),
+            pltpu.VMEM((slots, rows, 3 * lanes), bf16),
+            pltpu.VMEM((rows, 128), f32),
+        ],
         flops=2 * rows * width * 3 * H * HD,
         scalars=True,
     )
@@ -718,33 +733,30 @@
     )
     backs = exchanged(attended[:slots])
     attns = exchanged(attended[slots:])
-    (dresid,) = call(
-        functools.partial(tail_body, slots),
+    dresid, terms = call(
+        functools.partial(tail_body, slots, inner),
         "tail",
-        [shape((rows, width), bf16)],
-        (ids, *backs, sections, resid, cot, mod, qkv_weight, wq_oth),
+        [shape((rows, width), bf16), shape((27 * width // 128, 128), bf16)],
+        (ids, *backs, sections, resid, cot, mod, qkv_weight, wq_oth, tok, near, far),
         [
             pltpu.VMEM((slots, 3, rows, lanes), bf16),
             pltpu.VMEM((rows, 3 * H * HD), bf16),
             pltpu.VMEM((2, rows, width // 2), f32),
+            pltpu.VMEM((8 * 27 * width // 128, 128), f32),
+            pltpu.VMEM((rows, width), bf16),
+            pltpu.VMEM((rows, width), bf16),
+            pltpu.SemaphoreType.DMA((2,)),
         ],
         flops=2 * rows * width * 3 * H * HD,
         scalars=True,
+        far_args=(slots + 8, slots + 9),
     )
     dresid, attns = lax.optimization_barrier((dresid, attns))
-    (terms,) = call(
-        functools.partial(terms_body, inner),
-        "terms",
-        [shape((27 * width // 128, 128), bf16)],
-        (ids, dresid, tok, near, far),
-        [pltpu.VMEM((8 * 27 * width // 128, 128), f32)],
-        scalars=True,
-    )
     (out,) = call(
         functools.partial(out_body, slots),
         "out",
         [shape((rows, width), bf16)],
-        (ids, *attns, resid, mod, out_weight, wo_oth),
+        (ids, *attns, resid, mod, out_weight, wo_held),
         [pltpu.VMEM((slots, rows, lanes), bf16)],
         flops=2 * rows * width * H * HD,
         scalars=True,
@@ -779,7 +791,7 @@
         tokens, time_weight = args[0], args[3]
         lanes = H * HD // count
         fits = (
-            count in (2, 4)
+            count == 4
             and tokens.shape[0] == 1
             and tokens.shape[1] == 1
             and tokens.shape[3] % 16 == 0

time: 67.6 us -> 66.3 us (0.981)
  Pallas kernels: 18 us -> 16.3 us
  starting transfers between devices: 32.1 us -> 33.1 us
    pallas_call x9 -> x8, Pallas kernels: 18 us -> 16.3 us  [call(): pl.pallas_call(body, out_shape=tuple(outs), in_specs=specs, out_specs=(wh...]
    ppermute x20, waiting for transfers between devices: 14.3 us -> 13.3 us  [swapped(): return lax.ppermute(value, axis, [(i, i ^ distance) for i in range(count)])]
    ppermute x20, starting transfers between devices: 28.1 us -> 29 us  [swapped(): return lax.ppermute(value, axis, [(i, i ^ distance) for i in range(count)])]
  transfers between devices with their start and end apart: 25 -> 25, of which waited for: 10 -> 9; matrix products, arithmetic and copies ran while one was open for 0% -> 0% of each run, Pallas kernels for 23% -> 20%
where the time goes in v4:
time: 66.3 us; the launch traced here: 66.1 us
  starting transfers between devices  33.1 us (50%)
  Pallas kernels  16.3 us (25%)
  waiting for transfers between devices  15.1 us (23%)
  between operations  1.46 us (2%)
    ppermute x20, starting transfers between devices, swapped(): return lax.ppermute(value, axis, [(i, i ^ distance) for i in range(count)])  29 us
    pallas_call x8, Pallas kernels, call(): pl.pallas_call(body, out_shape=tuple(outs), in_specs=specs, out_specs=(wh...  16.3 us
    ppermute x20, waiting for transfers between devices, swapped(): return lax.ppermute(value, axis, [(i, i ^ distance) for i in range(count)])  13.3 us
    ppermute x2, starting transfers between devices, neighbours(): lax.ppermute(value, 'seq', middle + [(j, i) for i, j in middle])  2.25 us
    ppermute x3, starting transfers between devices, slab_shards(): lax.ppermute(terms, pair, [(i, i ^ gap) for i in range(4)])  1.86 us
    ppermute x3, waiting for transfers between devices, slab_shards(): lax.ppermute(terms, pair, [(i, i ^ gap) for i in range(4)])  1.78 us
  transfers between devices with their start and end apart: 25, of which 9 were waited for; matrix products, arithmetic and copies ran while one was open for 0% of the time, Pallas kernels for 20%

profile of v4, /device:TPU:0, one launch (start us, length us, event | category | flops | bytes accessed | tf_op | source)
XLA Modules:
  0.0 66.1 jit_solution(11571042458535981605)
XLA Ops:
  0.7 0.5 collective-permute-start.4
  1.7 1.4 %collective-permute-start.1 = (bf16[128,1024]{1,0:T(8,128)(2,1)}, bf16[128,1024]{1,0:T(8,128)(2,1)}, u32[]{:S(2)}, u32[]{:S(2)}) collective-permute-start(bf16[128,1024]{1,0:T(8,128)(2,1)} %bitcast.16), channel_id=1, source_target_pairs={{4,8},{8,4},{5,9},{9,5},{6,10},{10,6},{7,11},{11,7},{20,24},{24,20... | collective-permute-start | bytes 786440 | tf_op jit(solution)/shard_map/ppermute | solution.py:657
  3.1 4.8 %collective-permute-start = (bf16[128,1024]{1,0:T(8,128)(2,1)}, bf16[128,1024]{1,0:T(8,128)(2,1)}, u32[]{:S(2)}, u32[]{:S(2)}) collective-permute-start(bf16[128,1024]{1,0:T(8,128)(2,1)} %bitcast.17), channel_id=1, source_target_pairs={{0,4},{4,0},{8,12},{12,8},{1,5},{5,1},{9,13},{13,9},{2,6},{6,2},{1... | collective-permute-start | bytes 786440 | tf_op jit(solution)/shard_map/ppermute | solution.py:641
  8.8 2.8 %front.1 = (f32[3,1024]{1,0:T(4,128)S(1)}, bf16[256,1024]{1,0:T(8,128)(2,1)S(1)}, bf16[128,128]{1,0:T(8,128)(2,1)S(1)}, bf16[128,128]{1,0:T(8,128)(2,1)S(1)}, bf...) custom-call(s32[2]{0:T(128)S(1)} %pad_add_fusion.ids, bf16[2,8,128]{2,1,0:T(8,128)(2,1)S(1)} %broadcast_in_dim.10.feats, ...), custom_call_target="tpu_custom_call" | custom-call | flops 134217728 | bytes 3567624 | tf_op jit(solution)/shard_map/front/pallas_call | solution.py:627
  11.6 1.7 %collective-permute-start.5 = (bf16[128,128]{1,0:T(8,128)(2,1)S(1)}, bf16[128,128]{1,0:T(8,128)(2,1)S(1)}, u32[]{:S(2)}, u32[]{:S(2)}) collective-permute-start(bf16[128,128]{1,0:T(8,128)(2,1)S(1)} %get-tuple-element.48), channel_id=1, source_target_pairs={{0,8},{4,12},{8,0},{12,4},{1,9},{5,13},{9,1},{13,5},{2,10},{6,14},... | collective-permute-start | bytes 98312 | tf_op jit(solution)/shard_map/ppermute | solution.py:641
  13.3 1.4 %collective-permute-start.6 = (bf16[128,128]{1,0:T(8,128)(2,1)S(1)}, bf16[128,128]{1,0:T(8,128)(2,1)S(1)}, u32[]{:S(2)}, u32[]{:S(2)}) collective-permute-start(bf16[128,128]{1,0:T(8,128)(2,1)S(1)} %get-tuple-element.49), channel_id=1, source_target_pairs={{0,12},{4,8},{8,4},{12,0},{1,13},{5,9},{9,5},{13,1},{2,14},{6,10},... | collective-permute-start | bytes 98312 | tf_op jit(solution)/shard_map/ppermute | solution.py:641
  14.7 0.5 collective-permute-start.7
  15.2 3.2 %mix.1 = (bf16[128,1024]{1,0:T(8,128)(2,1)S(1)}, f32[128,1024]{1,0:T(8,128)S(1)}, bf16[128,384]{1,0:T(8,128)(2,1)S(1)}, bf16[128,384]{1,0:T(8,128)(2,1)S(1)}, bf...) custom-call(s32[2]{0:T(128)S(1)} %pad_add_fusion.ids, bf16[128,1024]{1,0:T(8,128)(2,1)S(1)} %bitcast.18, ...), custom_call_target="tpu_custom_call" | custom-call | flops 402653184 | bytes 5234696 | tf_op jit(solution)/shard_map/mix/pallas_call | solution.py:627
  18.4 0.6 collective-permute-done.6.refs_6_
  19.0 2.0 %collective-permute-start.8 = (bf16[128,384]{1,0:T(8,128)(2,1)S(1)}, bf16[128,384]{1,0:T(8,128)(2,1)S(1)}, u32[]{:S(2)}, u32[]{:S(2)}) collective-permute-start(bf16[128,384]{1,0:T(8,128)(2,1)S(1)} %get-tuple-element.52), channel_id=1, source_target_pairs={{0,8},{4,12},{8,0},{12,4},{1,9},{5,13},{9,1},{13,5},{2,10},{6,14},... | collective-permute-start | bytes 294920 | tf_op jit(solution)/shard_map/ppermute | solution.py:641
  21.0 1.6 %collective-permute-start.9 = (bf16[128,384]{1,0:T(8,128)(2,1)S(1)}, bf16[128,384]{1,0:T(8,128)(2,1)S(1)}, u32[]{:S(2)}, u32[]{:S(2)}) collective-permute-start(bf16[128,384]{1,0:T(8,128)(2,1)S(1)} %get-tuple-element.53), channel_id=1, source_target_pairs={{0,12},{4,8},{8,4},{12,0},{1,13},{5,9},{9,5},{13,1},{2,14},{6,10},... | collective-permute-start | bytes 294920 | tf_op jit(solution)/shard_map/ppermute | solution.py:641
  22.6 6.2 %collective-permute-done.8.refs_1_ = bf16[128,384]{1,0:T(8,128)(2,1)S(1)} collective-permute-done((bf16[128,384]{1,0:T(8,128)(2,1)S(1)}, bf16[128,384]{1,0:T(8,128)(2,1)S(1)}, u32[]{:S(2)}, u32[]{:S(2)}) %collective-permute-start.8) | collective-permute-done | bytes 98336 | tf_op jit(solution)/shard_map/ppermute | solution.py:641
  29.2 2.1 %attend.1 = (bf16[128,384]{1,0:T(8,128)(2,1)S(1)}, bf16[128,384]{1,0:T(8,128)(2,1)S(1)}, bf16[128,384]{1,0:T(8,128)(2,1)S(1)}, bf16[128,384]{1,0:T(8,128)(2,1)S(...) custom-call(bf16[128,384]{1,0:T(8,128)(2,1)S(1)} %get-tuple-element., ...), custom_call_target="tpu_custom_call" | custom-call | flops 402653184 | bytes 1048576 | tf_op jit(solution)/shard_map/attend/pallas_call | solution.py:627
  31.3 2.4 %collective-permute-start.11 = (bf16[128,384]{1,0:T(8,128)(2,1)S(1)}, bf16[128,384]{1,0:T(8,128)(2,1)S(1)}, u32[]{:S(2)}, u32[]{:S(2)}) collective-permute-start(bf16[128,384]{1,0:T(8,128)(2,1)S(1)} %get-tuple-element.60), channel_id=1, source_target_pairs={{0,8},{4,12},{8,0},{12,4},{1,9},{5,13},{9,1},{13,5},{2,10},{6,14},... | collective-permute-start | bytes 294920 | tf_op jit(solution)/shard_map/ppermute | solution.py:641
  33.7 1.2 %collective-permute-start.12 = (bf16[128,384]{1,0:T(8,128)(2,1)S(1)}, bf16[128,384]{1,0:T(8,128)(2,1)S(1)}, u32[]{:S(2)}, u32[]{:S(2)}) collective-permute-start(bf16[128,384]{1,0:T(8,128)(2,1)S(1)} %get-tuple-element.61), channel_id=1, source_target_pairs={{0,12},{4,8},{8,4},{12,0},{1,13},{5,9},{9,5},{13,1},{2,14},{6,10},... | collective-permute-start | bytes 294920 | tf_op jit(solution)/shard_map/ppermute | solution.py:641
  34.9 3.1 %collective-permute-start.15 = (bf16[128,128]{1,0:T(8,128)(2,1)S(1)}, bf16[128,128]{1,0:T(8,128)(2,1)S(1)}, u32[]{:S(2)}, u32[]{:S(2)}) collective-permute-start(bf16[128,128]{1,0:T(8,128)(2,1)S(1)} %get-tuple-element.68), channel_id=1, source_target_pairs={{0,8},{4,12},{8,0},{12,4},{1,9},{5,13},{9,1},{13,5},{2,10},{6,14},... | collective-permute-start | bytes 98312 | tf_op jit(solution)/shard_map/ppermute | solution.py:641
  38.1 1.2 %collective-permute-start.16 = (bf16[128,128]{1,0:T(8,128)(2,1)S(1)}, bf16[128,128]{1,0:T(8,128)(2,1)S(1)}, u32[]{:S(2)}, u32[]{:S(2)}) collective-permute-start(bf16[128,128]{1,0:T(8,128)(2,1)S(1)} %get-tuple-element.69), channel_id=1, source_target_pairs={{0,12},{4,8},{8,4},{12,0},{1,13},{5,9},{9,5},{13,1},{2,14},{6,10},... | collective-permute-start | bytes 98312 | tf_op jit(solution)/shard_map/ppermute | solution.py:641
  39.3 2.5 %collective-permute-done.11.refs_1_ = bf16[128,384]{1,0:T(8,128)(2,1)S(1)} collective-permute-done((bf16[128,384]{1,0:T(8,128)(2,1)S(1)}, bf16[128,384]{1,0:T(8,128)(2,1)S(1)}, u32[]{:S(2)}, u32[]{:S(2)}) %collective-permute-start.11) | collective-permute-done | bytes 98336 | tf_op jit(solution)/shard_map/ppermute | solution.py:641
  41.8 0.7 %collective-permute-done.13.refs_3_ = bf16[128,384]{1,0:T(8,128)(2,1)S(1)} collective-permute-done((bf16[128,384]{1,0:T(8,128)(2,1)S(1)}, bf16[128,384]{1,0:T(8,128)(2,1)S(1)}, u32[]{:S(2)}, u32[]{:S(2)}) %collective-permute-start.13) | collective-permute-done | bytes 98336 | tf_op jit(solution)/shard_map/ppermute | solution.py:641
  42.5 3.5 %tail.1 = (bf16[128,1024]{1,0:T(8,128)(2,1)S(1)}, bf16[216,128]{1,0:T(8,128)(2,1)S(1)}) custom-call(s32[2]{0:T(128)S(1)} %pad_add_fusion.ids, bf16[128,384]{1,0:T(8,128)(2,1)S(1)} %get-tuple-element.59.refs_0_, bf16[128,384]{1,0:T(8,128)(2,1)S(1)} %collective-permute-done.11.refs_1_, bf16[128,384]{1,0:T(8,128)(2,1)S(1)} %collective-permute-done.12.refs_2_, ...), custom_call_target="tpu_custom_call" | custom-call | flops 402653184 | bytes 5703688 | tf_op jit(solution)/shard_map/tail/pallas_call | solution.py:627
  46.1 0.9 %collective-permute-start.22 = (bf16[128,1024]{1,0:T(8,128)(2,1)S(1)}, bf16[128,1024]{1,0:T(8,128)(2,1)S(1)}, u32[]{:S(2)}, u32[]{:S(2)}) collective-permute-start(bf16[128,1024]{1,0:T(8,128)(2,1)S(1)} %get-tuple-element.78.grad), channel_id=1, source_target_pairs={{4,8},{8,4},{5,9},{9,5},{6,10},{10,6},{7,11},{11,7},{20,24},{24,20... | collective-permute-start | bytes 786440 | tf_op jit(solution)/shard_map/ppermute | solution.py:657
  46.9 4.4 %collective-permute-start.21 = (bf16[128,1024]{1,0:T(8,128)(2,1)S(1)}, bf16[128,1024]{1,0:T(8,128)(2,1)S(1)}, u32[]{:S(2)}, u32[]{:S(2)}) collective-permute-start(bf16[128,1024]{1,0:T(8,128)(2,1)S(1)} %get-tuple-element.78.grad), channel_id=1, source_target_pairs={{0,4},{4,0},{8,12},{12,8},{1,5},{5,1},{9,13},{13,9},{2,6},{6,2},{1... | collective-permute-start | bytes 786440 | tf_op jit(solution)/shard_map/ppermute | solution.py:641
  51.3 1.5 %collective-permute-start.19 = (bf16[216,128]{1,0:T(8,128)(2,1)S(1)}, bf16[216,128]{1,0:T(8,128)(2,1)S(1)}, u32[]{:S(2)}, u32[]{:S(2)}) collective-permute-start(bf16[216,128]{1,0:T(8,128)(2,1)S(1)} %get-tuple-element.65.refs_0_), channel_id=1, source_target_pairs={{0,2},{1,3},{2,0},{3,1},{4,6},{5,7},{6,4},{7,5},{8,10},{9,11},{10,... | collective-permute-start | bytes 165896 | tf_op jit(solution)/shard_map/ppermute | solution.py:766
  53.2 1.7 %out.1 = bf16[128,1024]{1,0:T(8,128)(2,1)} custom-call(s32[2]{0:T(128)S(1)} %pad_add_fusion.ids, bf16[128,128]{1,0:T(8,128)(2,1)S(1)} %get-tuple-element.71.refs_0_, bf16[128,128]{1,0:T(8,128)(2,1)S(1)} %collective-permute-done.15.refs_1_, bf16[128,128]{1,0:T(8,128)(2,1)S(1)} %collective-permute-done.16.refs_2_, ...), custom_call_target="tpu_custom_call" | custom-call | flops 134217728 | bytes 1716232 | tf_op jit(solution)/shard_map/out/pallas_call | solution.py:627
  54.8 0.6 collective-permute-done.14.refs_3_
  55.4 1.2 %collective-permute-done.19.refs_2_ = bf16[216,128]{1,0:T(8,128)(2,1)S(1)} collective-permute-done((bf16[216,128]{1,0:T(8,128)(2,1)S(1)}, bf16[216,128]{1,0:T(8,128)(2,1)S(1)}, u32[]{:S(2)}, u32[]{:S(2)}) %collective-permute-start.19) | collective-permute-done | bytes 55328 | tf_op jit(solution)/shard_map/ppermute | solution.py:766
  56.8 2.2 %collective-permute-start.24 = (bf16[216,128]{1,0:T(8,128)(2,1)S(1)}, bf16[216,128]{1,0:T(8,128)(2,1)S(1)}, u32[]{:S(2)}, u32[]{:S(2)}) collective-permute-start(bf16[216,128]{1,0:T(8,128)(2,1)S(1)} %add_dp.1.refs_0_), channel_id=1, source_target_pairs={{0,12},{4,8},{8,4},{12,0},{1,13},{5,9},{9,5},{13,1},{2,14},{6,10},... | collective-permute-start | bytes 165896 | tf_op jit(solution)/shard_map/ppermute | solution.py:641
  58.9 1.3 %collective-permute-start.23 = (bf16[216,128]{1,0:T(8,128)(2,1)S(1)}, bf16[216,128]{1,0:T(8,128)(2,1)S(1)}, u32[]{:S(2)}, u32[]{:S(2)}) collective-permute-start(bf16[216,128]{1,0:T(8,128)(2,1)S(1)} %add_dp.1.refs_0_), channel_id=1, source_target_pairs={{0,8},{4,12},{8,0},{12,4},{1,9},{5,13},{9,1},{13,5},{2,10},{6,14},... | collective-permute-start | bytes 165896 | tf_op jit(solution)/shard_map/ppermute | solution.py:641
  60.2 2.3 %back_conv.1 = bf16[128,1024]{1,0:T(8,128)(2,1)} custom-call(s32[2]{0:T(128)S(1)} %pad_add_fusion.ids, bf16[128,1024]{1,0:T(8,128)(2,1)S(1)} %get-tuple-element.78.grad, bf16[128,1024]{1,0:T(8,128)(2,1)S(1)} %collective-permute-done.21.near, bf16[128,1024]{1,0:T(8,128)(2,1)S(1)} %collective-permute-done.22.far, f32[27,1024]{1,0:T(8,128)S(1)} %copy-done.4), custom_call_target="tpu_custom_call" | custom-call | bytes 1159176 | tf_op jit(solution)/shard_map/back_conv/pallas_call | solution.py:627
  62.5 0.5 collective-permute-done.24.refs_2_
  63.0 2.4 %collective-permute-done.23.refs_1_ = bf16[216,128]{1,0:T(8,128)(2,1)S(1)} collective-permute-done((bf16[216,128]{1,0:T(8,128)(2,1)S(1)}, bf16[216,128]{1,0:T(8,128)(2,1)S(1)}, u32[]{:S(2)}, u32[]{:S(2)}) %collective-permute-start.23) | collective-permute-done | bytes 55328 | tf_op jit(solution)/shard_map/ppermute | solution.py:641
  65.4 0.7 %add_seq.1 = f32[27,1024]{1,0:T(8,128)} custom-call(bf16[216,128]{1,0:T(8,128)(2,1)S(1)} %add_dp.1.refs_0_, bf16[216,128]{1,0:T(8,128)(2,1)S(1)} %collective-permute-done.23.refs_1_, bf16[216,128]{1,0:T(8,128)(2,1)S(1)} %collective-permute-done.24.refs_2_, bf16[216,128]{1,0:T(8,128)(2,1)S(1)} %collective-permute-done.20.refs_3_), custom_call_target="tpu_custom_call" | custom-call | bytes 331776 | tf_op jit(solution)/shard_map/add_seq/pallas_call | solution.py:627
  (43 shorter events, 1.7 us)
Async XLA Ops:
  0.6 14.6 %copy-start = (bf16[512,1536]{1,0:T(8,128)(2,1)S(1)}, bf16[512,1536]{1,0:T(8,128)(2,1)}, u32[]{:S(2)}) copy-start(bf16[512,1536]{1,0:T(8,128)(2,1)} %refs_8_.1) | copy-start | bytes 4718596
  0.6 14.6 %copy-start.2 = (bf16[1,1,8,16,1024]{4,3,2,1,0:T(8,128)(2,1)S(1)}, bf16[1,1,8,16,1024]{4,3,2,1,0:T(8,128)(2,1)}, u32[]{:S(2)}) copy-start(bf16[1,1,8,16,1024]{4,3,2,1,0:T(8,128)(2,1)} %param.8) | copy-start | bytes 786436
  0.7 14.6 %copy-start.4 = (f32[27,1024]{1,0:T(8,128)S(1)}, f32[27,1024]{1,0:T(8,128)}, u32[]{:S(2)}) copy-start(f32[27,1024]{1,0:T(8,128)} %taps.3) | copy-start | bytes 331780
  0.7 14.5 %collective-permute-start.4 = (bf16[512,1536]{1,0:T(8,128)(2,1)}, bf16[512,1536]{1,0:T(8,128)(2,1)S(1)}, u32[]{:S(2)}, u32[]{:S(2)}) collective-permute-start(bf16[512,1536]{1,0:T(8,128)(2,1)} %refs_8_.1), channel_id=1, source_target_pairs={{0,1},{1,0},{2,3},{3,2},{4,5},{5,4},{6,7},{7,6},{8,9},{9,8},{10,11... | collective-permute-start | bytes 4718600 | tf_op jit(solution)/shard_map/ppermute | solution.py:641
  1.2 7.6 %collective-permute-start.2 = (bf16[128,3072]{1,0:T(8,128)(2,1)}, bf16[128,3072]{1,0:T(8,128)(2,1)}, u32[]{:S(2)}, u32[]{:S(2)}) collective-permute-start(bf16[128,3072]{1,0:T(8,128)(2,1)} %rest_0_.1), channel_id=1, source_target_pairs={{0,1},{1,0},{2,3},{3,2},{4,5},{5,4},{6,7},{7,6},{8,9},{9,8},{10,11... | collective-permute-start | bytes 2359304 | tf_op jit(solution)/shard_map/ppermute | solution.py:641
  1.3 7.5 %collective-permute-start.3 = (bf16[256,1024]{1,0:T(8,128)(2,1)}, bf16[256,1024]{1,0:T(8,128)(2,1)}, u32[]{:S(2)}, u32[]{:S(2)}) collective-permute-start(bf16[256,1024]{1,0:T(8,128)(2,1)} %refs_6_.1), channel_id=1, source_target_pairs={{0,1},{1,0},{2,3},{3,2},{4,5},{5,4},{6,7},{7,6},{8,9},{9,8},{10,11... | collective-permute-start | bytes 1572872 | tf_op jit(solution)/shard_map/ppermute | solution.py:641
  1.7 13.0 %collective-permute-start.1 = (bf16[128,1024]{1,0:T(8,128)(2,1)}, bf16[128,1024]{1,0:T(8,128)(2,1)}, u32[]{:S(2)}, u32[]{:S(2)}) collective-permute-start(bf16[128,1024]{1,0:T(8,128)(2,1)} %bitcast.16), channel_id=1, source_target_pairs={{4,8},{8,4},{5,9},{9,5},{6,10},{10,6},{7,11},{11,7},{20,24},{24,20... | collective-permute-start | bytes 786440 | tf_op jit(solution)/shard_map/ppermute | solution.py:657
  3.1 12.1 %collective-permute-start = (bf16[128,1024]{1,0:T(8,128)(2,1)}, bf16[128,1024]{1,0:T(8,128)(2,1)}, u32[]{:S(2)}, u32[]{:S(2)}) collective-permute-start(bf16[128,1024]{1,0:T(8,128)(2,1)} %bitcast.17), channel_id=1, source_target_pairs={{0,4},{4,0},{8,12},{12,8},{1,5},{5,1},{9,13},{13,9},{2,6},{6,2},{1... | collective-permute-start | bytes 786440 | tf_op jit(solution)/shard_map/ppermute | solution.py:641
  11.6 6.8 %collective-permute-start.5 = (bf16[128,128]{1,0:T(8,128)(2,1)S(1)}, bf16[128,128]{1,0:T(8,128)(2,1)S(1)}, u32[]{:S(2)}, u32[]{:S(2)}) collective-permute-start(bf16[128,128]{1,0:T(8,128)(2,1)S(1)} %get-tuple-element.48), channel_id=1, source_target_pairs={{0,8},{4,12},{8,0},{12,4},{1,9},{5,13},{9,1},{13,5},{2,10},{6,14},... | collective-permute-start | bytes 98312 | tf_op jit(solution)/shard_map/ppermute | solution.py:641
  13.3 5.7 %collective-permute-start.6 = (bf16[128,128]{1,0:T(8,128)(2,1)S(1)}, bf16[128,128]{1,0:T(8,128)(2,1)S(1)}, u32[]{:S(2)}, u32[]{:S(2)}) collective-permute-start(bf16[128,128]{1,0:T(8,128)(2,1)S(1)} %get-tuple-element.49), channel_id=1, source_target_pairs={{0,12},{4,8},{8,4},{12,0},{1,13},{5,9},{9,5},{13,1},{2,14},{6,10},... | collective-permute-start | bytes 98312 | tf_op jit(solution)/shard_map/ppermute | solution.py:641
  14.7 4.4 %collective-permute-start.7 = (bf16[128,128]{1,0:T(8,128)(2,1)S(1)}, bf16[128,128]{1,0:T(8,128)(2,1)S(1)}, u32[]{:S(2)}, u32[]{:S(2)}) collective-permute-start(bf16[128,128]{1,0:T(8,128)(2,1)S(1)} %get-tuple-element.50), channel_id=1, source_target_pairs={{0,4},{4,0},{8,12},{12,8},{1,5},{5,1},{9,13},{13,9},{2,6},{6,2},{1... | collective-permute-start | bytes 98312 | tf_op jit(solution)/shard_map/ppermute | solution.py:641
  18.4 24.1 %copy-start.3 = (bf16[1,1,8,16,1024]{4,3,2,1,0:T(8,128)(2,1)S(1)}, bf16[1,1,8,16,1024]{4,3,2,1,0:T(8,128)(2,1)}, u32[]{:S(2)}) copy-start(bf16[1,1,8,16,1024]{4,3,2,1,0:T(8,128)(2,1)} %param.15) | copy-start | bytes 786436
  19.0 9.8 %collective-permute-start.8 = (bf16[128,384]{1,0:T(8,128)(2,1)S(1)}, bf16[128,384]{1,0:T(8,128)(2,1)S(1)}, u32[]{:S(2)}, u32[]{:S(2)}) collective-permute-start(bf16[128,384]{1,0:T(8,128)(2,1)S(1)} %get-tuple-element.52), channel_id=1, source_target_pairs={{0,8},{4,12},{8,0},{12,4},{1,9},{5,13},{9,1},{13,5},{2,10},{6,14},... | collective-permute-start | bytes 294920 | tf_op jit(solution)/shard_map/ppermute | solution.py:641
  21.0 7.7 %collective-permute-start.9 = (bf16[128,384]{1,0:T(8,128)(2,1)S(1)}, bf16[128,384]{1,0:T(8,128)(2,1)S(1)}, u32[]{:S(2)}, u32[]{:S(2)}) collective-permute-start(bf16[128,384]{1,0:T(8,128)(2,1)S(1)} %get-tuple-element.53), channel_id=1, source_target_pairs={{0,12},{4,8},{8,4},{12,0},{1,13},{5,9},{9,5},{13,1},{2,14},{6,10},... | collective-permute-start | bytes 294920 | tf_op jit(solution)/shard_map/ppermute | solution.py:641
  22.6 6.6 %collective-permute-start.10 = (bf16[128,384]{1,0:T(8,128)(2,1)S(1)}, bf16[128,384]{1,0:T(8,128)(2,1)S(1)}, u32[]{:S(2)}, u32[]{:S(2)}) collective-permute-start(bf16[128,384]{1,0:T(8,128)(2,1)S(1)} %get-tuple-element.54), channel_id=1, source_target_pairs={{0,4},{4,0},{8,12},{12,8},{1,5},{5,1},{9,13},{13,9},{2,6},{6,2},{1... | collective-permute-start | bytes 294920 | tf_op jit(solution)/shard_map/ppermute | solution.py:641
  31.3 10.6 %collective-permute-start.11 = (bf16[128,384]{1,0:T(8,128)(2,1)S(1)}, bf16[128,384]{1,0:T(8,128)(2,1)S(1)}, u32[]{:S(2)}, u32[]{:S(2)}) collective-permute-start(bf16[128,384]{1,0:T(8,128)(2,1)S(1)} %get-tuple-element.60), channel_id=1, source_target_pairs={{0,8},{4,12},{8,0},{12,4},{1,9},{5,13},{9,1},{13,5},{2,10},{6,14},... | collective-permute-start | bytes 294920 | tf_op jit(solution)/shard_map/ppermute | solution.py:641
  33.7 8.2 %collective-permute-start.12 = (bf16[128,384]{1,0:T(8,128)(2,1)S(1)}, bf16[128,384]{1,0:T(8,128)(2,1)S(1)}, u32[]{:S(2)}, u32[]{:S(2)}) collective-permute-start(bf16[128,384]{1,0:T(8,128)(2,1)S(1)} %get-tuple-element.61), channel_id=1, source_target_pairs={{0,12},{4,8},{8,4},{12,0},{1,13},{5,9},{9,5},{13,1},{2,14},{6,10},... | collective-permute-start | bytes 294920 | tf_op jit(solution)/shard_map/ppermute | solution.py:641
  34.9 7.6 %collective-permute-start.13 = (bf16[128,384]{1,0:T(8,128)(2,1)S(1)}, bf16[128,384]{1,0:T(8,128)(2,1)S(1)}, u32[]{:S(2)}, u32[]{:S(2)}) collective-permute-start(bf16[128,384]{1,0:T(8,128)(2,1)S(1)} %get-tuple-element.62), channel_id=1, source_target_pairs={{0,4},{4,0},{8,12},{12,8},{1,5},{5,1},{9,13},{13,9},{2,6},{6,2},{1... | collective-permute-start | bytes 294920 | tf_op jit(solution)/shard_map/ppermute | solution.py:641
  34.9 11.1 %collective-permute-start.15 = (bf16[128,128]{1,0:T(8,128)(2,1)S(1)}, bf16[128,128]{1,0:T(8,128)(2,1)S(1)}, u32[]{:S(2)}, u32[]{:S(2)}) collective-permute-start(bf16[128,128]{1,0:T(8,128)(2,1)S(1)} %get-tuple-element.68), channel_id=1, source_target_pairs={{0,8},{4,12},{8,0},{12,4},{1,9},{5,13},{9,1},{13,5},{2,10},{6,14},... | collective-permute-start | bytes 98312 | tf_op jit(solution)/shard_map/ppermute | solution.py:641
  38.1 8.0 %collective-permute-start.16 = (bf16[128,128]{1,0:T(8,128)(2,1)S(1)}, bf16[128,128]{1,0:T(8,128)(2,1)S(1)}, u32[]{:S(2)}, u32[]{:S(2)}) collective-permute-start(bf16[128,128]{1,0:T(8,128)(2,1)S(1)} %get-tuple-element.69), channel_id=1, source_target_pairs={{0,12},{4,8},{8,4},{12,0},{1,13},{5,9},{9,5},{13,1},{2,14},{6,10},... | collective-permute-start | bytes 98312 | tf_op jit(solution)/shard_map/ppermute | solution.py:641
  41.8 4.2 %collective-permute-start.17 = (bf16[128,128]{1,0:T(8,128)(2,1)S(1)}, bf16[128,128]{1,0:T(8,128)(2,1)S(1)}, u32[]{:S(2)}, u32[]{:S(2)}) collective-permute-start(bf16[128,128]{1,0:T(8,128)(2,1)S(1)} %get-tuple-element.70), channel_id=1, source_target_pairs={{0,4},{4,0},{8,12},{12,8},{1,5},{5,1},{9,13},{13,9},{2,6},{6,2},{1... | collective-permute-start | bytes 98312 | tf_op jit(solution)/shard_map/ppermute | solution.py:641
  42.5 10.6 %copy-start.1 = (bf16[256,1024]{1,0:T(8,128)(2,1)S(1)}, bf16[256,1024]{1,0:T(8,128)(2,1)}, u32[]{:S(2)}) copy-start(bf16[256,1024]{1,0:T(8,128)(2,1)} %refs_6_.1) | copy-start | bytes 1572868
  46.1 14.1 %collective-permute-start.22 = (bf16[128,1024]{1,0:T(8,128)(2,1)S(1)}, bf16[128,1024]{1,0:T(8,128)(2,1)S(1)}, u32[]{:S(2)}, u32[]{:S(2)}) collective-permute-start(bf16[128,1024]{1,0:T(8,128)(2,1)S(1)} %get-tuple-element.78.grad), channel_id=1, source_target_pairs={{4,8},{8,4},{5,9},{9,5},{6,10},{10,6},{7,11},{11,7},{20,24},{24,20... | collective-permute-start | bytes 786440 | tf_op jit(solution)/shard_map/ppermute | solution.py:657
  46.9 13.3 %collective-permute-start.21 = (bf16[128,1024]{1,0:T(8,128)(2,1)S(1)}, bf16[128,1024]{1,0:T(8,128)(2,1)S(1)}, u32[]{:S(2)}, u32[]{:S(2)}) collective-permute-start(bf16[128,1024]{1,0:T(8,128)(2,1)S(1)} %get-tuple-element.78.grad), channel_id=1, source_target_pairs={{0,4},{4,0},{8,12},{12,8},{1,5},{5,1},{9,13},{13,9},{2,6},{6,2},{1... | collective-permute-start | bytes 786440 | tf_op jit(solution)/shard_map/ppermute | solution.py:641
  51.3 4.1 %collective-permute-start.14 = (bf16[216,128]{1,0:T(8,128)(2,1)S(1)}, bf16[216,128]{1,0:T(8,128)(2,1)S(1)}, u32[]{:S(2)}, u32[]{:S(2)}) collective-permute-start(bf16[216,128]{1,0:T(8,128)(2,1)S(1)} %get-tuple-element.65.refs_0_), channel_id=1, source_target_pairs={{0,3},{1,2},{2,1},{3,0},{4,7},{5,6},{6,5},{7,4},{8,11},{9,10},{10,... | collective-permute-start | bytes 165896 | tf_op jit(solution)/shard_map/ppermute | solution.py:766
  51.3 5.3 %collective-permute-start.19 = (bf16[216,128]{1,0:T(8,128)(2,1)S(1)}, bf16[216,128]{1,0:T(8,128)(2,1)S(1)}, u32[]{:S(2)}, u32[]{:S(2)}) collective-permute-start(bf16[216,128]{1,0:T(8,128)(2,1)S(1)} %get-tuple-element.65.refs_0_), channel_id=1, source_target_pairs={{0,2},{1,3},{2,0},{3,1},{4,6},{5,7},{6,4},{7,5},{8,10},{9,11},{10,... | collective-permute-start | bytes 165896 | tf_op jit(solution)/shard_map/ppermute | solution.py:766
  52.8 3.8 %collective-permute-start.18 = (bf16[216,128]{1,0:T(8,128)(2,1)S(1)}, bf16[216,128]{1,0:T(8,128)(2,1)S(1)}, u32[]{:S(2)}, u32[]{:S(2)}) collective-permute-start(bf16[216,128]{1,0:T(8,128)(2,1)S(1)} %get-tuple-element.65.refs_0_), channel_id=1, source_target_pairs={{0,1},{1,0},{2,3},{3,2},{4,5},{5,4},{6,7},{7,6},{8,9},{9,8},{10,11... | collective-permute-start | bytes 165896 | tf_op jit(solution)/shard_map/ppermute | solution.py:766
  56.6 5.9 %collective-permute-start.20 = (bf16[216,128]{1,0:T(8,128)(2,1)S(1)}, bf16[216,128]{1,0:T(8,128)(2,1)S(1)}, u32[]{:S(2)}, u32[]{:S(2)}) collective-permute-start(bf16[216,128]{1,0:T(8,128)(2,1)S(1)} %add_dp.1.refs_0_), channel_id=1, source_target_pairs={{0,4},{4,0},{8,12},{12,8},{1,5},{5,1},{9,13},{13,9},{2,6},{6,2},{1... | collective-permute-start | bytes 165896 | tf_op jit(solution)/shard_map/ppermute | solution.py:641
  56.8 6.2 %collective-permute-start.24 = (bf16[216,128]{1,0:T(8,128)(2,1)S(1)}, bf16[216,128]{1,0:T(8,128)(2,1)S(1)}, u32[]{:S(2)}, u32[]{:S(2)}) collective-permute-start(bf16[216,128]{1,0:T(8,128)(2,1)S(1)} %add_dp.1.refs_0_), channel_id=1, source_target_pairs={{0,12},{4,8},{8,4},{12,0},{1,13},{5,9},{9,5},{13,1},{2,14},{6,10},... | collective-permute-start | bytes 165896 | tf_op jit(solution)/shard_map/ppermute | solution.py:641
  58.9 6.5 %collective-permute-start.23 = (bf16[216,128]{1,0:T(8,128)(2,1)S(1)}, bf16[216,128]{1,0:T(8,128)(2,1)S(1)}, u32[]{:S(2)}, u32[]{:S(2)}) collective-permute-start(bf16[216,128]{1,0:T(8,128)(2,1)S(1)} %add_dp.1.refs_0_), channel_id=1, source_target_pairs={{0,8},{4,12},{8,0},{12,4},{1,9},{5,13},{9,1},{13,5},{2,10},{6,14},... | collective-permute-start | bytes 165896 | tf_op jit(solution)/shard_map/ppermute | solution.py:641

commit v5 on v4

--- a/solution.py
+++ b/solution.py
@@ -603,10 +603,13 @@
     out[...] = tree_sum([as_f32(ref[...]) for ref in refs[:-1]]).astype(out.dtype)
 
 
-def final_body(factor, slots, *refs):
+def seq_sum_body(slots, *refs):
     gaps = distances(slots)
-    out = refs[slots]
-    total = tree_sum([as_f32(refs[gaps.index(gap)][...]) for gap in range(slots)]) * factor
+    refs[slots][...] = tree_sum([refs[gaps.index(gap)][...].astype(jnp.float32) for gap in range(slots)])
+
+
+def final_body(factor, left, right, out):
+    total = (left[...] + right[...]) * factor
     lanes = total.shape[1]
     for block in range(out.shape[1] // lanes):
         out[:, block * lanes : (block + 1) * lanes] = total[27 * block : 27 * (block + 1)]
@@ -762,12 +765,9 @@
         scalars=True,
     )
     grad_near, grad_far = neighbours(dresid)
-    pair = ("dp", "fsdp")
-    others = [lax.ppermute(terms, pair, [(i, i ^ gap) for i in range(4)]) for gap in (1, 2, 3)]
-    others[-1], out = lax.optimization_barrier((others[-1], out))
-    (terms,) = call(
-        sum_body, "add_dp", [shape((27 * width // 128, 128), bf16)], (terms, *others)
-    )
+    other = swapped(terms, "dp", 1)
+    other, out = lax.optimization_barrier((other, out))
+    (terms,) = call(sum_body, "add_dp", [shape(terms.shape, bf16)], (terms, other))
     (token_grad,) = call(
         functools.partial(back_conv_body, inner),
         "back_conv",
@@ -778,8 +778,14 @@
     factor = 1.0 / math.sqrt(lax.axis_size("dp") * lax.axis_size("fsdp") * slots * rows)
     pieces = exchanged([terms] * slots)
     pieces[-1], token_grad = lax.optimization_barrier((pieces[-1], token_grad))
+    (summed,) = call(
+        functools.partial(seq_sum_body, slots), "add_seq", [shape(terms.shape, f32)], pieces
+    )
     (kernel_grad,) = call(
-        functools.partial(final_body, factor, slots), "add_seq", [shape((27, width), f32)], pieces
+        functools.partial(final_body, factor),
+        "final",
+        [shape((27, width), f32)],
+        (summed, swapped(summed, "fsdp", 1)),
     )
     return out.reshape(tokens.shape), token_grad.reshape(tokens.shape), kernel_grad
 

time: 66.3 us -> 65.5 us (0.988)
    ppermute x3 -> x0, starting transfers between devices: 1.86 us -> none  [slab_shards(): lax.ppermute(terms, pair, [(i, i ^ gap) for i in range(4)])]
    ppermute x3 -> x0, waiting for transfers between devices: 1.78 us -> none  [slab_shards(): lax.ppermute(terms, pair, [(i, i ^ gap) for i in range(4)])]
    ppermute x20 -> x22, starting transfers between devices: 29 us -> 30.5 us  [swapped(): return lax.ppermute(value, axis, [(i, i ^ distance) for i in range(count)])]
    ppermute x20 -> x22, waiting for transfers between devices: 13.3 us -> 14.8 us  [swapped(): return lax.ppermute(value, axis, [(i, i ^ distance) for i in range(count)])]
    pallas_call x8 -> x9, Pallas kernels: 16.3 us -> 16.3 us  [call(): pl.pallas_call(body, out_shape=tuple(outs), in_specs=specs, out_specs=(wh...]
  transfers between devices with their start and end apart: 25 -> 24, of which waited for: 9 -> 9; matrix products, arithmetic and copies ran while one was open for 0% -> 0% of each run, Pallas kernels for 20% -> 21%
where the time goes in v5:
time: 65.5 us; the launch traced here: 65.3 us
  starting transfers between devices  32.6 us (50%)
  Pallas kernels  16.3 us (25%)
  waiting for transfers between devices  14.8 us (23%)
  between operations  1.47 us (2%)
    ppermute x22, starting transfers between devices, swapped(): return lax.ppermute(value, axis, [(i, i ^ distance) for i in range(count)])  30.5 us
    pallas_call x9, Pallas kernels, call(): pl.pallas_call(body, out_shape=tuple(outs), in_specs=specs, out_specs=(wh...  16.3 us
    ppermute x22, waiting for transfers between devices, swapped(): return lax.ppermute(value, axis, [(i, i ^ distance) for i in range(count)])  14.8 us
    ppermute x2, starting transfers between devices, neighbours(): lax.ppermute(value, 'seq', middle + [(j, i) for i, j in middle])  2.07 us
  transfers between devices with their start and end apart: 24, of which 9 were waited for; matrix products, arithmetic and copies ran while one was open for 0% of the time, Pallas kernels for 21%

profile of v5, /device:TPU:0, one launch (start us, length us, event | category | flops | bytes accessed | tf_op | source)
XLA Modules:
  0.0 65.3 jit_solution(17151372419027321223)
XLA Ops:
  0.7 0.5 collective-permute-start.4
  1.3 0.4 collective-permute-start.3
  1.7 1.4 %collective-permute-start.1 = (bf16[128,1024]{1,0:T(8,128)(2,1)}, bf16[128,1024]{1,0:T(8,128)(2,1)}, u32[]{:S(2)}, u32[]{:S(2)}) collective-permute-start(bf16[128,1024]{1,0:T(8,128)(2,1)} %bitcast.16), channel_id=1, source_target_pairs={{4,8},{8,4},{5,9},{9,5},{6,10},{10,6},{7,11},{11,7},{20,24},{24,20... | collective-permute-start | bytes 786440 | tf_op jit(solution)/shard_map/ppermute | solution.py:660
  3.1 4.8 %collective-permute-start = (bf16[128,1024]{1,0:T(8,128)(2,1)}, bf16[128,1024]{1,0:T(8,128)(2,1)}, u32[]{:S(2)}, u32[]{:S(2)}) collective-permute-start(bf16[128,1024]{1,0:T(8,128)(2,1)} %bitcast.17), channel_id=1, source_target_pairs={{0,4},{4,0},{8,12},{12,8},{1,5},{5,1},{9,13},{13,9},{2,6},{6,2},{1... | collective-permute-start | bytes 786440 | tf_op jit(solution)/shard_map/ppermute | solution.py:644
  8.8 2.8 %front.1 = (f32[3,1024]{1,0:T(4,128)S(1)}, bf16[256,1024]{1,0:T(8,128)(2,1)S(1)}, bf16[128,128]{1,0:T(8,128)(2,1)S(1)}, bf16[128,128]{1,0:T(8,128)(2,1)S(1)}, bf...) custom-call(s32[2]{0:T(128)S(1)} %pad_add_fusion.ids, bf16[2,8,128]{2,1,0:T(8,128)(2,1)S(1)} %broadcast_in_dim.10.feats, ...), custom_call_target="tpu_custom_call" | custom-call | flops 134217728 | bytes 3567624 | tf_op jit(solution)/shard_map/front/pallas_call | solution.py:630
  11.6 1.7 %collective-permute-start.5 = (bf16[128,128]{1,0:T(8,128)(2,1)S(1)}, bf16[128,128]{1,0:T(8,128)(2,1)S(1)}, u32[]{:S(2)}, u32[]{:S(2)}) collective-permute-start(bf16[128,128]{1,0:T(8,128)(2,1)S(1)} %get-tuple-element.48), channel_id=1, source_target_pairs={{0,8},{4,12},{8,0},{12,4},{1,9},{5,13},{9,1},{13,5},{2,10},{6,14},... | collective-permute-start | bytes 98312 | tf_op jit(solution)/shard_map/ppermute | solution.py:644
  13.3 1.3 %collective-permute-start.6 = (bf16[128,128]{1,0:T(8,128)(2,1)S(1)}, bf16[128,128]{1,0:T(8,128)(2,1)S(1)}, u32[]{:S(2)}, u32[]{:S(2)}) collective-permute-start(bf16[128,128]{1,0:T(8,128)(2,1)S(1)} %get-tuple-element.49), channel_id=1, source_target_pairs={{0,12},{4,8},{8,4},{12,0},{1,13},{5,9},{9,5},{13,1},{2,14},{6,10},... | collective-permute-start | bytes 98312 | tf_op jit(solution)/shard_map/ppermute | solution.py:644
  14.7 0.5 collective-permute-start.7
  15.2 3.2 %mix.1 = (bf16[128,1024]{1,0:T(8,128)(2,1)S(1)}, f32[128,1024]{1,0:T(8,128)S(1)}, bf16[128,384]{1,0:T(8,128)(2,1)S(1)}, bf16[128,384]{1,0:T(8,128)(2,1)S(1)}, bf...) custom-call(s32[2]{0:T(128)S(1)} %pad_add_fusion.ids, bf16[128,1024]{1,0:T(8,128)(2,1)S(1)} %bitcast.18, ...), custom_call_target="tpu_custom_call" | custom-call | flops 402653184 | bytes 5234696 | tf_op jit(solution)/shard_map/mix/pallas_call | solution.py:630
  18.4 0.6 collective-permute-done.6.refs_6_
  19.0 2.0 %collective-permute-start.8 = (bf16[128,384]{1,0:T(8,128)(2,1)S(1)}, bf16[128,384]{1,0:T(8,128)(2,1)S(1)}, u32[]{:S(2)}, u32[]{:S(2)}) collective-permute-start(bf16[128,384]{1,0:T(8,128)(2,1)S(1)} %get-tuple-element.52), channel_id=1, source_target_pairs={{0,8},{4,12},{8,0},{12,4},{1,9},{5,13},{9,1},{13,5},{2,10},{6,14},... | collective-permute-start | bytes 294920 | tf_op jit(solution)/shard_map/ppermute | solution.py:644
  21.0 1.6 %collective-permute-start.9 = (bf16[128,384]{1,0:T(8,128)(2,1)S(1)}, bf16[128,384]{1,0:T(8,128)(2,1)S(1)}, u32[]{:S(2)}, u32[]{:S(2)}) collective-permute-start(bf16[128,384]{1,0:T(8,128)(2,1)S(1)} %get-tuple-element.53), channel_id=1, source_target_pairs={{0,12},{4,8},{8,4},{12,0},{1,13},{5,9},{9,5},{13,1},{2,14},{6,10},... | collective-permute-start | bytes 294920 | tf_op jit(solution)/shard_map/ppermute | solution.py:644
  22.6 6.2 %collective-permute-done.8.refs_1_ = bf16[128,384]{1,0:T(8,128)(2,1)S(1)} collective-permute-done((bf16[128,384]{1,0:T(8,128)(2,1)S(1)}, bf16[128,384]{1,0:T(8,128)(2,1)S(1)}, u32[]{:S(2)}, u32[]{:S(2)}) %collective-permute-start.8) | collective-permute-done | bytes 98336 | tf_op jit(solution)/shard_map/ppermute | solution.py:644
  29.2 2.1 %attend.1 = (bf16[128,384]{1,0:T(8,128)(2,1)S(1)}, bf16[128,384]{1,0:T(8,128)(2,1)S(1)}, bf16[128,384]{1,0:T(8,128)(2,1)S(1)}, bf16[128,384]{1,0:T(8,128)(2,1)S(...) custom-call(bf16[128,384]{1,0:T(8,128)(2,1)S(1)} %get-tuple-element., ...), custom_call_target="tpu_custom_call" | custom-call | flops 402653184 | bytes 1048576 | tf_op jit(solution)/shard_map/attend/pallas_call | solution.py:630
  31.3 2.4 %collective-permute-start.11 = (bf16[128,384]{1,0:T(8,128)(2,1)S(1)}, bf16[128,384]{1,0:T(8,128)(2,1)S(1)}, u32[]{:S(2)}, u32[]{:S(2)}) collective-permute-start(bf16[128,384]{1,0:T(8,128)(2,1)S(1)} %get-tuple-element.60), channel_id=1, source_target_pairs={{0,8},{4,12},{8,0},{12,4},{1,9},{5,13},{9,1},{13,5},{2,10},{6,14},... | collective-permute-start | bytes 294920 | tf_op jit(solution)/shard_map/ppermute | solution.py:644
  33.7 1.2 %collective-permute-start.12 = (bf16[128,384]{1,0:T(8,128)(2,1)S(1)}, bf16[128,384]{1,0:T(8,128)(2,1)S(1)}, u32[]{:S(2)}, u32[]{:S(2)}) collective-permute-start(bf16[128,384]{1,0:T(8,128)(2,1)S(1)} %get-tuple-element.61), channel_id=1, source_target_pairs={{0,12},{4,8},{8,4},{12,0},{1,13},{5,9},{9,5},{13,1},{2,14},{6,10},... | collective-permute-start | bytes 294920 | tf_op jit(solution)/shard_map/ppermute | solution.py:644
  34.9 3.1 %collective-permute-start.15 = (bf16[128,128]{1,0:T(8,128)(2,1)S(1)}, bf16[128,128]{1,0:T(8,128)(2,1)S(1)}, u32[]{:S(2)}, u32[]{:S(2)}) collective-permute-start(bf16[128,128]{1,0:T(8,128)(2,1)S(1)} %get-tuple-element.68), channel_id=1, source_target_pairs={{0,8},{4,12},{8,0},{12,4},{1,9},{5,13},{9,1},{13,5},{2,10},{6,14},... | collective-permute-start | bytes 98312 | tf_op jit(solution)/shard_map/ppermute | solution.py:644
  38.1 1.2 %collective-permute-start.16 = (bf16[128,128]{1,0:T(8,128)(2,1)S(1)}, bf16[128,128]{1,0:T(8,128)(2,1)S(1)}, u32[]{:S(2)}, u32[]{:S(2)}) collective-permute-start(bf16[128,128]{1,0:T(8,128)(2,1)S(1)} %get-tuple-element.69), channel_id=1, source_target_pairs={{0,12},{4,8},{8,4},{12,0},{1,13},{5,9},{9,5},{13,1},{2,14},{6,10},... | collective-permute-start | bytes 98312 | tf_op jit(solution)/shard_map/ppermute | solution.py:644
  39.3 2.5 %collective-permute-done.11.refs_1_ = bf16[128,384]{1,0:T(8,128)(2,1)S(1)} collective-permute-done((bf16[128,384]{1,0:T(8,128)(2,1)S(1)}, bf16[128,384]{1,0:T(8,128)(2,1)S(1)}, u32[]{:S(2)}, u32[]{:S(2)}) %collective-permute-start.11) | collective-permute-done | bytes 98336 | tf_op jit(solution)/shard_map/ppermute | solution.py:644
  41.8 0.7 %collective-permute-done.13.refs_3_ = bf16[128,384]{1,0:T(8,128)(2,1)S(1)} collective-permute-done((bf16[128,384]{1,0:T(8,128)(2,1)S(1)}, bf16[128,384]{1,0:T(8,128)(2,1)S(1)}, u32[]{:S(2)}, u32[]{:S(2)}) %collective-permute-start.13) | collective-permute-done | bytes 98336 | tf_op jit(solution)/shard_map/ppermute | solution.py:644
  42.5 3.5 %tail.1 = (bf16[128,1024]{1,0:T(8,128)(2,1)S(1)}, bf16[216,128]{1,0:T(8,128)(2,1)S(1)}) custom-call(s32[2]{0:T(128)S(1)} %pad_add_fusion.ids, bf16[128,384]{1,0:T(8,128)(2,1)S(1)} %get-tuple-element.59.refs_0_, bf16[128,384]{1,0:T(8,128)(2,1)S(1)} %collective-permute-done.11.refs_1_, bf16[128,384]{1,0:T(8,128)(2,1)S(1)} %collective-permute-done.12.refs_2_, ...), custom_call_target="tpu_custom_call" | custom-call | flops 402653184 | bytes 5703688 | tf_op jit(solution)/shard_map/tail/pallas_call | solution.py:630
  46.1 0.7 %collective-permute-start.20 = (bf16[128,1024]{1,0:T(8,128)(2,1)S(1)}, bf16[128,1024]{1,0:T(8,128)(2,1)S(1)}, u32[]{:S(2)}, u32[]{:S(2)}) collective-permute-start(bf16[128,1024]{1,0:T(8,128)(2,1)S(1)} %get-tuple-element.78.grad), channel_id=1, source_target_pairs={{4,8},{8,4},{5,9},{9,5},{6,10},{10,6},{7,11},{11,7},{20,24},{24,20... | collective-permute-start | bytes 786440 | tf_op jit(solution)/shard_map/ppermute | solution.py:660
  46.7 4.4 %collective-permute-start.19 = (bf16[128,1024]{1,0:T(8,128)(2,1)S(1)}, bf16[128,1024]{1,0:T(8,128)(2,1)S(1)}, u32[]{:S(2)}, u32[]{:S(2)}) collective-permute-start(bf16[128,1024]{1,0:T(8,128)(2,1)S(1)} %get-tuple-element.78.grad), channel_id=1, source_target_pairs={{0,4},{4,0},{8,12},{12,8},{1,5},{5,1},{9,13},{13,9},{2,6},{6,2},{1... | collective-permute-start | bytes 786440 | tf_op jit(solution)/shard_map/ppermute | solution.py:644
  51.1 1.5 %collective-permute-start.14 = (bf16[216,128]{1,0:T(8,128)(2,1)S(1)}, bf16[216,128]{1,0:T(8,128)(2,1)S(1)}, u32[]{:S(2)}, u32[]{:S(2)}) collective-permute-start(bf16[216,128]{1,0:T(8,128)(2,1)S(1)} %get-tuple-element.65.refs_0_), channel_id=1, source_target_pairs={{0,2},{2,0},{1,3},{3,1},{4,6},{6,4},{5,7},{7,5},{8,10},{10,8},{9,1... | collective-permute-start | bytes 165896 | tf_op jit(solution)/shard_map/ppermute | solution.py:644
  52.6 1.7 %out.1 = bf16[128,1024]{1,0:T(8,128)(2,1)} custom-call(s32[2]{0:T(128)S(1)} %pad_add_fusion.ids, bf16[128,128]{1,0:T(8,128)(2,1)S(1)} %get-tuple-element.71.refs_0_, bf16[128,128]{1,0:T(8,128)(2,1)S(1)} %collective-permute-done.15.refs_1_, bf16[128,128]{1,0:T(8,128)(2,1)S(1)} %collective-permute-done.16.refs_2_, ...), custom_call_target="tpu_custom_call" | custom-call | flops 134217728 | bytes 1716232 | tf_op jit(solution)/shard_map/out/pallas_call | solution.py:630
  54.3 1.0 %collective-permute-done.14.refs_1_ = bf16[216,128]{1,0:T(8,128)(2,1)S(1)} collective-permute-done((bf16[216,128]{1,0:T(8,128)(2,1)S(1)}, bf16[216,128]{1,0:T(8,128)(2,1)S(1)}, u32[]{:S(2)}, u32[]{:S(2)}) %collective-permute-start.14) | collective-permute-done | bytes 55328 | tf_op jit(solution)/shard_map/ppermute | solution.py:644
  55.4 2.2 %collective-permute-start.22 = (bf16[216,128]{1,0:T(8,128)(2,1)S(1)}, bf16[216,128]{1,0:T(8,128)(2,1)S(1)}, u32[]{:S(2)}, u32[]{:S(2)}) collective-permute-start(bf16[216,128]{1,0:T(8,128)(2,1)S(1)} %add_dp.1.refs_0_), channel_id=1, source_target_pairs={{0,12},{4,8},{8,4},{12,0},{1,13},{5,9},{9,5},{13,1},{2,14},{6,10},... | collective-permute-start | bytes 165896 | tf_op jit(solution)/shard_map/ppermute | solution.py:644
  57.6 1.3 %collective-permute-start.21 = (bf16[216,128]{1,0:T(8,128)(2,1)S(1)}, bf16[216,128]{1,0:T(8,128)(2,1)S(1)}, u32[]{:S(2)}, u32[]{:S(2)}) collective-permute-start(bf16[216,128]{1,0:T(8,128)(2,1)S(1)} %add_dp.1.refs_0_), channel_id=1, source_target_pairs={{0,8},{4,12},{8,0},{12,4},{1,9},{5,13},{9,1},{13,5},{2,10},{6,14},... | collective-permute-start | bytes 165896 | tf_op jit(solution)/shard_map/ppermute | solution.py:644
  58.8 2.3 %back_conv.1 = bf16[128,1024]{1,0:T(8,128)(2,1)} custom-call(s32[2]{0:T(128)S(1)} %pad_add_fusion.ids, bf16[128,1024]{1,0:T(8,128)(2,1)S(1)} %get-tuple-element.78.grad, bf16[128,1024]{1,0:T(8,128)(2,1)S(1)} %collective-permute-done.19.near, bf16[128,1024]{1,0:T(8,128)(2,1)S(1)} %collective-permute-done.20.far, f32[27,1024]{1,0:T(8,128)S(1)} %copy-done.4), custom_call_target="tpu_custom_call" | custom-call | bytes 1159176 | tf_op jit(solution)/shard_map/back_conv/pallas_call | solution.py:630
  61.5 1.7 %collective-permute-done.21.refs_1_ = bf16[216,128]{1,0:T(8,128)(2,1)S(1)} collective-permute-done((bf16[216,128]{1,0:T(8,128)(2,1)S(1)}, bf16[216,128]{1,0:T(8,128)(2,1)S(1)}, u32[]{:S(2)}, u32[]{:S(2)}) %collective-permute-start.21) | collective-permute-done | bytes 55328 | tf_op jit(solution)/shard_map/ppermute | solution.py:644
  63.3 1.3 %collective-permute-done.23.right = f32[216,128]{1,0:T(8,128)S(1)} collective-permute-done((f32[216,128]{1,0:T(8,128)S(1)}, f32[216,128]{1,0:T(8,128)S(1)}, u32[]{:S(2)}, u32[]{:S(2)}) %collective-permute-start.23) | collective-permute-done | bytes 110624 | tf_op jit(solution)/shard_map/ppermute | solution.py:644
  64.6 0.7 %final.1 = f32[27,1024]{1,0:T(8,128)} custom-call(f32[216,128]{1,0:T(8,128)S(1)} %add_seq.1.left, f32[216,128]{1,0:T(8,128)S(1)} %collective-permute-done.23.right), custom_call_target="tpu_custom_call" | custom-call | bytes 331776 | tf_op jit(solution)/shard_map/final/pallas_call | solution.py:630
  (42 shorter events, 1.3 us)
Async XLA Ops:
  0.6 14.6 %copy-start = (bf16[512,1536]{1,0:T(8,128)(2,1)S(1)}, bf16[512,1536]{1,0:T(8,128)(2,1)}, u32[]{:S(2)}) copy-start(bf16[512,1536]{1,0:T(8,128)(2,1)} %refs_8_.1) | copy-start | bytes 4718596
  0.6 14.6 %copy-start.2 = (bf16[1,1,8,16,1024]{4,3,2,1,0:T(8,128)(2,1)S(1)}, bf16[1,1,8,16,1024]{4,3,2,1,0:T(8,128)(2,1)}, u32[]{:S(2)}) copy-start(bf16[1,1,8,16,1024]{4,3,2,1,0:T(8,128)(2,1)} %param.8) | copy-start | bytes 786436
  0.7 14.6 %copy-start.4 = (f32[27,1024]{1,0:T(8,128)S(1)}, f32[27,1024]{1,0:T(8,128)}, u32[]{:S(2)}) copy-start(f32[27,1024]{1,0:T(8,128)} %taps.3) | copy-start | bytes 331780
  0.7 14.5 %collective-permute-start.4 = (bf16[512,1536]{1,0:T(8,128)(2,1)}, bf16[512,1536]{1,0:T(8,128)(2,1)S(1)}, u32[]{:S(2)}, u32[]{:S(2)}) collective-permute-start(bf16[512,1536]{1,0:T(8,128)(2,1)} %refs_8_.1), channel_id=1, source_target_pairs={{0,1},{1,0},{2,3},{3,2},{4,5},{5,4},{6,7},{7,6},{8,9},{9,8},{10,11... | collective-permute-start | bytes 4718600 | tf_op jit(solution)/shard_map/ppermute | solution.py:644
  1.2 7.6 %collective-permute-start.2 = (bf16[128,3072]{1,0:T(8,128)(2,1)}, bf16[128,3072]{1,0:T(8,128)(2,1)}, u32[]{:S(2)}, u32[]{:S(2)}) collective-permute-start(bf16[128,3072]{1,0:T(8,128)(2,1)} %rest_0_.1), channel_id=1, source_target_pairs={{0,1},{1,0},{2,3},{3,2},{4,5},{5,4},{6,7},{7,6},{8,9},{9,8},{10,11... | collective-permute-start | bytes 2359304 | tf_op jit(solution)/shard_map/ppermute | solution.py:644
  1.3 7.5 %collective-permute-start.3 = (bf16[256,1024]{1,0:T(8,128)(2,1)}, bf16[256,1024]{1,0:T(8,128)(2,1)}, u32[]{:S(2)}, u32[]{:S(2)}) collective-permute-start(bf16[256,1024]{1,0:T(8,128)(2,1)} %refs_6_.1), channel_id=1, source_target_pairs={{0,1},{1,0},{2,3},{3,2},{4,5},{5,4},{6,7},{7,6},{8,9},{9,8},{10,11... | collective-permute-start | bytes 1572872 | tf_op jit(solution)/shard_map/ppermute | solution.py:644
  1.7 13.0 %collective-permute-start.1 = (bf16[128,1024]{1,0:T(8,128)(2,1)}, bf16[128,1024]{1,0:T(8,128)(2,1)}, u32[]{:S(2)}, u32[]{:S(2)}) collective-permute-start(bf16[128,1024]{1,0:T(8,128)(2,1)} %bitcast.16), channel_id=1, source_target_pairs={{4,8},{8,4},{5,9},{9,5},{6,10},{10,6},{7,11},{11,7},{20,24},{24,20... | collective-permute-start | bytes 786440 | tf_op jit(solution)/shard_map/ppermute | solution.py:660
  3.1 12.1 %collective-permute-start = (bf16[128,1024]{1,0:T(8,128)(2,1)}, bf16[128,1024]{1,0:T(8,128)(2,1)}, u32[]{:S(2)}, u32[]{:S(2)}) collective-permute-start(bf16[128,1024]{1,0:T(8,128)(2,1)} %bitcast.17), channel_id=1, source_target_pairs={{0,4},{4,0},{8,12},{12,8},{1,5},{5,1},{9,13},{13,9},{2,6},{6,2},{1... | collective-permute-start | bytes 786440 | tf_op jit(solution)/shard_map/ppermute | solution.py:644
  11.6 6.8 %collective-permute-start.5 = (bf16[128,128]{1,0:T(8,128)(2,1)S(1)}, bf16[128,128]{1,0:T(8,128)(2,1)S(1)}, u32[]{:S(2)}, u32[]{:S(2)}) collective-permute-start(bf16[128,128]{1,0:T(8,128)(2,1)S(1)} %get-tuple-element.48), channel_id=1, source_target_pairs={{0,8},{4,12},{8,0},{12,4},{1,9},{5,13},{9,1},{13,5},{2,10},{6,14},... | collective-permute-start | bytes 98312 | tf_op jit(solution)/shard_map/ppermute | solution.py:644
  13.3 5.7 %collective-permute-start.6 = (bf16[128,128]{1,0:T(8,128)(2,1)S(1)}, bf16[128,128]{1,0:T(8,128)(2,1)S(1)}, u32[]{:S(2)}, u32[]{:S(2)}) collective-permute-start(bf16[128,128]{1,0:T(8,128)(2,1)S(1)} %get-tuple-element.49), channel_id=1, source_target_pairs={{0,12},{4,8},{8,4},{12,0},{1,13},{5,9},{9,5},{13,1},{2,14},{6,10},... | collective-permute-start | bytes 98312 | tf_op jit(solution)/shard_map/ppermute | solution.py:644
  14.7 4.4 %collective-permute-start.7 = (bf16[128,128]{1,0:T(8,128)(2,1)S(1)}, bf16[128,128]{1,0:T(8,128)(2,1)S(1)}, u32[]{:S(2)}, u32[]{:S(2)}) collective-permute-start(bf16[128,128]{1,0:T(8,128)(2,1)S(1)} %get-tuple-element.50), channel_id=1, source_target_pairs={{0,4},{4,0},{8,12},{12,8},{1,5},{5,1},{9,13},{13,9},{2,6},{6,2},{1... | collective-permute-start | bytes 98312 | tf_op jit(solution)/shard_map/ppermute | solution.py:644
  18.4 24.1 %copy-start.3 = (bf16[1,1,8,16,1024]{4,3,2,1,0:T(8,128)(2,1)S(1)}, bf16[1,1,8,16,1024]{4,3,2,1,0:T(8,128)(2,1)}, u32[]{:S(2)}) copy-start(bf16[1,1,8,16,1024]{4,3,2,1,0:T(8,128)(2,1)} %param.15) | copy-start | bytes 786436
  19.0 9.7 %collective-permute-start.8 = (bf16[128,384]{1,0:T(8,128)(2,1)S(1)}, bf16[128,384]{1,0:T(8,128)(2,1)S(1)}, u32[]{:S(2)}, u32[]{:S(2)}) collective-permute-start(bf16[128,384]{1,0:T(8,128)(2,1)S(1)} %get-tuple-element.52), channel_id=1, source_target_pairs={{0,8},{4,12},{8,0},{12,4},{1,9},{5,13},{9,1},{13,5},{2,10},{6,14},... | collective-permute-start | bytes 294920 | tf_op jit(solution)/shard_map/ppermute | solution.py:644
  21.0 7.7 %collective-permute-start.9 = (bf16[128,384]{1,0:T(8,128)(2,1)S(1)}, bf16[128,384]{1,0:T(8,128)(2,1)S(1)}, u32[]{:S(2)}, u32[]{:S(2)}) collective-permute-start(bf16[128,384]{1,0:T(8,128)(2,1)S(1)} %get-tuple-element.53), channel_id=1, source_target_pairs={{0,12},{4,8},{8,4},{12,0},{1,13},{5,9},{9,5},{13,1},{2,14},{6,10},... | collective-permute-start | bytes 294920 | tf_op jit(solution)/shard_map/ppermute | solution.py:644
  22.6 6.6 %collective-permute-start.10 = (bf16[128,384]{1,0:T(8,128)(2,1)S(1)}, bf16[128,384]{1,0:T(8,128)(2,1)S(1)}, u32[]{:S(2)}, u32[]{:S(2)}) collective-permute-start(bf16[128,384]{1,0:T(8,128)(2,1)S(1)} %get-tuple-element.54), channel_id=1, source_target_pairs={{0,4},{4,0},{8,12},{12,8},{1,5},{5,1},{9,13},{13,9},{2,6},{6,2},{1... | collective-permute-start | bytes 294920 | tf_op jit(solution)/shard_map/ppermute | solution.py:644
  31.3 10.6 %collective-permute-start.11 = (bf16[128,384]{1,0:T(8,128)(2,1)S(1)}, bf16[128,384]{1,0:T(8,128)(2,1)S(1)}, u32[]{:S(2)}, u32[]{:S(2)}) collective-permute-start(bf16[128,384]{1,0:T(8,128)(2,1)S(1)} %get-tuple-element.60), channel_id=1, source_target_pairs={{0,8},{4,12},{8,0},{12,4},{1,9},{5,13},{9,1},{13,5},{2,10},{6,14},... | collective-permute-start | bytes 294920 | tf_op jit(solution)/shard_map/ppermute | solution.py:644
  33.7 8.2 %collective-permute-start.12 = (bf16[128,384]{1,0:T(8,128)(2,1)S(1)}, bf16[128,384]{1,0:T(8,128)(2,1)S(1)}, u32[]{:S(2)}, u32[]{:S(2)}) collective-permute-start(bf16[128,384]{1,0:T(8,128)(2,1)S(1)} %get-tuple-element.61), channel_id=1, source_target_pairs={{0,12},{4,8},{8,4},{12,0},{1,13},{5,9},{9,5},{13,1},{2,14},{6,10},... | collective-permute-start | bytes 294920 | tf_op jit(solution)/shard_map/ppermute | solution.py:644
  34.9 7.6 %collective-permute-start.13 = (bf16[128,384]{1,0:T(8,128)(2,1)S(1)}, bf16[128,384]{1,0:T(8,128)(2,1)S(1)}, u32[]{:S(2)}, u32[]{:S(2)}) collective-permute-start(bf16[128,384]{1,0:T(8,128)(2,1)S(1)} %get-tuple-element.62), channel_id=1, source_target_pairs={{0,4},{4,0},{8,12},{12,8},{1,5},{5,1},{9,13},{13,9},{2,6},{6,2},{1... | collective-permute-start | bytes 294920 | tf_op jit(solution)/shard_map/ppermute | solution.py:644
  34.9 11.1 %collective-permute-start.15 = (bf16[128,128]{1,0:T(8,128)(2,1)S(1)}, bf16[128,128]{1,0:T(8,128)(2,1)S(1)}, u32[]{:S(2)}, u32[]{:S(2)}) collective-permute-start(bf16[128,128]{1,0:T(8,128)(2,1)S(1)} %get-tuple-element.68), channel_id=1, source_target_pairs={{0,8},{4,12},{8,0},{12,4},{1,9},{5,13},{9,1},{13,5},{2,10},{6,14},... | collective-permute-start | bytes 98312 | tf_op jit(solution)/shard_map/ppermute | solution.py:644
  38.1 8.0 %collective-permute-start.16 = (bf16[128,128]{1,0:T(8,128)(2,1)S(1)}, bf16[128,128]{1,0:T(8,128)(2,1)S(1)}, u32[]{:S(2)}, u32[]{:S(2)}) collective-permute-start(bf16[128,128]{1,0:T(8,128)(2,1)S(1)} %get-tuple-element.69), channel_id=1, source_target_pairs={{0,12},{4,8},{8,4},{12,0},{1,13},{5,9},{9,5},{13,1},{2,14},{6,10},... | collective-permute-start | bytes 98312 | tf_op jit(solution)/shard_map/ppermute | solution.py:644
  41.8 4.2 %collective-permute-start.17 = (bf16[128,128]{1,0:T(8,128)(2,1)S(1)}, bf16[128,128]{1,0:T(8,128)(2,1)S(1)}, u32[]{:S(2)}, u32[]{:S(2)}) collective-permute-start(bf16[128,128]{1,0:T(8,128)(2,1)S(1)} %get-tuple-element.70), channel_id=1, source_target_pairs={{0,4},{4,0},{8,12},{12,8},{1,5},{5,1},{9,13},{13,9},{2,6},{6,2},{1... | collective-permute-start | bytes 98312 | tf_op jit(solution)/shard_map/ppermute | solution.py:644
  42.5 10.1 %copy-start.1 = (bf16[256,1024]{1,0:T(8,128)(2,1)S(1)}, bf16[256,1024]{1,0:T(8,128)(2,1)}, u32[]{:S(2)}) copy-start(bf16[256,1024]{1,0:T(8,128)(2,1)} %refs_6_.1) | copy-start | bytes 1572868
  46.1 12.8 %collective-permute-start.20 = (bf16[128,1024]{1,0:T(8,128)(2,1)S(1)}, bf16[128,1024]{1,0:T(8,128)(2,1)S(1)}, u32[]{:S(2)}, u32[]{:S(2)}) collective-permute-start(bf16[128,1024]{1,0:T(8,128)(2,1)S(1)} %get-tuple-element.78.grad), channel_id=1, source_target_pairs={{4,8},{8,4},{5,9},{9,5},{6,10},{10,6},{7,11},{11,7},{20,24},{24,20... | collective-permute-start | bytes 786440 | tf_op jit(solution)/shard_map/ppermute | solution.py:660
  46.7 12.1 %collective-permute-start.19 = (bf16[128,1024]{1,0:T(8,128)(2,1)S(1)}, bf16[128,1024]{1,0:T(8,128)(2,1)S(1)}, u32[]{:S(2)}, u32[]{:S(2)}) collective-permute-start(bf16[128,1024]{1,0:T(8,128)(2,1)S(1)} %get-tuple-element.78.grad), channel_id=1, source_target_pairs={{0,4},{4,0},{8,12},{12,8},{1,5},{5,1},{9,13},{13,9},{2,6},{6,2},{1... | collective-permute-start | bytes 786440 | tf_op jit(solution)/shard_map/ppermute | solution.py:644
  51.1 4.2 %collective-permute-start.14 = (bf16[216,128]{1,0:T(8,128)(2,1)S(1)}, bf16[216,128]{1,0:T(8,128)(2,1)S(1)}, u32[]{:S(2)}, u32[]{:S(2)}) collective-permute-start(bf16[216,128]{1,0:T(8,128)(2,1)S(1)} %get-tuple-element.65.refs_0_), channel_id=1, source_target_pairs={{0,2},{2,0},{1,3},{3,1},{4,6},{6,4},{5,7},{7,5},{8,10},{10,8},{9,1... | collective-permute-start | bytes 165896 | tf_op jit(solution)/shard_map/ppermute | solution.py:644
  55.3 5.9 %collective-permute-start.18 = (bf16[216,128]{1,0:T(8,128)(2,1)S(1)}, bf16[216,128]{1,0:T(8,128)(2,1)S(1)}, u32[]{:S(2)}, u32[]{:S(2)}) collective-permute-start(bf16[216,128]{1,0:T(8,128)(2,1)S(1)} %add_dp.1.refs_0_), channel_id=1, source_target_pairs={{0,4},{4,0},{8,12},{12,8},{1,5},{5,1},{9,13},{13,9},{2,6},{6,2},{1... | collective-permute-start | bytes 165896 | tf_op jit(solution)/shard_map/ppermute | solution.py:644
  55.4 6.1 %collective-permute-start.22 = (bf16[216,128]{1,0:T(8,128)(2,1)S(1)}, bf16[216,128]{1,0:T(8,128)(2,1)S(1)}, u32[]{:S(2)}, u32[]{:S(2)}) collective-permute-start(bf16[216,128]{1,0:T(8,128)(2,1)S(1)} %add_dp.1.refs_0_), channel_id=1, source_target_pairs={{0,12},{4,8},{8,4},{12,0},{1,13},{5,9},{9,5},{13,1},{2,14},{6,10},... | collective-permute-start | bytes 165896 | tf_op jit(solution)/shard_map/ppermute | solution.py:644
  57.6 5.6 %collective-permute-start.21 = (bf16[216,128]{1,0:T(8,128)(2,1)S(1)}, bf16[216,128]{1,0:T(8,128)(2,1)S(1)}, u32[]{:S(2)}, u32[]{:S(2)}) collective-permute-start(bf16[216,128]{1,0:T(8,128)(2,1)S(1)} %add_dp.1.refs_0_), channel_id=1, source_target_pairs={{0,8},{4,12},{8,0},{12,4},{1,9},{5,13},{9,1},{13,5},{2,10},{6,14},... | collective-permute-start | bytes 165896 | tf_op jit(solution)/shard_map/ppermute | solution.py:644
  63.3 1.4 %collective-permute-start.23 = (f32[216,128]{1,0:T(8,128)S(1)}, f32[216,128]{1,0:T(8,128)S(1)}, u32[]{:S(2)}, u32[]{:S(2)}) collective-permute-start(f32[216,128]{1,0:T(8,128)S(1)} %add_seq.1.left), channel_id=1, source_target_pairs={{0,1},{1,0},{2,3},{3,2},{4,5},{5,4},{6,7},{7,6},{8,9},{9,8},{10,11... | collective-permute-start | bytes 331784 | tf_op jit(solution)/shard_map/ppermute | solution.py:644

commit v6 on v5

--- a/solution.py
+++ b/solution.py
@@ -364,11 +364,28 @@
         grads = nt_dot(gated, weight[...]).astype(jnp.bfloat16)
         for j in range(per_half):
             by_group[part * per_half + j] = grads[:, j * lanes : (j + 1) * lanes]
-    for k, gap in enumerate(distances(slots)):
-        sends[k][...] = by_group[lax.bitwise_xor(me, gap)]
-
-
-def mix_body(slots, inner, ids, tok, near, far, taps, mod, w_own, w_oth, *rest):
+    for k in range(slots):
+        sends[k][...] = by_group[lax.bitwise_xor(me, gap_of(half, k))]
+
+
+def own_conv_body(inner, tok_far, taps_far, out, tok, taps, arrive):
+    @pl.when(lax.axis_index("fsdp") == 0)
+    def work():
+        copies = [
+            pltpu.make_async_copy(tok_far, tok, arrive.at[0]),
+            pltpu.make_async_copy(taps_far, taps, arrive.at[1]),
+        ]
+        for copy in copies:
+            copy.start()
+        for copy in copies:
+            copy.wait()
+        for start in range(0, tok.shape[1], 128):
+            cols = slice(start, start + 128)
+            plane = as_f32(tok[:, cols])
+            out[:, cols] = plane + conv_lanes({1: plane}, taps[:, cols], False, inner)
+
+
+def mix_body(slots, inner, ids, centre, tok, near, far, taps, mod, w_own, w_oth, *rest):
     resid, sections = rest[0], rest[1]
     sends = rest[2 : 2 + slots]
     normed, by_group, sums_ref = rest[2 + slots :]
@@ -376,18 +393,28 @@
     rows, width = tok.shape
     step = 128
 
-    def all_planes(before, after):
+    def all_planes(has_centre, before, after):
         sums = jnp.zeros((rows, step), jnp.float32)
         for start in range(0, width, step):
             cols = slice(start, start + step)
-            planes = {i: as_f32(ref[:, cols]) for i, ref in enumerate((before, tok, after))}
-            rounded = planes[1] + conv_lanes(planes, taps[:, cols], False, inner)
+            planes = {0: as_f32(before[:, cols]), 2: as_f32(after[:, cols])}
+            if has_centre:
+                total = centre[:, cols]
+            else:
+                planes[1] = as_f32(tok[:, cols])
+                total = planes[1]
+            rounded = total + conv_lanes(planes, taps[:, cols], False, inner)
             rounded = rounded.astype(jnp.bfloat16)
             resid[:, cols] = rounded
             sums = sums + as_f32(rounded)
         sums_ref[...] = sums
 
-    sided(lax.rem(me, 2) == 1, near, far, all_planes)
+    for has_centre in (True, False):
+
+        @pl.when((half == 0) == has_centre)
+        def work():
+            sided(lax.rem(me, 2) == 1, near, far, functools.partial(all_planes, has_centre))
+
     sums = sums_ref[...]
     mean = jnp.sum(sums, axis=1, keepdims=True) * (1.0 / width)
     squares = jnp.zeros((rows, step), jnp.float32)
@@ -413,8 +440,8 @@
             if part < 2:
                 block = block * lax.rsqrt(head_mean(block * block) + 1e-06)
             by_group[group, :, part * lanes : (part + 1) * lanes] = block.astype(jnp.bfloat16)
-    for k, gap in enumerate(distances(slots)):
-        sends[k][...] = by_group[lax.bitwise_xor(me, gap)]
+    for k in range(slots):
+        sends[k][...] = by_group[lax.bitwise_xor(me, gap_of(half, k))]
 
 
 def attend_body(slots, *refs):
@@ -484,8 +511,8 @@
     rows, width = resid.shape
     lanes = by_group.shape[3]
     inner_width = H * HD
-    for k, gap in enumerate(distances(slots)):
-        group = lax.bitwise_xor(me, gap)
+    for k in range(slots):
+        group = lax.bitwise_xor(me, gap_of(half, k))
         for part in range(3):
             by_group[group, part] = backs[k][:, part * lanes : (part + 1) * lanes]
     for group in range(slots):
@@ -568,8 +595,8 @@
     me, half = ids[0], ids[1]
     lanes = attns[0].shape[1]
     per_half = wo_own.shape[0] // lanes
-    for k, gap in enumerate(distances(slots)):
-        by_group[lax.bitwise_xor(me, gap)] = attns[k][...]
+    for k in range(slots):
+        by_group[lax.bitwise_xor(me, gap_of(half, k))] = attns[k][...]
     total = None
     for weight, part in ((wo_own, half), (wo_oth, 1 - half)):
         for j in range(per_half):
@@ -601,11 +628,6 @@
 def sum_body(*refs):
     out = refs[-1]
     out[...] = tree_sum([as_f32(ref[...]) for ref in refs[:-1]]).astype(out.dtype)
-
-
-def seq_sum_body(slots, *refs):
-    gaps = distances(slots)
-    refs[slots][...] = tree_sum([refs[gaps.index(gap)][...].astype(jnp.float32) for gap in range(slots)])
 
 
 def final_body(factor, left, right, out):
@@ -644,13 +666,24 @@
     return lax.ppermute(value, axis, [(i, i ^ distance) for i in range(count)])
 
 
-def distances(slots):
-    return (0, 2, 3, 1)[:slots]
+ORDERS = ((0, 1, 3, 2), (0, 2, 3, 1))
+
+
+def gap_of(half, k):
+    return jnp.where(half == 0, ORDERS[0][k], ORDERS[1][k])
 
 
 def exchanged(pieces):
-    pairs = list(zip(pieces, distances(len(pieces))))
-    return [pieces[0]] + [swapped(piece, "seq", k) for piece, k in pairs[1:]]
+    seqs, cores = lax.axis_size("seq"), lax.axis_size("fsdp")
+    received = [pieces[0]]
+    for k in range(1, len(pieces)):
+        pairs = [
+            (cores * z + core, cores * (z ^ ORDERS[core][k]) + core)
+            for z in range(seqs)
+            for core in range(cores)
+        ]
+        received.append(lax.ppermute(pieces[k], ("seq", "fsdp"), pairs))
+    return received
 
 
 def neighbours(value):
@@ -677,7 +710,20 @@
 
     wo_oth = swapped(out_weight, "fsdp", 1)
     wt_oth = swapped(time_weight, "fsdp", 1)
-    near, far = neighbours(tok)
+    (centre,) = call(
+        functools.partial(own_conv_body, inner),
+        "own_conv",
+        [shape((rows, width), f32)],
+        (tok, conv_kernel),
+        [
+            pltpu.VMEM((rows, width), bf16),
+            pltpu.VMEM(conv_kernel.shape, f32),
+            pltpu.SemaphoreType.DMA((2,)),
+        ],
+        far_args=(0, 1),
+    )
+    tok_sent, centre = lax.optimization_barrier((tok, centre))
+    near, far = neighbours(pltpu.with_memory_space_constraint(tok_sent, pltpu.HBM))
     wq_oth = swapped(qkv_weight, "fsdp", 1)
 
     freq = 2 * time_weight.shape[0]
@@ -709,7 +755,7 @@
         "mix",
         [shape((rows, width), bf16), shape((rows, 2 * H * HD), f32)]
         + [shape((rows, 3 * lanes), bf16)] * slots,
-        (ids, tok, near, far, conv_kernel, mod, qkv_weight, wq_oth),
+        (ids, centre, tok, near, far, conv_kernel, mod, qkv_weight, wq_oth),
         [
             pltpu.VMEM((2, rows, width // 2), bf16),
             pltpu.VMEM((slots, rows, 3 * lanes), bf16),
@@ -778,9 +824,7 @@
     factor = 1.0 / math.sqrt(lax.axis_size("dp") * lax.axis_size("fsdp") * slots * rows)
     pieces = exchanged([terms] * slots)
     pieces[-1], token_grad = lax.optimization_barrier((pieces[-1], token_grad))
-    (summed,) = call(
-        functools.partial(seq_sum_body, slots), "add_seq", [shape(terms.shape, f32)], pieces
-    )
+    (summed,) = call(sum_body, "add_seq", [shape(terms.shape, f32)], pieces)
     (kernel_grad,) = call(
         functools.partial(final_body, factor),
         "final",

time: 65.5 us -> 62.8 us (0.959)
  starting transfers between devices: 32.6 us -> 29.6 us
  waiting for transfers between devices: 14.8 us -> 13 us
  Pallas kernels: 16.3 us -> 17.5 us
  local copies, waits for them, and re-layouts: 0.04 us -> 0.86 us
    ppermute x22 -> x7, starting transfers between devices: 30.5 us -> 9.58 us  [swapped(): return lax.ppermute(value, axis, [(i, i ^ distance) for i in range(count)])]
    ppermute x0 -> x15, starting transfers between devices: none -> 17.8 us  [exchanged(): received.append(lax.ppermute(pieces[k], ('seq', 'fsdp'), pairs))]
    ppermute x22 -> x7, waiting for transfers between devices: 14.8 us -> 2.31 us  [swapped(): return lax.ppermute(value, axis, [(i, i ^ distance) for i in range(count)])]
    ppermute x0 -> x15, waiting for transfers between devices: none -> 10.7 us  [exchanged(): received.append(lax.ppermute(pieces[k], ('seq', 'fsdp'), pairs))]
    pallas_call x9 -> x10, Pallas kernels: 16.3 us -> 17.5 us  [call(): pl.pallas_call(body, out_shape=tuple(outs), in_specs=specs, out_specs=(wh...]
    unnamed x11 -> x15, local copies, waits for them, and re-layouts: 0.03 us -> 0.84 us
  transfers between devices with their start and end apart: 24 -> 24, of which waited for: 9 -> 9; matrix products, arithmetic and copies ran while one was open for 0% -> 0% of each run, Pallas kernels for 21% -> 24%
where the time goes in v6:
time: 62.8 us; the launch traced here: 62.6 us
  starting transfers between devices  29.6 us (47%)
  Pallas kernels  17.5 us (28%)
  waiting for transfers between devices  13 us (21%)
  between operations  1.5 us (2%)
  local copies, waits for them, and re-layouts  0.86 us (1%)
    ppermute x15, starting transfers between devices, exchanged(): received.append(lax.ppermute(pieces[k], ('seq', 'fsdp'), pairs))  17.8 us
    pallas_call x10, Pallas kernels, call(): pl.pallas_call(body, out_shape=tuple(outs), in_specs=specs, out_specs=(wh...  17.5 us
    ppermute x15, waiting for transfers between devices, exchanged(): received.append(lax.ppermute(pieces[k], ('seq', 'fsdp'), pairs))  10.7 us
    ppermute x7, starting transfers between devices, swapped(): return lax.ppermute(value, axis, [(i, i ^ distance) for i in range(count)])  9.58 us
    ppermute x7, waiting for transfers between devices, swapped(): return lax.ppermute(value, axis, [(i, i ^ distance) for i in range(count)])  2.31 us
    ppermute x2, starting transfers between devices, neighbours(): lax.ppermute(value, 'seq', middle + [(j, i) for i, j in middle])  2.18 us
  transfers between devices with their start and end apart: 24, of which 9 were waited for; matrix products, arithmetic and copies ran while one was open for 0% of the time, Pallas kernels for 24%

profile of v6, /device:TPU:0, one launch (start us, length us, event | category | flops | bytes accessed | tf_op | source)
XLA Modules:
  0.0 62.6 jit_solution(9002155463717262396)
XLA Ops:
  1.7 1.4 %own_conv.1.centre = f32[128,1024]{1,0:T(8,128)S(1)} custom-call(bf16[128,1024]{1,0:T(8,128)(2,1)} %bitcast.16, f32[27,1024]{1,0:T(8,128)} %taps.3), custom_call_target="tpu_custom_call" | custom-call | bytes 897024 | tf_op jit(solution)/shard_map/own_conv/pallas_call | solution.py:652
  3.1 0.8 %copy-done.2 = f32[128,1024]{1,0:T(8,128)} copy-done((f32[128,1024]{1,0:T(8,128)}, f32[128,1024]{1,0:T(8,128)S(1)}, u32[]{:S(2)}) %copy-start.2) | copy-done | bytes 524312
  3.9 1.5 %collective-permute-start.1 = (bf16[128,1024]{1,0:T(8,128)(2,1)}, bf16[128,1024]{1,0:T(8,128)(2,1)}, u32[]{:S(2)}, u32[]{:S(2)}) collective-permute-start(bf16[128,1024]{1,0:T(8,128)(2,1)} %bitcast.17), channel_id=1, source_target_pairs={{4,8},{8,4},{5,9},{9,5},{6,10},{10,6},{7,11},{11,7},{20,24},{24,20... | collective-permute-start | bytes 786440 | tf_op jit(solution)/shard_map/ppermute | solution.py:693
  5.4 4.8 %collective-permute-start = (bf16[128,1024]{1,0:T(8,128)(2,1)}, bf16[128,1024]{1,0:T(8,128)(2,1)}, u32[]{:S(2)}, u32[]{:S(2)}) collective-permute-start(bf16[128,1024]{1,0:T(8,128)(2,1)} %bitcast.18), channel_id=1, source_target_pairs={{0,4},{4,0},{8,12},{12,8},{1,5},{5,1},{9,13},{13,9},{2,6},{6,2},{1... | collective-permute-start | bytes 786440 | tf_op jit(solution)/shard_map/ppermute | solution.py:666
  11.1 2.8 %front.1 = (f32[3,1024]{1,0:T(4,128)S(1)}, bf16[256,1024]{1,0:T(8,128)(2,1)S(1)}, bf16[128,128]{1,0:T(8,128)(2,1)S(1)}, bf16[128,128]{1,0:T(8,128)(2,1)S(1)}, bf...) custom-call(s32[2]{0:T(128)S(1)} %pad_add_fusion.ids, bf16[2,8,128]{2,1,0:T(8,128)(2,1)S(1)} %broadcast_in_dim.10.feats, ...), custom_call_target="tpu_custom_call" | custom-call | flops 134217728 | bytes 3567624 | tf_op jit(solution)/shard_map/front/pallas_call | solution.py:652
  14.0 1.9 %collective-permute-start.6 = (bf16[128,128]{1,0:T(8,128)(2,1)S(1)}, bf16[128,128]{1,0:T(8,128)(2,1)S(1)}, u32[]{:S(2)}, u32[]{:S(2)}) collective-permute-start(bf16[128,128]{1,0:T(8,128)(2,1)S(1)} %get-tuple-element.53), channel_id=1, source_target_pairs={{0,12},{1,13},{4,8},{5,9},{8,4},{9,5},{12,0},{13,1},{2,14},{3,15},... | collective-permute-start | bytes 98312 | tf_op jit(solution)/shard_map/ppermute | solution.py:685
  15.9 1.6 %collective-permute-start.7 = (bf16[128,128]{1,0:T(8,128)(2,1)S(1)}, bf16[128,128]{1,0:T(8,128)(2,1)S(1)}, u32[]{:S(2)}, u32[]{:S(2)}) collective-permute-start(bf16[128,128]{1,0:T(8,128)(2,1)S(1)} %get-tuple-element.54), channel_id=1, source_target_pairs={{0,8},{1,5},{4,12},{5,1},{8,0},{9,13},{12,4},{13,9},{2,10},{3,7},{... | collective-permute-start | bytes 98312 | tf_op jit(solution)/shard_map/ppermute | solution.py:685
  17.6 2.9 %mix.1 = (bf16[128,1024]{1,0:T(8,128)(2,1)S(1)}, f32[128,1024]{1,0:T(8,128)S(1)}, bf16[128,384]{1,0:T(8,128)(2,1)S(1)}, bf16[128,384]{1,0:T(8,128)(2,1)S(1)}, bf...) custom-call(s32[2]{0:T(128)S(1)} %pad_add_fusion.ids, f32[128,1024]{1,0:T(8,128)S(1)} %copy-done.3, ...), custom_call_target="tpu_custom_call" | custom-call | flops 402653184 | bytes 5758984 | tf_op jit(solution)/shard_map/mix/pallas_call | solution.py:652
  21.5 2.3 %collective-permute-start.9 = (bf16[128,384]{1,0:T(8,128)(2,1)S(1)}, bf16[128,384]{1,0:T(8,128)(2,1)S(1)}, u32[]{:S(2)}, u32[]{:S(2)}) collective-permute-start(bf16[128,384]{1,0:T(8,128)(2,1)S(1)} %get-tuple-element.57), channel_id=1, source_target_pairs={{0,12},{1,13},{4,8},{5,9},{8,4},{9,5},{12,0},{13,1},{2,14},{3,15},... | collective-permute-start | bytes 294920 | tf_op jit(solution)/shard_map/ppermute | solution.py:685
  23.8 0.8 %collective-permute-start.10 = (bf16[128,384]{1,0:T(8,128)(2,1)S(1)}, bf16[128,384]{1,0:T(8,128)(2,1)S(1)}, u32[]{:S(2)}, u32[]{:S(2)}) collective-permute-start(bf16[128,384]{1,0:T(8,128)(2,1)S(1)} %get-tuple-element.58), channel_id=1, source_target_pairs={{0,8},{1,5},{4,12},{5,1},{8,0},{9,13},{12,4},{13,9},{2,10},{3,7},{... | collective-permute-start | bytes 294920 | tf_op jit(solution)/shard_map/ppermute | solution.py:685
  24.5 2.7 %collective-permute-done.8.refs_1_ = bf16[128,384]{1,0:T(8,128)(2,1)S(1)} collective-permute-done((bf16[128,384]{1,0:T(8,128)(2,1)S(1)}, bf16[128,384]{1,0:T(8,128)(2,1)S(1)}, u32[]{:S(2)}, u32[]{:S(2)}) %collective-permute-start.8) | collective-permute-done | bytes 98336 | tf_op jit(solution)/shard_map/ppermute | solution.py:685
  27.3 1.4 %collective-permute-done.9.refs_2_ = bf16[128,384]{1,0:T(8,128)(2,1)S(1)} collective-permute-done((bf16[128,384]{1,0:T(8,128)(2,1)S(1)}, bf16[128,384]{1,0:T(8,128)(2,1)S(1)}, u32[]{:S(2)}, u32[]{:S(2)}) %collective-permute-start.9) | collective-permute-done | bytes 98336 | tf_op jit(solution)/shard_map/ppermute | solution.py:685
  28.7 2.1 %collective-permute-done.10.refs_3_ = bf16[128,384]{1,0:T(8,128)(2,1)S(1)} collective-permute-done((bf16[128,384]{1,0:T(8,128)(2,1)S(1)}, bf16[128,384]{1,0:T(8,128)(2,1)S(1)}, u32[]{:S(2)}, u32[]{:S(2)}) %collective-permute-start.10) | collective-permute-done | bytes 98336 | tf_op jit(solution)/shard_map/ppermute | solution.py:685
  30.8 2.1 %attend.1 = (bf16[128,384]{1,0:T(8,128)(2,1)S(1)}, bf16[128,384]{1,0:T(8,128)(2,1)S(1)}, bf16[128,384]{1,0:T(8,128)(2,1)S(1)}, bf16[128,384]{1,0:T(8,128)(2,1)S(...) custom-call(bf16[128,384]{1,0:T(8,128)(2,1)S(1)} %get-tuple-element., ...), custom_call_target="tpu_custom_call" | custom-call | flops 402653184 | bytes 1048576 | tf_op jit(solution)/shard_map/attend/pallas_call | solution.py:652
  32.9 1.8 %collective-permute-start.12 = (bf16[128,384]{1,0:T(8,128)(2,1)S(1)}, bf16[128,384]{1,0:T(8,128)(2,1)S(1)}, u32[]{:S(2)}, u32[]{:S(2)}) collective-permute-start(bf16[128,384]{1,0:T(8,128)(2,1)S(1)} %get-tuple-element.65), channel_id=1, source_target_pairs={{0,12},{1,13},{4,8},{5,9},{8,4},{9,5},{12,0},{13,1},{2,14},{3,15},... | collective-permute-start | bytes 294920 | tf_op jit(solution)/shard_map/ppermute | solution.py:685
  34.7 1.7 %collective-permute-start.13 = (bf16[128,384]{1,0:T(8,128)(2,1)S(1)}, bf16[128,384]{1,0:T(8,128)(2,1)S(1)}, u32[]{:S(2)}, u32[]{:S(2)}) collective-permute-start(bf16[128,384]{1,0:T(8,128)(2,1)S(1)} %get-tuple-element.66), channel_id=1, source_target_pairs={{0,8},{1,5},{4,12},{5,1},{8,0},{9,13},{12,4},{13,9},{2,10},{3,7},{... | collective-permute-start | bytes 294920 | tf_op jit(solution)/shard_map/ppermute | solution.py:685
  36.4 1.0 %collective-permute-start.15 = (bf16[128,128]{1,0:T(8,128)(2,1)S(1)}, bf16[128,128]{1,0:T(8,128)(2,1)S(1)}, u32[]{:S(2)}, u32[]{:S(2)}) collective-permute-start(bf16[128,128]{1,0:T(8,128)(2,1)S(1)} %get-tuple-element.72), channel_id=1, source_target_pairs={{0,4},{1,9},{4,0},{5,13},{8,12},{9,1},{12,8},{13,5},{2,6},{3,11},{... | collective-permute-start | bytes 98312 | tf_op jit(solution)/shard_map/ppermute | solution.py:685
  37.4 1.8 %collective-permute-start.16 = (bf16[128,128]{1,0:T(8,128)(2,1)S(1)}, bf16[128,128]{1,0:T(8,128)(2,1)S(1)}, u32[]{:S(2)}, u32[]{:S(2)}) collective-permute-start(bf16[128,128]{1,0:T(8,128)(2,1)S(1)} %get-tuple-element.73), channel_id=1, source_target_pairs={{0,12},{1,13},{4,8},{5,9},{8,4},{9,5},{12,0},{13,1},{2,14},{3,15},... | collective-permute-start | bytes 98312 | tf_op jit(solution)/shard_map/ppermute | solution.py:685
  39.1 1.0 %collective-permute-start.17 = (bf16[128,128]{1,0:T(8,128)(2,1)S(1)}, bf16[128,128]{1,0:T(8,128)(2,1)S(1)}, u32[]{:S(2)}, u32[]{:S(2)}) collective-permute-start(bf16[128,128]{1,0:T(8,128)(2,1)S(1)} %get-tuple-element.74), channel_id=1, source_target_pairs={{0,8},{1,5},{4,12},{5,1},{8,0},{9,13},{12,4},{13,9},{2,10},{3,7},{... | collective-permute-start | bytes 98312 | tf_op jit(solution)/shard_map/ppermute | solution.py:685
  40.1 2.5 %collective-permute-done.13.refs_3_ = bf16[128,384]{1,0:T(8,128)(2,1)S(1)} collective-permute-done((bf16[128,384]{1,0:T(8,128)(2,1)S(1)}, bf16[128,384]{1,0:T(8,128)(2,1)S(1)}, u32[]{:S(2)}, u32[]{:S(2)}) %collective-permute-start.13) | collective-permute-done | bytes 98336 | tf_op jit(solution)/shard_map/ppermute | solution.py:685
  42.6 3.6 %tail.1 = (bf16[128,1024]{1,0:T(8,128)(2,1)S(1)}, bf16[216,128]{1,0:T(8,128)(2,1)S(1)}) custom-call(s32[2]{0:T(128)S(1)} %pad_add_fusion.ids, bf16[128,384]{1,0:T(8,128)(2,1)S(1)} %get-tuple-element.63.refs_0_, bf16[128,384]{1,0:T(8,128)(2,1)S(1)} %collective-permute-done.11.refs_1_, bf16[128,384]{1,0:T(8,128)(2,1)S(1)} %collective-permute-done.12.refs_2_, ...), custom_call_target="tpu_custom_call" | custom-call | flops 402653184 | bytes 5703688 | tf_op jit(solution)/shard_map/tail/pallas_call | solution.py:652
  46.3 0.7 %collective-permute-start.20 = (bf16[128,1024]{1,0:T(8,128)(2,1)S(1)}, bf16[128,1024]{1,0:T(8,128)(2,1)S(1)}, u32[]{:S(2)}, u32[]{:S(2)}) collective-permute-start(bf16[128,1024]{1,0:T(8,128)(2,1)S(1)} %get-tuple-element.82.grad), channel_id=1, source_target_pairs={{4,8},{8,4},{5,9},{9,5},{6,10},{10,6},{7,11},{11,7},{20,24},{24,20... | collective-permute-start | bytes 786440 | tf_op jit(solution)/shard_map/ppermute | solution.py:693
  47.0 2.1 %collective-permute-start.19 = (bf16[128,1024]{1,0:T(8,128)(2,1)S(1)}, bf16[128,1024]{1,0:T(8,128)(2,1)S(1)}, u32[]{:S(2)}, u32[]{:S(2)}) collective-permute-start(bf16[128,1024]{1,0:T(8,128)(2,1)S(1)} %get-tuple-element.82.grad), channel_id=1, source_target_pairs={{0,4},{4,0},{8,12},{12,8},{1,5},{5,1},{9,13},{13,9},{2,6},{6,2},{1... | collective-permute-start | bytes 786440 | tf_op jit(solution)/shard_map/ppermute | solution.py:666
  49.1 1.5 %collective-permute-start.14 = (bf16[216,128]{1,0:T(8,128)(2,1)S(1)}, bf16[216,128]{1,0:T(8,128)(2,1)S(1)}, u32[]{:S(2)}, u32[]{:S(2)}) collective-permute-start(bf16[216,128]{1,0:T(8,128)(2,1)S(1)} %get-tuple-element.69.refs_0_), channel_id=1, source_target_pairs={{0,2},{2,0},{1,3},{3,1},{4,6},{6,4},{5,7},{7,5},{8,10},{10,8},{9,1... | collective-permute-start | bytes 165896 | tf_op jit(solution)/shard_map/ppermute | solution.py:666
  50.6 1.7 %out.1 = bf16[128,1024]{1,0:T(8,128)(2,1)} custom-call(s32[2]{0:T(128)S(1)} %pad_add_fusion.ids, bf16[128,128]{1,0:T(8,128)(2,1)S(1)} %get-tuple-element.75.refs_0_, bf16[128,128]{1,0:T(8,128)(2,1)S(1)} %collective-permute-done.15.refs_1_, bf16[128,128]{1,0:T(8,128)(2,1)S(1)} %collective-permute-done.16.refs_2_, ...), custom_call_target="tpu_custom_call" | custom-call | flops 134217728 | bytes 1716232 | tf_op jit(solution)/shard_map/out/pallas_call | solution.py:652
  52.3 1.0 %collective-permute-done.14.refs_1_ = bf16[216,128]{1,0:T(8,128)(2,1)S(1)} collective-permute-done((bf16[216,128]{1,0:T(8,128)(2,1)S(1)}, bf16[216,128]{1,0:T(8,128)(2,1)S(1)}, u32[]{:S(2)}, u32[]{:S(2)}) %collective-permute-start.14) | collective-permute-done | bytes 55328 | tf_op jit(solution)/shard_map/ppermute | solution.py:666
  53.3 1.1 %collective-permute-start.18 = (bf16[216,128]{1,0:T(8,128)(2,1)S(1)}, bf16[216,128]{1,0:T(8,128)(2,1)S(1)}, u32[]{:S(2)}, u32[]{:S(2)}) collective-permute-start(bf16[216,128]{1,0:T(8,128)(2,1)S(1)} %add_dp.1.refs_0_), channel_id=1, source_target_pairs={{0,8},{1,5},{4,12},{5,1},{8,0},{9,13},{12,4},{13,9},{2,10},{3,7},{... | collective-permute-start | bytes 165896 | tf_op jit(solution)/shard_map/ppermute | solution.py:685
  54.4 1.4 %collective-permute-start.22 = (bf16[216,128]{1,0:T(8,128)(2,1)S(1)}, bf16[216,128]{1,0:T(8,128)(2,1)S(1)}, u32[]{:S(2)}, u32[]{:S(2)}) collective-permute-start(bf16[216,128]{1,0:T(8,128)(2,1)S(1)} %add_dp.1.refs_0_), channel_id=1, source_target_pairs={{0,12},{1,13},{4,8},{5,9},{8,4},{9,5},{12,0},{13,1},{2,14},{3,15},... | collective-permute-start | bytes 165896 | tf_op jit(solution)/shard_map/ppermute | solution.py:685
  55.8 1.0 %collective-permute-start.21 = (bf16[216,128]{1,0:T(8,128)(2,1)S(1)}, bf16[216,128]{1,0:T(8,128)(2,1)S(1)}, u32[]{:S(2)}, u32[]{:S(2)}) collective-permute-start(bf16[216,128]{1,0:T(8,128)(2,1)S(1)} %add_dp.1.refs_0_), channel_id=1, source_target_pairs={{0,4},{1,9},{4,0},{5,13},{8,12},{9,1},{12,8},{13,5},{2,6},{3,11},{... | collective-permute-start | bytes 165896 | tf_op jit(solution)/shard_map/ppermute | solution.py:685
  56.8 2.3 %back_conv.1 = bf16[128,1024]{1,0:T(8,128)(2,1)} custom-call(s32[2]{0:T(128)S(1)} %pad_add_fusion.ids, bf16[128,1024]{1,0:T(8,128)(2,1)S(1)} %get-tuple-element.82.grad, bf16[128,1024]{1,0:T(8,128)(2,1)S(1)} %collective-permute-done.19.near, bf16[128,1024]{1,0:T(8,128)(2,1)S(1)} %collective-permute-done.20.far, f32[27,1024]{1,0:T(8,128)S(1)} %copy-done.5), custom_call_target="tpu_custom_call" | custom-call | bytes 1159176 | tf_op jit(solution)/shard_map/back_conv/pallas_call | solution.py:652
  59.1 1.3 %collective-permute-done.22.refs_2_ = bf16[216,128]{1,0:T(8,128)(2,1)S(1)} collective-permute-done((bf16[216,128]{1,0:T(8,128)(2,1)S(1)}, bf16[216,128]{1,0:T(8,128)(2,1)S(1)}, u32[]{:S(2)}, u32[]{:S(2)}) %collective-permute-start.22) | collective-permute-done | bytes 55328 | tf_op jit(solution)/shard_map/ppermute | solution.py:685
  60.6 1.3 %collective-permute-done.23.right = f32[216,128]{1,0:T(8,128)S(1)} collective-permute-done((f32[216,128]{1,0:T(8,128)S(1)}, f32[216,128]{1,0:T(8,128)S(1)}, u32[]{:S(2)}, u32[]{:S(2)}) %collective-permute-start.23) | collective-permute-done | bytes 110624 | tf_op jit(solution)/shard_map/ppermute | solution.py:666
  (47 shorter events, 3.3 us)
Async XLA Ops:
  0.6 16.9 %collective-permute-start.4 = (bf16[512,1536]{1,0:T(8,128)(2,1)}, bf16[512,1536]{1,0:T(8,128)(2,1)S(1)}, u32[]{:S(2)}, u32[]{:S(2)}) collective-permute-start(bf16[512,1536]{1,0:T(8,128)(2,1)} %refs_8_.1), channel_id=1, source_target_pairs={{0,1},{1,0},{2,3},{3,2},{4,5},{5,4},{6,7},{7,6},{8,9},{9,8},{10,11... | collective-permute-start | bytes 4718600 | tf_op jit(solution)/shard_map/ppermute | solution.py:666
  1.1 9.9 %collective-permute-start.2 = (bf16[128,3072]{1,0:T(8,128)(2,1)}, bf16[128,3072]{1,0:T(8,128)(2,1)}, u32[]{:S(2)}, u32[]{:S(2)}) collective-permute-start(bf16[128,3072]{1,0:T(8,128)(2,1)} %rest_0_.1), channel_id=1, source_target_pairs={{0,1},{1,0},{2,3},{3,2},{4,5},{5,4},{6,7},{7,6},{8,9},{9,8},{10,11... | collective-permute-start | bytes 2359304 | tf_op jit(solution)/shard_map/ppermute | solution.py:666
  1.2 9.9 %collective-permute-start.3 = (bf16[256,1024]{1,0:T(8,128)(2,1)}, bf16[256,1024]{1,0:T(8,128)(2,1)}, u32[]{:S(2)}, u32[]{:S(2)}) collective-permute-start(bf16[256,1024]{1,0:T(8,128)(2,1)} %refs_6_.1), channel_id=1, source_target_pairs={{0,1},{1,0},{2,3},{3,2},{4,5},{5,4},{6,7},{7,6},{8,9},{9,8},{10,11... | collective-permute-start | bytes 1572872 | tf_op jit(solution)/shard_map/ppermute | solution.py:666
  3.1 0.8 %copy-start.2 = (f32[128,1024]{1,0:T(8,128)}, f32[128,1024]{1,0:T(8,128)S(1)}, u32[]{:S(2)}) copy-start(f32[128,1024]{1,0:T(8,128)S(1)} %own_conv.1.centre) | copy-start | bytes 1572868
  3.9 13.6 %copy-start = (bf16[512,1536]{1,0:T(8,128)(2,1)S(1)}, bf16[512,1536]{1,0:T(8,128)(2,1)}, u32[]{:S(2)}) copy-start(bf16[512,1536]{1,0:T(8,128)(2,1)} %refs_8_.1) | copy-start | bytes 4718596
  3.9 13.6 %copy-start.1 = (bf16[1,1,8,16,1024]{4,3,2,1,0:T(8,128)(2,1)S(1)}, bf16[1,1,8,16,1024]{4,3,2,1,0:T(8,128)(2,1)}, u32[]{:S(2)}) copy-start(bf16[1,1,8,16,1024]{4,3,2,1,0:T(8,128)(2,1)} %param.8) | copy-start | bytes 786436
  3.9 13.7 %copy-start.5 = (f32[27,1024]{1,0:T(8,128)S(1)}, f32[27,1024]{1,0:T(8,128)}, u32[]{:S(2)}) copy-start(f32[27,1024]{1,0:T(8,128)} %taps.3) | copy-start | bytes 331780
  3.9 12.0 %collective-permute-start.1 = (bf16[128,1024]{1,0:T(8,128)(2,1)}, bf16[128,1024]{1,0:T(8,128)(2,1)}, u32[]{:S(2)}, u32[]{:S(2)}) collective-permute-start(bf16[128,1024]{1,0:T(8,128)(2,1)} %bitcast.17), channel_id=1, source_target_pairs={{4,8},{8,4},{5,9},{9,5},{6,10},{10,6},{7,11},{11,7},{20,24},{24,20... | collective-permute-start | bytes 786440 | tf_op jit(solution)/shard_map/ppermute | solution.py:693
  5.4 12.1 %collective-permute-start = (bf16[128,1024]{1,0:T(8,128)(2,1)}, bf16[128,1024]{1,0:T(8,128)(2,1)}, u32[]{:S(2)}, u32[]{:S(2)}) collective-permute-start(bf16[128,1024]{1,0:T(8,128)(2,1)} %bitcast.18), channel_id=1, source_target_pairs={{0,4},{4,0},{8,12},{12,8},{1,5},{5,1},{9,13},{13,9},{2,6},{6,2},{1... | collective-permute-start | bytes 786440 | tf_op jit(solution)/shard_map/ppermute | solution.py:666
  11.0 6.6 %copy-start.3 = (f32[128,1024]{1,0:T(8,128)S(1)}, f32[128,1024]{1,0:T(8,128)}, u32[]{:S(2)}) copy-start(f32[128,1024]{1,0:T(8,128)} %copy-done.2) | copy-start | bytes 1572868
  14.0 6.5 %collective-permute-start.5 = (bf16[128,128]{1,0:T(8,128)(2,1)S(1)}, bf16[128,128]{1,0:T(8,128)(2,1)S(1)}, u32[]{:S(2)}, u32[]{:S(2)}) collective-permute-start(bf16[128,128]{1,0:T(8,128)(2,1)S(1)} %get-tuple-element.52), channel_id=1, source_target_pairs={{0,4},{1,9},{4,0},{5,13},{8,12},{9,1},{12,8},{13,5},{2,6},{3,11},{... | collective-permute-start | bytes 98312 | tf_op jit(solution)/shard_map/ppermute | solution.py:685
  14.0 6.4 %collective-permute-start.6 = (bf16[128,128]{1,0:T(8,128)(2,1)S(1)}, bf16[128,128]{1,0:T(8,128)(2,1)S(1)}, u32[]{:S(2)}, u32[]{:S(2)}) collective-permute-start(bf16[128,128]{1,0:T(8,128)(2,1)S(1)} %get-tuple-element.53), channel_id=1, source_target_pairs={{0,12},{1,13},{4,8},{5,9},{8,4},{9,5},{12,0},{13,1},{2,14},{3,15},... | collective-permute-start | bytes 98312 | tf_op jit(solution)/shard_map/ppermute | solution.py:685
  15.9 5.2 %collective-permute-start.7 = (bf16[128,128]{1,0:T(8,128)(2,1)S(1)}, bf16[128,128]{1,0:T(8,128)(2,1)S(1)}, u32[]{:S(2)}, u32[]{:S(2)}) collective-permute-start(bf16[128,128]{1,0:T(8,128)(2,1)S(1)} %get-tuple-element.54), channel_id=1, source_target_pairs={{0,8},{1,5},{4,12},{5,1},{8,0},{9,13},{12,4},{13,9},{2,10},{3,7},{... | collective-permute-start | bytes 98312 | tf_op jit(solution)/shard_map/ppermute | solution.py:685
  20.4 22.1 %copy-start.6 = (bf16[1,1,8,16,1024]{4,3,2,1,0:T(8,128)(2,1)S(1)}, bf16[1,1,8,16,1024]{4,3,2,1,0:T(8,128)(2,1)}, u32[]{:S(2)}) copy-start(bf16[1,1,8,16,1024]{4,3,2,1,0:T(8,128)(2,1)} %param.15) | copy-start | bytes 786436
  21.1 6.2 %collective-permute-start.8 = (bf16[128,384]{1,0:T(8,128)(2,1)S(1)}, bf16[128,384]{1,0:T(8,128)(2,1)S(1)}, u32[]{:S(2)}, u32[]{:S(2)}) collective-permute-start(bf16[128,384]{1,0:T(8,128)(2,1)S(1)} %get-tuple-element.56), channel_id=1, source_target_pairs={{0,4},{1,9},{4,0},{5,13},{8,12},{9,1},{12,8},{13,5},{2,6},{3,11},{... | collective-permute-start | bytes 294920 | tf_op jit(solution)/shard_map/ppermute | solution.py:685
  21.5 7.2 %collective-permute-start.9 = (bf16[128,384]{1,0:T(8,128)(2,1)S(1)}, bf16[128,384]{1,0:T(8,128)(2,1)S(1)}, u32[]{:S(2)}, u32[]{:S(2)}) collective-permute-start(bf16[128,384]{1,0:T(8,128)(2,1)S(1)} %get-tuple-element.57), channel_id=1, source_target_pairs={{0,12},{1,13},{4,8},{5,9},{8,4},{9,5},{12,0},{13,1},{2,14},{3,15},... | collective-permute-start | bytes 294920 | tf_op jit(solution)/shard_map/ppermute | solution.py:685
  23.8 7.0 %collective-permute-start.10 = (bf16[128,384]{1,0:T(8,128)(2,1)S(1)}, bf16[128,384]{1,0:T(8,128)(2,1)S(1)}, u32[]{:S(2)}, u32[]{:S(2)}) collective-permute-start(bf16[128,384]{1,0:T(8,128)(2,1)S(1)} %get-tuple-element.58), channel_id=1, source_target_pairs={{0,8},{1,5},{4,12},{5,1},{8,0},{9,13},{12,4},{13,9},{2,10},{3,7},{... | collective-permute-start | bytes 294920 | tf_op jit(solution)/shard_map/ppermute | solution.py:685
  32.8 6.3 %collective-permute-start.11 = (bf16[128,384]{1,0:T(8,128)(2,1)S(1)}, bf16[128,384]{1,0:T(8,128)(2,1)S(1)}, u32[]{:S(2)}, u32[]{:S(2)}) collective-permute-start(bf16[128,384]{1,0:T(8,128)(2,1)S(1)} %get-tuple-element.64), channel_id=1, source_target_pairs={{0,4},{1,9},{4,0},{5,13},{8,12},{9,1},{12,8},{13,5},{2,6},{3,11},{... | collective-permute-start | bytes 294920 | tf_op jit(solution)/shard_map/ppermute | solution.py:685
  32.9 7.2 %collective-permute-start.12 = (bf16[128,384]{1,0:T(8,128)(2,1)S(1)}, bf16[128,384]{1,0:T(8,128)(2,1)S(1)}, u32[]{:S(2)}, u32[]{:S(2)}) collective-permute-start(bf16[128,384]{1,0:T(8,128)(2,1)S(1)} %get-tuple-element.65), channel_id=1, source_target_pairs={{0,12},{1,13},{4,8},{5,9},{8,4},{9,5},{12,0},{13,1},{2,14},{3,15},... | collective-permute-start | bytes 294920 | tf_op jit(solution)/shard_map/ppermute | solution.py:685
  34.7 7.8 %collective-permute-start.13 = (bf16[128,384]{1,0:T(8,128)(2,1)S(1)}, bf16[128,384]{1,0:T(8,128)(2,1)S(1)}, u32[]{:S(2)}, u32[]{:S(2)}) collective-permute-start(bf16[128,384]{1,0:T(8,128)(2,1)S(1)} %get-tuple-element.66), channel_id=1, source_target_pairs={{0,8},{1,5},{4,12},{5,1},{8,0},{9,13},{12,4},{13,9},{2,10},{3,7},{... | collective-permute-start | bytes 294920 | tf_op jit(solution)/shard_map/ppermute | solution.py:685
  36.4 9.8 %collective-permute-start.15 = (bf16[128,128]{1,0:T(8,128)(2,1)S(1)}, bf16[128,128]{1,0:T(8,128)(2,1)S(1)}, u32[]{:S(2)}, u32[]{:S(2)}) collective-permute-start(bf16[128,128]{1,0:T(8,128)(2,1)S(1)} %get-tuple-element.72), channel_id=1, source_target_pairs={{0,4},{1,9},{4,0},{5,13},{8,12},{9,1},{12,8},{13,5},{2,6},{3,11},{... | collective-permute-start | bytes 98312 | tf_op jit(solution)/shard_map/ppermute | solution.py:685
  37.4 8.9 %collective-permute-start.16 = (bf16[128,128]{1,0:T(8,128)(2,1)S(1)}, bf16[128,128]{1,0:T(8,128)(2,1)S(1)}, u32[]{:S(2)}, u32[]{:S(2)}) collective-permute-start(bf16[128,128]{1,0:T(8,128)(2,1)S(1)} %get-tuple-element.73), channel_id=1, source_target_pairs={{0,12},{1,13},{4,8},{5,9},{8,4},{9,5},{12,0},{13,1},{2,14},{3,15},... | collective-permute-start | bytes 98312 | tf_op jit(solution)/shard_map/ppermute | solution.py:685
  39.1 7.1 %collective-permute-start.17 = (bf16[128,128]{1,0:T(8,128)(2,1)S(1)}, bf16[128,128]{1,0:T(8,128)(2,1)S(1)}, u32[]{:S(2)}, u32[]{:S(2)}) collective-permute-start(bf16[128,128]{1,0:T(8,128)(2,1)S(1)} %get-tuple-element.74), channel_id=1, source_target_pairs={{0,8},{1,5},{4,12},{5,1},{8,0},{9,13},{12,4},{13,9},{2,10},{3,7},{... | collective-permute-start | bytes 98312 | tf_op jit(solution)/shard_map/ppermute | solution.py:685
  42.6 8.0 %copy-start.4 = (bf16[256,1024]{1,0:T(8,128)(2,1)S(1)}, bf16[256,1024]{1,0:T(8,128)(2,1)}, u32[]{:S(2)}) copy-start(bf16[256,1024]{1,0:T(8,128)(2,1)} %refs_6_.1) | copy-start | bytes 1572868
  46.3 10.6 %collective-permute-start.20 = (bf16[128,1024]{1,0:T(8,128)(2,1)S(1)}, bf16[128,1024]{1,0:T(8,128)(2,1)S(1)}, u32[]{:S(2)}, u32[]{:S(2)}) collective-permute-start(bf16[128,1024]{1,0:T(8,128)(2,1)S(1)} %get-tuple-element.82.grad), channel_id=1, source_target_pairs={{4,8},{8,4},{5,9},{9,5},{6,10},{10,6},{7,11},{11,7},{20,24},{24,20... | collective-permute-start | bytes 786440 | tf_op jit(solution)/shard_map/ppermute | solution.py:693
  47.0 9.9 %collective-permute-start.19 = (bf16[128,1024]{1,0:T(8,128)(2,1)S(1)}, bf16[128,1024]{1,0:T(8,128)(2,1)S(1)}, u32[]{:S(2)}, u32[]{:S(2)}) collective-permute-start(bf16[128,1024]{1,0:T(8,128)(2,1)S(1)} %get-tuple-element.82.grad), channel_id=1, source_target_pairs={{0,4},{4,0},{8,12},{12,8},{1,5},{5,1},{9,13},{13,9},{2,6},{6,2},{1... | collective-permute-start | bytes 786440 | tf_op jit(solution)/shard_map/ppermute | solution.py:666
  49.1 4.2 %collective-permute-start.14 = (bf16[216,128]{1,0:T(8,128)(2,1)S(1)}, bf16[216,128]{1,0:T(8,128)(2,1)S(1)}, u32[]{:S(2)}, u32[]{:S(2)}) collective-permute-start(bf16[216,128]{1,0:T(8,128)(2,1)S(1)} %get-tuple-element.69.refs_0_), channel_id=1, source_target_pairs={{0,2},{2,0},{1,3},{3,1},{4,6},{6,4},{5,7},{7,5},{8,10},{10,8},{9,1... | collective-permute-start | bytes 165896 | tf_op jit(solution)/shard_map/ppermute | solution.py:666
  53.3 5.9 %collective-permute-start.18 = (bf16[216,128]{1,0:T(8,128)(2,1)S(1)}, bf16[216,128]{1,0:T(8,128)(2,1)S(1)}, u32[]{:S(2)}, u32[]{:S(2)}) collective-permute-start(bf16[216,128]{1,0:T(8,128)(2,1)S(1)} %add_dp.1.refs_0_), channel_id=1, source_target_pairs={{0,8},{1,5},{4,12},{5,1},{8,0},{9,13},{12,4},{13,9},{2,10},{3,7},{... | collective-permute-start | bytes 165896 | tf_op jit(solution)/shard_map/ppermute | solution.py:685
  54.4 6.1 %collective-permute-start.22 = (bf16[216,128]{1,0:T(8,128)(2,1)S(1)}, bf16[216,128]{1,0:T(8,128)(2,1)S(1)}, u32[]{:S(2)}, u32[]{:S(2)}) collective-permute-start(bf16[216,128]{1,0:T(8,128)(2,1)S(1)} %add_dp.1.refs_0_), channel_id=1, source_target_pairs={{0,12},{1,13},{4,8},{5,9},{8,4},{9,5},{12,0},{13,1},{2,14},{3,15},... | collective-permute-start | bytes 165896 | tf_op jit(solution)/shard_map/ppermute | solution.py:685
  55.8 4.7 %collective-permute-start.21 = (bf16[216,128]{1,0:T(8,128)(2,1)S(1)}, bf16[216,128]{1,0:T(8,128)(2,1)S(1)}, u32[]{:S(2)}, u32[]{:S(2)}) collective-permute-start(bf16[216,128]{1,0:T(8,128)(2,1)S(1)} %add_dp.1.refs_0_), channel_id=1, source_target_pairs={{0,4},{1,9},{4,0},{5,13},{8,12},{9,1},{12,8},{13,5},{2,6},{3,11},{... | collective-permute-start | bytes 165896 | tf_op jit(solution)/shard_map/ppermute | solution.py:685
  60.6 1.4 %collective-permute-start.23 = (f32[216,128]{1,0:T(8,128)S(1)}, f32[216,128]{1,0:T(8,128)S(1)}, u32[]{:S(2)}, u32[]{:S(2)}) collective-permute-start(f32[216,128]{1,0:T(8,128)S(1)} %add_seq.1.left), channel_id=1, source_target_pairs={{0,1},{1,0},{2,3},{3,2},{4,5},{5,4},{6,7},{7,6},{8,9},{9,8},{10,11... | collective-permute-start | bytes 331784 | tf_op jit(solution)/shard_map/ppermute | solution.py:666

commit v7 on v6

--- a/solution.py
+++ b/solution.py
@@ -812,7 +812,6 @@
     )
     grad_near, grad_far = neighbours(dresid)
     other = swapped(terms, "dp", 1)
-    other, out = lax.optimization_barrier((other, out))
     (terms,) = call(sum_body, "add_dp", [shape(terms.shape, bf16)], (terms, other))
     (token_grad,) = call(
         functools.partial(back_conv_body, inner),
@@ -823,7 +822,7 @@
     )
     factor = 1.0 / math.sqrt(lax.axis_size("dp") * lax.axis_size("fsdp") * slots * rows)
     pieces = exchanged([terms] * slots)
-    pieces[-1], token_grad = lax.optimization_barrier((pieces[-1], token_grad))
+    pieces[-1], token_grad, out = lax.optimization_barrier((pieces[-1], token_grad, out))
     (summed,) = call(sum_body, "add_seq", [shape(terms.shape, f32)], pieces)
     (kernel_grad,) = call(
         functools.partial(final_body, factor),

time: 62.8 us -> 63.1 us (level)
    ppermute x7, waiting for transfers between devices: 2.31 us -> 3.98 us  [swapped(): return lax.ppermute(value, axis, [(i, i ^ distance) for i in range(count)])]
    ppermute x15, waiting for transfers between devices: 10.7 us -> 9.3 us  [exchanged(): received.append(lax.ppermute(pieces[k], ('seq', 'fsdp'), pairs))]
  transfers between devices with their start and end apart: 24 -> 24, of which waited for: 9 -> 7; matrix products, arithmetic and copies ran while one was open for 0% -> 0% of each run, Pallas kernels for 24% -> 23%
where the time goes in v7:
time: 63.1 us; the launch traced here: 62.9 us
  starting transfers between devices  29.6 us (47%)
  Pallas kernels  17.5 us (28%)
  waiting for transfers between devices  13.3 us (21%)
  between operations  1.5 us (2%)
  local copies, waits for them, and re-layouts  0.86 us (1%)
    ppermute x15, starting transfers between devices, exchanged(): received.append(lax.ppermute(pieces[k], ('seq', 'fsdp'), pairs))  17.8 us
    pallas_call x10, Pallas kernels, call(): pl.pallas_call(body, out_shape=tuple(outs), in_specs=specs, out_specs=(wh...  17.5 us
    ppermute x7, starting transfers between devices, swapped(): return lax.ppermute(value, axis, [(i, i ^ distance) for i in range(count)])  9.58 us
    ppermute x15, waiting for transfers between devices, exchanged(): received.append(lax.ppermute(pieces[k], ('seq', 'fsdp'), pairs))  9.3 us
    ppermute x7, waiting for transfers between devices, swapped(): return lax.ppermute(value, axis, [(i, i ^ distance) for i in range(count)])  3.98 us
    ppermute x2, starting transfers between devices, neighbours(): lax.ppermute(value, 'seq', middle + [(j, i) for i, j in middle])  2.18 us
  transfers between devices with their start and end apart: 24, of which 7 were waited for; matrix products, arithmetic and copies ran while one was open for 0% of the time, Pallas kernels for 23%

profile of v7, /device:TPU:0, one launch (start us, length us, event | category | flops | bytes accessed | tf_op | source)
XLA Modules:
  0.0 62.9 jit_solution(11510652361674041151)
XLA Ops:
  1.7 1.4 %own_conv.1.centre = f32[128,1024]{1,0:T(8,128)S(1)} custom-call(bf16[128,1024]{1,0:T(8,128)(2,1)} %bitcast.16, f32[27,1024]{1,0:T(8,128)} %taps.3), custom_call_target="tpu_custom_call" | custom-call | bytes 897024 | tf_op jit(solution)/shard_map/own_conv/pallas_call | solution.py:652
  3.1 0.8 %copy-done.2 = f32[128,1024]{1,0:T(8,128)} copy-done((f32[128,1024]{1,0:T(8,128)}, f32[128,1024]{1,0:T(8,128)S(1)}, u32[]{:S(2)}) %copy-start.2) | copy-done | bytes 524312
  3.9 1.5 %collective-permute-start.1 = (bf16[128,1024]{1,0:T(8,128)(2,1)}, bf16[128,1024]{1,0:T(8,128)(2,1)}, u32[]{:S(2)}, u32[]{:S(2)}) collective-permute-start(bf16[128,1024]{1,0:T(8,128)(2,1)} %bitcast.17), channel_id=1, source_target_pairs={{4,8},{8,4},{5,9},{9,5},{6,10},{10,6},{7,11},{11,7},{20,24},{24,20... | collective-permute-start | bytes 786440 | tf_op jit(solution)/shard_map/ppermute | solution.py:693
  5.4 4.8 %collective-permute-start = (bf16[128,1024]{1,0:T(8,128)(2,1)}, bf16[128,1024]{1,0:T(8,128)(2,1)}, u32[]{:S(2)}, u32[]{:S(2)}) collective-permute-start(bf16[128,1024]{1,0:T(8,128)(2,1)} %bitcast.18), channel_id=1, source_target_pairs={{0,4},{4,0},{8,12},{12,8},{1,5},{5,1},{9,13},{13,9},{2,6},{6,2},{1... | collective-permute-start | bytes 786440 | tf_op jit(solution)/shard_map/ppermute | solution.py:666
  11.1 2.8 %front.1 = (f32[3,1024]{1,0:T(4,128)S(1)}, bf16[256,1024]{1,0:T(8,128)(2,1)S(1)}, bf16[128,128]{1,0:T(8,128)(2,1)S(1)}, bf16[128,128]{1,0:T(8,128)(2,1)S(1)}, bf...) custom-call(s32[2]{0:T(128)S(1)} %pad_add_fusion.ids, bf16[2,8,128]{2,1,0:T(8,128)(2,1)S(1)} %broadcast_in_dim.10.feats, ...), custom_call_target="tpu_custom_call" | custom-call | flops 134217728 | bytes 3567624 | tf_op jit(solution)/shard_map/front/pallas_call | solution.py:652
  14.0 1.9 %collective-permute-start.6 = (bf16[128,128]{1,0:T(8,128)(2,1)S(1)}, bf16[128,128]{1,0:T(8,128)(2,1)S(1)}, u32[]{:S(2)}, u32[]{:S(2)}) collective-permute-start(bf16[128,128]{1,0:T(8,128)(2,1)S(1)} %get-tuple-element.52), channel_id=1, source_target_pairs={{0,12},{1,13},{4,8},{5,9},{8,4},{9,5},{12,0},{13,1},{2,14},{3,15},... | collective-permute-start | bytes 98312 | tf_op jit(solution)/shard_map/ppermute | solution.py:685
  15.9 1.6 %collective-permute-start.7 = (bf16[128,128]{1,0:T(8,128)(2,1)S(1)}, bf16[128,128]{1,0:T(8,128)(2,1)S(1)}, u32[]{:S(2)}, u32[]{:S(2)}) collective-permute-start(bf16[128,128]{1,0:T(8,128)(2,1)S(1)} %get-tuple-element.53), channel_id=1, source_target_pairs={{0,8},{1,5},{4,12},{5,1},{8,0},{9,13},{12,4},{13,9},{2,10},{3,7},{... | collective-permute-start | bytes 98312 | tf_op jit(solution)/shard_map/ppermute | solution.py:685
  17.6 2.9 %mix.1 = (bf16[128,1024]{1,0:T(8,128)(2,1)S(1)}, f32[128,1024]{1,0:T(8,128)S(1)}, bf16[128,384]{1,0:T(8,128)(2,1)S(1)}, bf16[128,384]{1,0:T(8,128)(2,1)S(1)}, bf...) custom-call(s32[2]{0:T(128)S(1)} %pad_add_fusion.ids, f32[128,1024]{1,0:T(8,128)S(1)} %copy-done.3, ...), custom_call_target="tpu_custom_call" | custom-call | flops 402653184 | bytes 5758984 | tf_op jit(solution)/shard_map/mix/pallas_call | solution.py:652
  21.5 2.3 %collective-permute-start.9 = (bf16[128,384]{1,0:T(8,128)(2,1)S(1)}, bf16[128,384]{1,0:T(8,128)(2,1)S(1)}, u32[]{:S(2)}, u32[]{:S(2)}) collective-permute-start(bf16[128,384]{1,0:T(8,128)(2,1)S(1)} %get-tuple-element.56), channel_id=1, source_target_pairs={{0,12},{1,13},{4,8},{5,9},{8,4},{9,5},{12,0},{13,1},{2,14},{3,15},... | collective-permute-start | bytes 294920 | tf_op jit(solution)/shard_map/ppermute | solution.py:685
  23.8 0.8 %collective-permute-start.10 = (bf16[128,384]{1,0:T(8,128)(2,1)S(1)}, bf16[128,384]{1,0:T(8,128)(2,1)S(1)}, u32[]{:S(2)}, u32[]{:S(2)}) collective-permute-start(bf16[128,384]{1,0:T(8,128)(2,1)S(1)} %get-tuple-element.57), channel_id=1, source_target_pairs={{0,8},{1,5},{4,12},{5,1},{8,0},{9,13},{12,4},{13,9},{2,10},{3,7},{... | collective-permute-start | bytes 294920 | tf_op jit(solution)/shard_map/ppermute | solution.py:685
  24.5 2.7 %collective-permute-done.8.refs_1_ = bf16[128,384]{1,0:T(8,128)(2,1)S(1)} collective-permute-done((bf16[128,384]{1,0:T(8,128)(2,1)S(1)}, bf16[128,384]{1,0:T(8,128)(2,1)S(1)}, u32[]{:S(2)}, u32[]{:S(2)}) %collective-permute-start.8) | collective-permute-done | bytes 98336 | tf_op jit(solution)/shard_map/ppermute | solution.py:685
  27.3 1.4 %collective-permute-done.9.refs_2_ = bf16[128,384]{1,0:T(8,128)(2,1)S(1)} collective-permute-done((bf16[128,384]{1,0:T(8,128)(2,1)S(1)}, bf16[128,384]{1,0:T(8,128)(2,1)S(1)}, u32[]{:S(2)}, u32[]{:S(2)}) %collective-permute-start.9) | collective-permute-done | bytes 98336 | tf_op jit(solution)/shard_map/ppermute | solution.py:685
  28.7 2.1 %collective-permute-done.10.refs_3_ = bf16[128,384]{1,0:T(8,128)(2,1)S(1)} collective-permute-done((bf16[128,384]{1,0:T(8,128)(2,1)S(1)}, bf16[128,384]{1,0:T(8,128)(2,1)S(1)}, u32[]{:S(2)}, u32[]{:S(2)}) %collective-permute-start.10) | collective-permute-done | bytes 98336 | tf_op jit(solution)/shard_map/ppermute | solution.py:685
  30.8 2.1 %attend.1 = (bf16[128,384]{1,0:T(8,128)(2,1)S(1)}, bf16[128,384]{1,0:T(8,128)(2,1)S(1)}, bf16[128,384]{1,0:T(8,128)(2,1)S(1)}, bf16[128,384]{1,0:T(8,128)(2,1)S(...) custom-call(bf16[128,384]{1,0:T(8,128)(2,1)S(1)} %get-tuple-element., ...), custom_call_target="tpu_custom_call" | custom-call | flops 402653184 | bytes 1048576 | tf_op jit(solution)/shard_map/attend/pallas_call | solution.py:652
  32.9 1.8 %collective-permute-start.12 = (bf16[128,384]{1,0:T(8,128)(2,1)S(1)}, bf16[128,384]{1,0:T(8,128)(2,1)S(1)}, u32[]{:S(2)}, u32[]{:S(2)}) collective-permute-start(bf16[128,384]{1,0:T(8,128)(2,1)S(1)} %get-tuple-element.64), channel_id=1, source_target_pairs={{0,12},{1,13},{4,8},{5,9},{8,4},{9,5},{12,0},{13,1},{2,14},{3,15},... | collective-permute-start | bytes 294920 | tf_op jit(solution)/shard_map/ppermute | solution.py:685
  34.7 1.7 %collective-permute-start.13 = (bf16[128,384]{1,0:T(8,128)(2,1)S(1)}, bf16[128,384]{1,0:T(8,128)(2,1)S(1)}, u32[]{:S(2)}, u32[]{:S(2)}) collective-permute-start(bf16[128,384]{1,0:T(8,128)(2,1)S(1)} %get-tuple-element.65), channel_id=1, source_target_pairs={{0,8},{1,5},{4,12},{5,1},{8,0},{9,13},{12,4},{13,9},{2,10},{3,7},{... | collective-permute-start | bytes 294920 | tf_op jit(solution)/shard_map/ppermute | solution.py:685
  36.4 1.0 %collective-permute-start.16 = (bf16[128,128]{1,0:T(8,128)(2,1)S(1)}, bf16[128,128]{1,0:T(8,128)(2,1)S(1)}, u32[]{:S(2)}, u32[]{:S(2)}) collective-permute-start(bf16[128,128]{1,0:T(8,128)(2,1)S(1)} %get-tuple-element.71), channel_id=1, source_target_pairs={{0,4},{1,9},{4,0},{5,13},{8,12},{9,1},{12,8},{13,5},{2,6},{3,11},{... | collective-permute-start | bytes 98312 | tf_op jit(solution)/shard_map/ppermute | solution.py:685
  37.4 1.8 %collective-permute-start.17 = (bf16[128,128]{1,0:T(8,128)(2,1)S(1)}, bf16[128,128]{1,0:T(8,128)(2,1)S(1)}, u32[]{:S(2)}, u32[]{:S(2)}) collective-permute-start(bf16[128,128]{1,0:T(8,128)(2,1)S(1)} %get-tuple-element.72), channel_id=1, source_target_pairs={{0,12},{1,13},{4,8},{5,9},{8,4},{9,5},{12,0},{13,1},{2,14},{3,15},... | collective-permute-start | bytes 98312 | tf_op jit(solution)/shard_map/ppermute | solution.py:685
  39.1 1.0 %collective-permute-start.18 = (bf16[128,128]{1,0:T(8,128)(2,1)S(1)}, bf16[128,128]{1,0:T(8,128)(2,1)S(1)}, u32[]{:S(2)}, u32[]{:S(2)}) collective-permute-start(bf16[128,128]{1,0:T(8,128)(2,1)S(1)} %get-tuple-element.73), channel_id=1, source_target_pairs={{0,8},{1,5},{4,12},{5,1},{8,0},{9,13},{12,4},{13,9},{2,10},{3,7},{... | collective-permute-start | bytes 98312 | tf_op jit(solution)/shard_map/ppermute | solution.py:685
  40.1 2.5 %collective-permute-done.13.refs_3_ = bf16[128,384]{1,0:T(8,128)(2,1)S(1)} collective-permute-done((bf16[128,384]{1,0:T(8,128)(2,1)S(1)}, bf16[128,384]{1,0:T(8,128)(2,1)S(1)}, u32[]{:S(2)}, u32[]{:S(2)}) %collective-permute-start.13) | collective-permute-done | bytes 98336 | tf_op jit(solution)/shard_map/ppermute | solution.py:685
  42.6 3.6 %tail.1 = (bf16[128,1024]{1,0:T(8,128)(2,1)S(1)}, bf16[216,128]{1,0:T(8,128)(2,1)S(1)}) custom-call(s32[2]{0:T(128)S(1)} %pad_add_fusion.ids, bf16[128,384]{1,0:T(8,128)(2,1)S(1)} %get-tuple-element.62.refs_0_, bf16[128,384]{1,0:T(8,128)(2,1)S(1)} %collective-permute-done.11.refs_1_, bf16[128,384]{1,0:T(8,128)(2,1)S(1)} %collective-permute-done.12.refs_2_, ...), custom_call_target="tpu_custom_call" | custom-call | flops 402653184 | bytes 5703688 | tf_op jit(solution)/shard_map/tail/pallas_call | solution.py:652
  46.3 0.7 %collective-permute-start.20 = (bf16[128,1024]{1,0:T(8,128)(2,1)S(1)}, bf16[128,1024]{1,0:T(8,128)(2,1)S(1)}, u32[]{:S(2)}, u32[]{:S(2)}) collective-permute-start(bf16[128,1024]{1,0:T(8,128)(2,1)S(1)} %get-tuple-element.74.grad), channel_id=1, source_target_pairs={{4,8},{8,4},{5,9},{9,5},{6,10},{10,6},{7,11},{11,7},{20,24},{24,20... | collective-permute-start | bytes 786440 | tf_op jit(solution)/shard_map/ppermute | solution.py:693
  47.0 2.1 %collective-permute-start.19 = (bf16[128,1024]{1,0:T(8,128)(2,1)S(1)}, bf16[128,1024]{1,0:T(8,128)(2,1)S(1)}, u32[]{:S(2)}, u32[]{:S(2)}) collective-permute-start(bf16[128,1024]{1,0:T(8,128)(2,1)S(1)} %get-tuple-element.74.grad), channel_id=1, source_target_pairs={{0,4},{4,0},{8,12},{12,8},{1,5},{5,1},{9,13},{13,9},{2,6},{6,2},{1... | collective-permute-start | bytes 786440 | tf_op jit(solution)/shard_map/ppermute | solution.py:666
  49.1 1.5 %collective-permute-start.14 = (bf16[216,128]{1,0:T(8,128)(2,1)S(1)}, bf16[216,128]{1,0:T(8,128)(2,1)S(1)}, u32[]{:S(2)}, u32[]{:S(2)}) collective-permute-start(bf16[216,128]{1,0:T(8,128)(2,1)S(1)} %get-tuple-element.68.refs_0_), channel_id=1, source_target_pairs={{0,2},{2,0},{1,3},{3,1},{4,6},{6,4},{5,7},{7,5},{8,10},{10,8},{9,1... | collective-permute-start | bytes 165896 | tf_op jit(solution)/shard_map/ppermute | solution.py:666
  50.6 2.7 %collective-permute-done.14.refs_1_ = bf16[216,128]{1,0:T(8,128)(2,1)S(1)} collective-permute-done((bf16[216,128]{1,0:T(8,128)(2,1)S(1)}, bf16[216,128]{1,0:T(8,128)(2,1)S(1)}, u32[]{:S(2)}, u32[]{:S(2)}) %collective-permute-start.14) | collective-permute-done | bytes 55328 | tf_op jit(solution)/shard_map/ppermute | solution.py:666
  53.3 1.1 %collective-permute-start.15 = (bf16[216,128]{1,0:T(8,128)(2,1)S(1)}, bf16[216,128]{1,0:T(8,128)(2,1)S(1)}, u32[]{:S(2)}, u32[]{:S(2)}) collective-permute-start(bf16[216,128]{1,0:T(8,128)(2,1)S(1)} %add_dp.1.refs_0_), channel_id=1, source_target_pairs={{0,8},{1,5},{4,12},{5,1},{8,0},{9,13},{12,4},{13,9},{2,10},{3,7},{... | collective-permute-start | bytes 165896 | tf_op jit(solution)/shard_map/ppermute | solution.py:685
  54.4 1.4 %collective-permute-start.22 = (bf16[216,128]{1,0:T(8,128)(2,1)S(1)}, bf16[216,128]{1,0:T(8,128)(2,1)S(1)}, u32[]{:S(2)}, u32[]{:S(2)}) collective-permute-start(bf16[216,128]{1,0:T(8,128)(2,1)S(1)} %add_dp.1.refs_0_), channel_id=1, source_target_pairs={{0,12},{1,13},{4,8},{5,9},{8,4},{9,5},{12,0},{13,1},{2,14},{3,15},... | collective-permute-start | bytes 165896 | tf_op jit(solution)/shard_map/ppermute | solution.py:685
  55.8 1.0 %collective-permute-start.21 = (bf16[216,128]{1,0:T(8,128)(2,1)S(1)}, bf16[216,128]{1,0:T(8,128)(2,1)S(1)}, u32[]{:S(2)}, u32[]{:S(2)}) collective-permute-start(bf16[216,128]{1,0:T(8,128)(2,1)S(1)} %add_dp.1.refs_0_), channel_id=1, source_target_pairs={{0,4},{1,9},{4,0},{5,13},{8,12},{9,1},{12,8},{13,5},{2,6},{3,11},{... | collective-permute-start | bytes 165896 | tf_op jit(solution)/shard_map/ppermute | solution.py:685
  56.8 1.7 %out.1 = bf16[128,1024]{1,0:T(8,128)(2,1)} custom-call(s32[2]{0:T(128)S(1)} %pad_add_fusion.ids, bf16[128,128]{1,0:T(8,128)(2,1)S(1)} %get-tuple-element.75.refs_0_, bf16[128,128]{1,0:T(8,128)(2,1)S(1)} %collective-permute-done.16.refs_1_, bf16[128,128]{1,0:T(8,128)(2,1)S(1)} %collective-permute-done.17.refs_2_, ...), custom_call_target="tpu_custom_call" | custom-call | flops 134217728 | bytes 1716232 | tf_op jit(solution)/shard_map/out/pallas_call | solution.py:652
  58.5 2.3 %back_conv.1 = bf16[128,1024]{1,0:T(8,128)(2,1)} custom-call(s32[2]{0:T(128)S(1)} %pad_add_fusion.ids, bf16[128,1024]{1,0:T(8,128)(2,1)S(1)} %get-tuple-element.74.grad, bf16[128,1024]{1,0:T(8,128)(2,1)S(1)} %collective-permute-done.19.near, bf16[128,1024]{1,0:T(8,128)(2,1)S(1)} %collective-permute-done.20.far, f32[27,1024]{1,0:T(8,128)S(1)} %copy-done.5), custom_call_target="tpu_custom_call" | custom-call | bytes 1159176 | tf_op jit(solution)/shard_map/back_conv/pallas_call | solution.py:652
  60.9 1.3 %collective-permute-done.23.right = f32[216,128]{1,0:T(8,128)S(1)} collective-permute-done((f32[216,128]{1,0:T(8,128)S(1)}, f32[216,128]{1,0:T(8,128)S(1)}, u32[]{:S(2)}, u32[]{:S(2)}) %collective-permute-start.23) | collective-permute-done | bytes 110624 | tf_op jit(solution)/shard_map/ppermute | solution.py:666
  62.3 0.7 %final.1 = f32[27,1024]{1,0:T(8,128)} custom-call(f32[216,128]{1,0:T(8,128)S(1)} %add_seq.1.left, f32[216,128]{1,0:T(8,128)S(1)} %collective-permute-done.23.right), custom_call_target="tpu_custom_call" | custom-call | bytes 331776 | tf_op jit(solution)/shard_map/final/pallas_call | solution.py:652
  (47 shorter events, 2.6 us)
Async XLA Ops:
  0.6 16.9 %collective-permute-start.4 = (bf16[512,1536]{1,0:T(8,128)(2,1)}, bf16[512,1536]{1,0:T(8,128)(2,1)S(1)}, u32[]{:S(2)}, u32[]{:S(2)}) collective-permute-start(bf16[512,1536]{1,0:T(8,128)(2,1)} %refs_8_.1), channel_id=1, source_target_pairs={{0,1},{1,0},{2,3},{3,2},{4,5},{5,4},{6,7},{7,6},{8,9},{9,8},{10,11... | collective-permute-start | bytes 4718600 | tf_op jit(solution)/shard_map/ppermute | solution.py:666
  1.1 9.9 %collective-permute-start.2 = (bf16[128,3072]{1,0:T(8,128)(2,1)}, bf16[128,3072]{1,0:T(8,128)(2,1)}, u32[]{:S(2)}, u32[]{:S(2)}) collective-permute-start(bf16[128,3072]{1,0:T(8,128)(2,1)} %rest_0_.1), channel_id=1, source_target_pairs={{0,1},{1,0},{2,3},{3,2},{4,5},{5,4},{6,7},{7,6},{8,9},{9,8},{10,11... | collective-permute-start | bytes 2359304 | tf_op jit(solution)/shard_map/ppermute | solution.py:666
  1.2 9.9 %collective-permute-start.3 = (bf16[256,1024]{1,0:T(8,128)(2,1)}, bf16[256,1024]{1,0:T(8,128)(2,1)}, u32[]{:S(2)}, u32[]{:S(2)}) collective-permute-start(bf16[256,1024]{1,0:T(8,128)(2,1)} %refs_6_.1), channel_id=1, source_target_pairs={{0,1},{1,0},{2,3},{3,2},{4,5},{5,4},{6,7},{7,6},{8,9},{9,8},{10,11... | collective-permute-start | bytes 1572872 | tf_op jit(solution)/shard_map/ppermute | solution.py:666
  3.1 0.8 %copy-start.2 = (f32[128,1024]{1,0:T(8,128)}, f32[128,1024]{1,0:T(8,128)S(1)}, u32[]{:S(2)}) copy-start(f32[128,1024]{1,0:T(8,128)S(1)} %own_conv.1.centre) | copy-start | bytes 1572868
  3.9 13.6 %copy-start = (bf16[512,1536]{1,0:T(8,128)(2,1)S(1)}, bf16[512,1536]{1,0:T(8,128)(2,1)}, u32[]{:S(2)}) copy-start(bf16[512,1536]{1,0:T(8,128)(2,1)} %refs_8_.1) | copy-start | bytes 4718596
  3.9 13.6 %copy-start.1 = (bf16[1,1,8,16,1024]{4,3,2,1,0:T(8,128)(2,1)S(1)}, bf16[1,1,8,16,1024]{4,3,2,1,0:T(8,128)(2,1)}, u32[]{:S(2)}) copy-start(bf16[1,1,8,16,1024]{4,3,2,1,0:T(8,128)(2,1)} %param.8) | copy-start | bytes 786436
  3.9 13.7 %copy-start.5 = (f32[27,1024]{1,0:T(8,128)S(1)}, f32[27,1024]{1,0:T(8,128)}, u32[]{:S(2)}) copy-start(f32[27,1024]{1,0:T(8,128)} %taps.3) | copy-start | bytes 331780
  3.9 12.0 %collective-permute-start.1 = (bf16[128,1024]{1,0:T(8,128)(2,1)}, bf16[128,1024]{1,0:T(8,128)(2,1)}, u32[]{:S(2)}, u32[]{:S(2)}) collective-permute-start(bf16[128,1024]{1,0:T(8,128)(2,1)} %bitcast.17), channel_id=1, source_target_pairs={{4,8},{8,4},{5,9},{9,5},{6,10},{10,6},{7,11},{11,7},{20,24},{24,20... | collective-permute-start | bytes 786440 | tf_op jit(solution)/shard_map/ppermute | solution.py:693
  5.4 12.1 %collective-permute-start = (bf16[128,1024]{1,0:T(8,128)(2,1)}, bf16[128,1024]{1,0:T(8,128)(2,1)}, u32[]{:S(2)}, u32[]{:S(2)}) collective-permute-start(bf16[128,1024]{1,0:T(8,128)(2,1)} %bitcast.18), channel_id=1, source_target_pairs={{0,4},{4,0},{8,12},{12,8},{1,5},{5,1},{9,13},{13,9},{2,6},{6,2},{1... | collective-permute-start | bytes 786440 | tf_op jit(solution)/shard_map/ppermute | solution.py:666
  11.0 6.6 %copy-start.3 = (f32[128,1024]{1,0:T(8,128)S(1)}, f32[128,1024]{1,0:T(8,128)}, u32[]{:S(2)}) copy-start(f32[128,1024]{1,0:T(8,128)} %copy-done.2) | copy-start | bytes 1572868
  14.0 6.5 %collective-permute-start.5 = (bf16[128,128]{1,0:T(8,128)(2,1)S(1)}, bf16[128,128]{1,0:T(8,128)(2,1)S(1)}, u32[]{:S(2)}, u32[]{:S(2)}) collective-permute-start(bf16[128,128]{1,0:T(8,128)(2,1)S(1)} %get-tuple-element.51), channel_id=1, source_target_pairs={{0,4},{1,9},{4,0},{5,13},{8,12},{9,1},{12,8},{13,5},{2,6},{3,11},{... | collective-permute-start | bytes 98312 | tf_op jit(solution)/shard_map/ppermute | solution.py:685
  14.0 6.4 %collective-permute-start.6 = (bf16[128,128]{1,0:T(8,128)(2,1)S(1)}, bf16[128,128]{1,0:T(8,128)(2,1)S(1)}, u32[]{:S(2)}, u32[]{:S(2)}) collective-permute-start(bf16[128,128]{1,0:T(8,128)(2,1)S(1)} %get-tuple-element.52), channel_id=1, source_target_pairs={{0,12},{1,13},{4,8},{5,9},{8,4},{9,5},{12,0},{13,1},{2,14},{3,15},... | collective-permute-start | bytes 98312 | tf_op jit(solution)/shard_map/ppermute | solution.py:685
  15.9 5.2 %collective-permute-start.7 = (bf16[128,128]{1,0:T(8,128)(2,1)S(1)}, bf16[128,128]{1,0:T(8,128)(2,1)S(1)}, u32[]{:S(2)}, u32[]{:S(2)}) collective-permute-start(bf16[128,128]{1,0:T(8,128)(2,1)S(1)} %get-tuple-element.53), channel_id=1, source_target_pairs={{0,8},{1,5},{4,12},{5,1},{8,0},{9,13},{12,4},{13,9},{2,10},{3,7},{... | collective-permute-start | bytes 98312 | tf_op jit(solution)/shard_map/ppermute | solution.py:685
  20.4 22.1 %copy-start.6 = (bf16[1,1,8,16,1024]{4,3,2,1,0:T(8,128)(2,1)S(1)}, bf16[1,1,8,16,1024]{4,3,2,1,0:T(8,128)(2,1)}, u32[]{:S(2)}) copy-start(bf16[1,1,8,16,1024]{4,3,2,1,0:T(8,128)(2,1)} %param.15) | copy-start | bytes 786436
  21.1 6.2 %collective-permute-start.8 = (bf16[128,384]{1,0:T(8,128)(2,1)S(1)}, bf16[128,384]{1,0:T(8,128)(2,1)S(1)}, u32[]{:S(2)}, u32[]{:S(2)}) collective-permute-start(bf16[128,384]{1,0:T(8,128)(2,1)S(1)} %get-tuple-element.55), channel_id=1, source_target_pairs={{0,4},{1,9},{4,0},{5,13},{8,12},{9,1},{12,8},{13,5},{2,6},{3,11},{... | collective-permute-start | bytes 294920 | tf_op jit(solution)/shard_map/ppermute | solution.py:685
  21.5 7.2 %collective-permute-start.9 = (bf16[128,384]{1,0:T(8,128)(2,1)S(1)}, bf16[128,384]{1,0:T(8,128)(2,1)S(1)}, u32[]{:S(2)}, u32[]{:S(2)}) collective-permute-start(bf16[128,384]{1,0:T(8,128)(2,1)S(1)} %get-tuple-element.56), channel_id=1, source_target_pairs={{0,12},{1,13},{4,8},{5,9},{8,4},{9,5},{12,0},{13,1},{2,14},{3,15},... | collective-permute-start | bytes 294920 | tf_op jit(solution)/shard_map/ppermute | solution.py:685
  23.8 7.0 %collective-permute-start.10 = (bf16[128,384]{1,0:T(8,128)(2,1)S(1)}, bf16[128,384]{1,0:T(8,128)(2,1)S(1)}, u32[]{:S(2)}, u32[]{:S(2)}) collective-permute-start(bf16[128,384]{1,0:T(8,128)(2,1)S(1)} %get-tuple-element.57), channel_id=1, source_target_pairs={{0,8},{1,5},{4,12},{5,1},{8,0},{9,13},{12,4},{13,9},{2,10},{3,7},{... | collective-permute-start | bytes 294920 | tf_op jit(solution)/shard_map/ppermute | solution.py:685
  32.8 6.3 %collective-permute-start.11 = (bf16[128,384]{1,0:T(8,128)(2,1)S(1)}, bf16[128,384]{1,0:T(8,128)(2,1)S(1)}, u32[]{:S(2)}, u32[]{:S(2)}) collective-permute-start(bf16[128,384]{1,0:T(8,128)(2,1)S(1)} %get-tuple-element.63), channel_id=1, source_target_pairs={{0,4},{1,9},{4,0},{5,13},{8,12},{9,1},{12,8},{13,5},{2,6},{3,11},{... | collective-permute-start | bytes 294920 | tf_op jit(solution)/shard_map/ppermute | solution.py:685
  32.9 7.2 %collective-permute-start.12 = (bf16[128,384]{1,0:T(8,128)(2,1)S(1)}, bf16[128,384]{1,0:T(8,128)(2,1)S(1)}, u32[]{:S(2)}, u32[]{:S(2)}) collective-permute-start(bf16[128,384]{1,0:T(8,128)(2,1)S(1)} %get-tuple-element.64), channel_id=1, source_target_pairs={{0,12},{1,13},{4,8},{5,9},{8,4},{9,5},{12,0},{13,1},{2,14},{3,15},... | collective-permute-start | bytes 294920 | tf_op jit(solution)/shard_map/ppermute | solution.py:685
  34.7 7.8 %collective-permute-start.13 = (bf16[128,384]{1,0:T(8,128)(2,1)S(1)}, bf16[128,384]{1,0:T(8,128)(2,1)S(1)}, u32[]{:S(2)}, u32[]{:S(2)}) collective-permute-start(bf16[128,384]{1,0:T(8,128)(2,1)S(1)} %get-tuple-element.65), channel_id=1, source_target_pairs={{0,8},{1,5},{4,12},{5,1},{8,0},{9,13},{12,4},{13,9},{2,10},{3,7},{... | collective-permute-start | bytes 294920 | tf_op jit(solution)/shard_map/ppermute | solution.py:685
  36.4 9.8 %collective-permute-start.16 = (bf16[128,128]{1,0:T(8,128)(2,1)S(1)}, bf16[128,128]{1,0:T(8,128)(2,1)S(1)}, u32[]{:S(2)}, u32[]{:S(2)}) collective-permute-start(bf16[128,128]{1,0:T(8,128)(2,1)S(1)} %get-tuple-element.71), channel_id=1, source_target_pairs={{0,4},{1,9},{4,0},{5,13},{8,12},{9,1},{12,8},{13,5},{2,6},{3,11},{... | collective-permute-start | bytes 98312 | tf_op jit(solution)/shard_map/ppermute | solution.py:685
  37.4 8.9 %collective-permute-start.17 = (bf16[128,128]{1,0:T(8,128)(2,1)S(1)}, bf16[128,128]{1,0:T(8,128)(2,1)S(1)}, u32[]{:S(2)}, u32[]{:S(2)}) collective-permute-start(bf16[128,128]{1,0:T(8,128)(2,1)S(1)} %get-tuple-element.72), channel_id=1, source_target_pairs={{0,12},{1,13},{4,8},{5,9},{8,4},{9,5},{12,0},{13,1},{2,14},{3,15},... | collective-permute-start | bytes 98312 | tf_op jit(solution)/shard_map/ppermute | solution.py:685
  39.1 7.1 %collective-permute-start.18 = (bf16[128,128]{1,0:T(8,128)(2,1)S(1)}, bf16[128,128]{1,0:T(8,128)(2,1)S(1)}, u32[]{:S(2)}, u32[]{:S(2)}) collective-permute-start(bf16[128,128]{1,0:T(8,128)(2,1)S(1)} %get-tuple-element.73), channel_id=1, source_target_pairs={{0,8},{1,5},{4,12},{5,1},{8,0},{9,13},{12,4},{13,9},{2,10},{3,7},{... | collective-permute-start | bytes 98312 | tf_op jit(solution)/shard_map/ppermute | solution.py:685
  42.6 14.3 %copy-start.4 = (bf16[256,1024]{1,0:T(8,128)(2,1)S(1)}, bf16[256,1024]{1,0:T(8,128)(2,1)}, u32[]{:S(2)}) copy-start(bf16[256,1024]{1,0:T(8,128)(2,1)} %refs_6_.1) | copy-start | bytes 1572868
  46.3 12.2 %collective-permute-start.20 = (bf16[128,1024]{1,0:T(8,128)(2,1)S(1)}, bf16[128,1024]{1,0:T(8,128)(2,1)S(1)}, u32[]{:S(2)}, u32[]{:S(2)}) collective-permute-start(bf16[128,1024]{1,0:T(8,128)(2,1)S(1)} %get-tuple-element.74.grad), channel_id=1, source_target_pairs={{4,8},{8,4},{5,9},{9,5},{6,10},{10,6},{7,11},{11,7},{20,24},{24,20... | collective-permute-start | bytes 786440 | tf_op jit(solution)/shard_map/ppermute | solution.py:693
  47.0 11.6 %collective-permute-start.19 = (bf16[128,1024]{1,0:T(8,128)(2,1)S(1)}, bf16[128,1024]{1,0:T(8,128)(2,1)S(1)}, u32[]{:S(2)}, u32[]{:S(2)}) collective-permute-start(bf16[128,1024]{1,0:T(8,128)(2,1)S(1)} %get-tuple-element.74.grad), channel_id=1, source_target_pairs={{0,4},{4,0},{8,12},{12,8},{1,5},{5,1},{9,13},{13,9},{2,6},{6,2},{1... | collective-permute-start | bytes 786440 | tf_op jit(solution)/shard_map/ppermute | solution.py:666
  49.1 4.2 %collective-permute-start.14 = (bf16[216,128]{1,0:T(8,128)(2,1)S(1)}, bf16[216,128]{1,0:T(8,128)(2,1)S(1)}, u32[]{:S(2)}, u32[]{:S(2)}) collective-permute-start(bf16[216,128]{1,0:T(8,128)(2,1)S(1)} %get-tuple-element.68.refs_0_), channel_id=1, source_target_pairs={{0,2},{2,0},{1,3},{3,1},{4,6},{6,4},{5,7},{7,5},{8,10},{10,8},{9,1... | collective-permute-start | bytes 165896 | tf_op jit(solution)/shard_map/ppermute | solution.py:666
  53.3 7.5 %collective-permute-start.15 = (bf16[216,128]{1,0:T(8,128)(2,1)S(1)}, bf16[216,128]{1,0:T(8,128)(2,1)S(1)}, u32[]{:S(2)}, u32[]{:S(2)}) collective-permute-start(bf16[216,128]{1,0:T(8,128)(2,1)S(1)} %add_dp.1.refs_0_), channel_id=1, source_target_pairs={{0,8},{1,5},{4,12},{5,1},{8,0},{9,13},{12,4},{13,9},{2,10},{3,7},{... | collective-permute-start | bytes 165896 | tf_op jit(solution)/shard_map/ppermute | solution.py:685
  54.4 6.4 %collective-permute-start.22 = (bf16[216,128]{1,0:T(8,128)(2,1)S(1)}, bf16[216,128]{1,0:T(8,128)(2,1)S(1)}, u32[]{:S(2)}, u32[]{:S(2)}) collective-permute-start(bf16[216,128]{1,0:T(8,128)(2,1)S(1)} %add_dp.1.refs_0_), channel_id=1, source_target_pairs={{0,12},{1,13},{4,8},{5,9},{8,4},{9,5},{12,0},{13,1},{2,14},{3,15},... | collective-permute-start | bytes 165896 | tf_op jit(solution)/shard_map/ppermute | solution.py:685
  55.8 5.0 %collective-permute-start.21 = (bf16[216,128]{1,0:T(8,128)(2,1)S(1)}, bf16[216,128]{1,0:T(8,128)(2,1)S(1)}, u32[]{:S(2)}, u32[]{:S(2)}) collective-permute-start(bf16[216,128]{1,0:T(8,128)(2,1)S(1)} %add_dp.1.refs_0_), channel_id=1, source_target_pairs={{0,4},{1,9},{4,0},{5,13},{8,12},{9,1},{12,8},{13,5},{2,6},{3,11},{... | collective-permute-start | bytes 165896 | tf_op jit(solution)/shard_map/ppermute | solution.py:685
  60.9 1.4 %collective-permute-start.23 = (f32[216,128]{1,0:T(8,128)S(1)}, f32[216,128]{1,0:T(8,128)S(1)}, u32[]{:S(2)}, u32[]{:S(2)}) collective-permute-start(f32[216,128]{1,0:T(8,128)S(1)} %add_seq.1.left), channel_id=1, source_target_pairs={{0,1},{1,0},{2,3},{3,2},{4,5},{5,4},{6,7},{7,6},{8,9},{9,8},{10,11... | collective-permute-start | bytes 331784 | tf_op jit(solution)/shard_map/ppermute | solution.py:666
